TPU v7x, 128 devices: a whole 4x4x4 slice. The times are simulated.
128 devices in a mesh: tm: 4 (over x), lat: 32 (over z, y, core).
Axes of the slice: x: 4, y: 4, z: 4, core: 2. Of those that a mesh axis runs over, the one named last changes fastest.
Arguments:
- sketch: bfloat16 [256, 3, 256, 1024], P('tm', None, 'lat'), may hold values from -6 to 6
- test_sketch: bfloat16 [256, 3, 256, 1024], P('tm', None, 'lat'), may hold values from -6 to 6
- checkpoints: bfloat16 [16, 3, 256, 1024], P('tm', None, 'lat'), may hold values from -2.5 to 2.5
- checkpoint_step: int32 [4], P('tm'), may hold values from 0 to 3
- station_row: int32 [4, 4096], P('tm', 'lat'), may hold values from 0 to 255, as said below
- station_column: int32 [4, 4096], P('tm', 'lat'), may hold values from 0 to 1023
- station_value: float32 [4, 4096], P('tm', 'lat'), may hold values from -6 to 6
Outputs:
- increment: float32 [4, 3, 256, 1024], P('tm', None, 'lat')
- reduced_adjoint: float32 [4, 64], P('tm')
- total_cost: float32 [], replicated
Inputs may be any that keep to these rules, and one draw needn't show every extreme that they name: `station_row`: in each group's list, entries 128 * j to 128 * (j + 1) - 1 lie in latitude rows 8 * j to 8 * (j + 1) - 1.
All inputs are finite; a program needn't handle non-finite values.
Results may differ from a plain program's by a relative error of at most 0.0003.
Values may be sent and summed in bfloat16 or wider, within the bound.
No kernel may reach another device: no remote copies, remote signals or barrier semaphores. Data moves between devices by JAX's collectives and lax.ppermute only.
A program may use at most 128 MiB of HBM per device.

v0:
```python
import functools
import math

import jax
import jax.numpy as jnp
from jax import lax
from jax.experimental import pallas as pl
from jax.experimental.pallas import tpu as pltpu
from jax.sharding import Mesh
from jax.sharding import PartitionSpec as P

STEPS = 4
LAT = ("lat_0", "lat_1", "lat_2")
KC = 16
HALO = STEPS

flow_coef = 0.4
coriolis_coef = 0.5
map_scale = 0.5
MIB = 1 << 20

VMEM = pl.BlockSpec(memory_space=pltpu.VMEM)
SMEM = pl.BlockSpec(memory_space=pltpu.SMEM)
HBM = pl.BlockSpec(memory_space=pltpu.HBM)


def lon_difference(x):
    lon = x.shape[-1]
    return pltpu.roll(x, lon - 1, 1) - pltpu.roll(x, 1, 1)


def split3(x):
    high = x.astype(jnp.bfloat16)
    rest = x - high.astype(jnp.float32)
    middle = rest.astype(jnp.bfloat16)
    low = (rest - middle.astype(jnp.float32)).astype(jnp.bfloat16)
    return high, middle, low


def across(a, b):
    return lax.dot_general(a, b, (((1,), (1,)), ((), ())), preferred_element_type=jnp.float32)


def pack_kernel(
    step_ref, core_ref, sketch_hbm, base_hbm, outer_ref, inner_ref, outer_base, inner_base, base_ref, sketch, base, sems
):
    chunks = sketch.shape[0] // KC
    fields = sketch.shape[1]

    def copy(c):
        at = pl.ds(c * KC, KC)
        return pltpu.make_async_copy(sketch_hbm.at[at], sketch.at[at], sems.at[c])

    base_copy = pltpu.make_async_copy(base_hbm.at[step_ref[0]], base, sems.at[chunks])
    for c in range(chunks):
        copy(c).start()
    base_copy.start()
    for c in range(chunks):
        copy(c).wait()
        for core in range(2):
            low, high = (outer_ref, inner_ref) if core == 0 else (inner_ref, outer_ref)

            @pl.when(core_ref[0] == core)
            def _(c=c, low=low, high=high):
                for f in range(fields):
                    part = jnp.swapaxes(sketch[c * KC : (c + 1) * KC, f].astype(jnp.float32), 0, 1)
                    part = part.astype(jnp.bfloat16)
                    for ref, rows in ((low, part[:HALO]), (high, part[HALO:])):
                        ref[f * HALO : (f + 1) * HALO, c * KC : (c + 1) * KC] = rows

    base_copy.wait()
    values = base[...].astype(jnp.float32)
    base_ref[...] = values
    pad = jnp.zeros((16 - fields * HALO, values.shape[-1]), jnp.float32)
    for core in range(2):
        low, high = (outer_base, inner_base) if core == 0 else (inner_base, outer_base)

        @pl.when(core_ref[0] == core)
        def _(low=low, high=high):
            for ref, at in ((low, 0), (high, HALO)):
                rows = [values[f, at : at + HALO] for f in range(fields)]
                ref[...] = jnp.concatenate([*rows, pad], axis=0).astype(jnp.bfloat16)


def pack(sketch, checkpoints, checkpoint_step, core):
    rank, fields, rows, lon = sketch.shape
    half = jax.ShapeDtypeStruct((fields * HALO, rank, lon), jnp.bfloat16)
    lines = jax.ShapeDtypeStruct((16, lon), jnp.bfloat16)
    return pl.pallas_call(
        pack_kernel,
        out_shape=(half, half, lines, lines, jax.ShapeDtypeStruct((fields, rows, lon), jnp.float32)),
        in_specs=[SMEM, SMEM, HBM, HBM],
        out_specs=(VMEM,) * 5,
        scratch_shapes=[
            pltpu.VMEM(sketch.shape, jnp.bfloat16),
            pltpu.VMEM((fields, rows, lon), jnp.bfloat16),
            pltpu.SemaphoreType.DMA((rank // KC + 1,)),
        ],
        compiler_params=pltpu.CompilerParams(vmem_limit_bytes=12 * MIB),
        name="pack",
    )(checkpoint_step, core, sketch, checkpoints)


def observe_kernel(scales, band_ref, base_ref, row_ref, column_ref, value_ref, field_ref, cost_ref):
    total_rows, observed, groups = scales
    rows, lon = base_ref.shape[-2:]
    count = row_ref.shape[-1]
    station_row = row_ref[...]
    local = station_row - band_ref[0] * rows
    at_column = lax.broadcasted_iota(jnp.int32, (lon, count), 0) == column_ref[...]
    at_column = jnp.where(at_column, 1.0, 0.0).astype(jnp.bfloat16)
    at_row = lax.broadcasted_iota(jnp.int32, (rows, count), 0) == local
    found = lax.dot_general(
        base_ref[0].astype(jnp.bfloat16), at_column, (((1,), (0,)), ((), ())), preferred_element_type=jnp.float32
    )
    here = jnp.sum(jnp.where(at_row, found, 0.0), axis=0, keepdims=True)
    innovation = here - value_ref[...]
    weight = 1.0 + 2.0 * station_row.astype(jnp.float32) / total_rows
    weighted = weight * innovation
    cost = jnp.sum(weighted * innovation, axis=1, keepdims=True) / (2.0 * groups * observed)
    cost_ref[...] = jnp.broadcast_to(cost, cost_ref.shape)
    spread = jnp.where(at_row, weighted / (2.0 * math.sqrt(observed)), 0.0)
    field = jnp.zeros((rows, lon), jnp.float32)
    for piece in split3(spread):
        field += across(piece, at_column)
    for n, piece in enumerate(split3(field)):
        field_ref[n * rows : (n + 1) * rows] = piece.astype(jnp.float32)


def observe(band, base, station_row, station_column, station_value, scales):
    rows, lon = base.shape[-2:]
    return pl.pallas_call(
        functools.partial(observe_kernel, scales),
        out_shape=(
            jax.ShapeDtypeStruct((3 * rows, lon), jnp.float32),
            jax.ShapeDtypeStruct((1, 128), jnp.float32),
        ),
        in_specs=[SMEM] + [VMEM] * 4,
        out_specs=(VMEM, VMEM),
        compiler_params=pltpu.CompilerParams(vmem_limit_bytes=8 * MIB),
        cost_estimate=pl.CostEstimate(flops=20_000_000, bytes_accessed=1_000_000, transcendentals=0),
        name="observe",
    )(band, base, station_row, station_column, station_value)


def sweep_kernel(
    scale,
    bands,
    band_ref,
    core_ref,
    test_hbm,
    base_ref,
    outer_base,
    inner_base,
    outer_ref,
    inner_ref,
    field_ref,
    cost_ref,
    back_ref,
    coef_ref,
    share_ref,
    test,
    one,
    two,
    coef,
    sems,
):
    rank, fields, rows, lon = test.shape
    extended = rows + 2 * HALO
    band, core = band_ref[0], core_ref[0]

    def copy(c):
        at = pl.ds(c * KC, KC)
        return pltpu.make_async_copy(test_hbm.at[at], test.at[at], sems.at[c])

    for c in range(rank // KC):
        copy(c).start()

    def latitude(e):
        return band * rows - HALO + e

    def inside(e):
        at = latitude(e)
        return jnp.where((at >= 0) & (at < rows * bands), 1.0, 0.0)

    def put(f, e, line):
        line = 0.0625 + 0.015625 * line if f == 0 else (0.2 * flow_coef) * line
        line = line * inside(e)
        coef[f, e] = jnp.broadcast_to(line, (8, lon))
        coef_ref[f, pl.ds(e, 1)] = line

    for f in range(fields):
        for r in range(rows):
            put(f, HALO + r, base_ref[f, r : r + 1])
    for ref, first in ((outer_base, core), (inner_base, 1 - core)):
        values = ref[...].astype(jnp.float32)
        for f in range(fields):
            for r in range(HALO):
                put(f, first * (extended - HALO) + r, values[f * HALO + r : f * HALO + r + 1])

    turns = [
        0.5 * coriolis_coef * (2.0 * (latitude(e).astype(jnp.float32) + 0.5) / (rows * bands) - 1.0)
        for e in range(extended)
    ]
    insides = [inside(e) for e in range(extended)]

    def terms(source, e, at):
        depth, east, north = (coef[f, e] for f in range(3))
        h, u, v = (source[e, f, at] for f in range(3))
        deep = depth * h
        mine = (
            h + lon_difference(u + east * h),
            u - turns[e] * v + lon_difference(east * u + deep),
            v + turns[e] * u + lon_difference(east * v),
        )
        edge = v if HALO <= e < HALO + rows else insides[e] * v
        beside = (edge + north * h, north * u, north * v + deep)
        return mine, beside

    def backward_step(source, target, first, last, at):
        before = here = mine = None
        for e in range(first - 1, last + 2):
            after_mine, after = terms(source, e + 1, at) if e + 1 <= last else (None, None)
            for f in range(fields):
                total = mine[f] if mine is not None else None
                if after is not None:
                    total = after[f] if total is None else total + after[f]
                if before is not None:
                    total = -before[f] if total is None else total - before[f]
                target[e, f, at] = total
            before, here, mine = here, after, after_mine

    def chunk_body(c, carry):
        copy(c).wait()
        for half in range(KC // 8):
            at = pl.ds(half * 8, 8)
            for f in range(fields):
                part = test[pl.ds(c * KC + half * 8, 8), f].astype(jnp.float32)
                part = jnp.swapaxes(part, 0, 1)
                for r in range(rows):
                    one[HALO + r, f, at] = 4.0 * part[r] if f == 0 else part[r]
            source, target = one, two
            for step in range(STEPS):
                backward_step(source, target, HALO - step, HALO + rows - 1 + step, at)
                source, target = target, source
        for e in range(extended):
            for f in range(fields):
                value = one[e, f]
                if f == 0:
                    value = 0.25 * value
                upper = value.astype(jnp.bfloat16)
                lower = (value - upper.astype(jnp.float32)).astype(jnp.bfloat16)
                back_ref[f * extended + e, pl.ds(c * KC, KC)] = upper
                back_ref[f * extended + e, pl.ds(rank + c * KC, KC)] = lower
        return carry

    lax.fori_loop(0, rank // KC, chunk_body, 0)

    share = jnp.zeros((2 * rank, rank), jnp.float32)
    forced = jnp.zeros((3 * rows, rank), jnp.float32)
    line = lax.broadcasted_iota(jnp.int32, (3 * rows, rank), 0) % rows
    field = field_ref[...].astype(jnp.bfloat16)
    for ref, first in ((outer_ref, core), (inner_ref, 1 - core)):
        for f in range(fields):
            for r in range(HALO):
                columns = ref[f * HALO + r]
                share += across(back_ref[f * extended + HALO + first * HALO + r], columns)
                if f == 0:
                    forced += jnp.where(line == first * HALO + r, across(field, columns), 0.0)
    share = (share[:rank] + share[rank:]) * scale
    share_ref[:rank] = share
    lane = lax.broadcasted_iota(jnp.int32, (8, rank), 0)
    forced = jnp.sum(forced, axis=0, keepdims=True)
    share_ref[rank:] = jnp.where(lane == 0, forced, jnp.where(lane == 1, cost_ref[0:1, :rank], 0.0))


def sweep(band, core, test_sketch, base, outer_base, inner_base, outer, inner, field, cost, scale, bands):
    rank, fields, rows, lon = test_sketch.shape
    extended = rows + 2 * HALO
    return pl.pallas_call(
        functools.partial(sweep_kernel, scale, bands),
        out_shape=(
            jax.ShapeDtypeStruct((fields * extended, 2 * rank, lon), jnp.bfloat16),
            jax.ShapeDtypeStruct((fields, extended, lon), jnp.float32),
            jax.ShapeDtypeStruct((rank + 8, rank), jnp.float32),
        ),
        in_specs=[SMEM, SMEM, HBM] + [VMEM] * 7,
        out_specs=(VMEM,) * 3,
        scratch_shapes=[
            pltpu.VMEM(test_sketch.shape, jnp.bfloat16),
            pltpu.VMEM((extended, fields, KC, lon), jnp.float32),
            pltpu.VMEM((extended, fields, KC, lon), jnp.float32),
            pltpu.VMEM((fields, extended, 8, lon), jnp.float32),
            pltpu.SemaphoreType.DMA((rank // KC,)),
        ],
        compiler_params=pltpu.CompilerParams(vmem_limit_bytes=24 * MIB),
        cost_estimate=pl.CostEstimate(flops=2_000_000_000, bytes_accessed=30_000_000, transcendentals=0),
        name="sweep",
    )(band, core, test_sketch, base, outer_base, inner_base, outer, inner, field, cost)


def join_kernel(scale, core_ref, back_ref, own_ref, outer_hbm, inner_hbm, outer_ref, inner_ref, share_ref, sems):
    rank = own_ref.shape[1]
    extended = back_ref.shape[0] // 3
    core = core_ref[0]
    size = outer_ref.shape[0]
    pieces = 3
    step = size // pieces
    sides = ((inner_hbm, inner_ref, 1 - core), (outer_hbm, outer_ref, core))

    def copy(n, side):
        at = pl.ds(n * step, step)
        return pltpu.make_async_copy(side[0].at[at], side[1].at[at], sems.at[n])

    for s, side in enumerate(sides):
        for n in range(pieces):
            at = pl.ds(n * step, step)
            pltpu.make_async_copy(side[0].at[at], side[1].at[at], sems.at[s * pieces + n]).start()
    share = jnp.zeros((2 * rank, rank), jnp.float32)
    for s, side in enumerate(sides):
        for n in range(pieces):
            at = pl.ds(n * step, step)
            pltpu.make_async_copy(side[0].at[at], side[1].at[at], sems.at[s * pieces + n]).wait()
            for i in range(n * step, (n + 1) * step):
                f, r = i // HALO, i % HALO
                share += across(back_ref[f * extended + side[2] * (extended - HALO) + r], side[1][i])
    share = own_ref[:rank] + (share[:rank] + share[rank:]) * scale
    half = rank // 2
    share_ref[:half] = jnp.concatenate([share[:half], share[half:]], axis=1)
    tail = own_ref[rank:]
    share_ref[half:] = jnp.concatenate([tail, tail], axis=1)


def join(core, back, own, outer, inner, scale):
    rank = own.shape[1]
    received = jax.ShapeDtypeStruct(outer.shape, outer.dtype)
    return pl.pallas_call(
        functools.partial(join_kernel, scale),
        out_shape=(received, received, jax.ShapeDtypeStruct((rank // 2 + 8, 2 * rank), jnp.float32)),
        in_specs=[SMEM, VMEM, VMEM, HBM, HBM],
        out_specs=(VMEM,) * 3,
        scratch_shapes=[pltpu.SemaphoreType.DMA((6,))],
        compiler_params=pltpu.CompilerParams(vmem_limit_bytes=8 * MIB),
        name="join",
    )(core, back, own, outer, inner)


def combine_kernel(
    scale,
    groups,
    bands,
    group_ref,
    band_ref,
    core_ref,
    *refs,
):
    shares = refs[:groups]
    (
        outer_ref,
        inner_ref,
        far_outer_ref,
        far_inner_ref,
        coef_ref,
        increment_hbm,
        adjoint_hbm,
        cost_hbm,
        increment,
        adjoint,
        cost_out,
        combined,
        sems,
    ) = refs[groups:]
    half = shares[0].shape[0] - 8
    rank = 2 * half
    fields, extended, lon = coef_ref.shape
    rows = extended - 2 * HALO
    core = core_ref[0]

    line = lax.broadcasted_iota(jnp.int32, (half, 2 * rank), 0)
    lane = lax.broadcasted_iota(jnp.int32, (half, 2 * rank), 1)
    left = lane < rank
    row = jnp.zeros((1, 2 * rank), jnp.float32)
    cost = jnp.zeros((1, 2 * rank), jnp.float32)
    for ahead in reversed(range(groups)):
        share = shares[ahead][...]
        cost += share[half + 1 : half + 2]
        upper = jnp.sum(jnp.where(lane == line, row, 0.0), axis=1, keepdims=True)
        lower = jnp.sum(jnp.where(lane == line + half, row, 0.0), axis=1, keepdims=True)
        product = jnp.sum(share[:half] * jnp.where(left, upper, lower), axis=0, keepdims=True)
        row = product + pltpu.roll(product, rank, 1) + share[half : half + 1]
        if ahead:
            row = jnp.where(group_ref[0] + ahead < groups, row, 0.0)
    adjoint[...] = row[:, :rank]
    cost_out[...] = cost
    copies = [
        pltpu.make_async_copy(adjoint, adjoint_hbm, sems.at[0]),
        pltpu.make_async_copy(cost_out, cost_hbm, sems.at[1]),
    ]
    for copy in copies:
        copy.start()

    pick = lax.broadcasted_iota(jnp.int32, (8, rank), 0)
    factor = jnp.zeros((8, rank), jnp.float32)
    for n, piece in enumerate(split3(row[:, :rank] * scale)):
        factor = jnp.where(pick == n, piece.astype(jnp.float32), factor)
    factor = factor.astype(jnp.bfloat16)
    places = (
        (outer_ref, HALO + core * HALO),
        (inner_ref, 2 * HALO - core * HALO),
        (far_outer_ref, core * (extended - HALO)),
        (far_inner_ref, (1 - core) * (extended - HALO)),
    )
    for ref, first in places:
        for f in range(fields):
            for r in range(HALO):
                part = lax.dot_general(
                    factor, ref[f * HALO + r], (((1,), (0,)), ((), ())), preferred_element_type=jnp.float32
                )
                combined[f, pl.ds(first + r, 1)] = jnp.sum(part, axis=0, keepdims=True)

    latitude = band_ref[0] * rows - HALO + lax.broadcasted_iota(jnp.int32, (extended, lon), 0)
    present = (latitude >= 0) & (latitude < rows * bands)
    turn = 0.5 * coriolis_coef * (2.0 * (latitude.astype(jnp.float32) + 0.5) / (rows * bands) - 1.0)
    depth, east, north = (coef_ref[f] for f in range(3))
    h, u, v = 0.25 * combined[0], combined[1], combined[2]

    def lat_difference(x):
        return pltpu.roll(x, extended - 1, 0) - pltpu.roll(x, 1, 0)

    for _ in range(STEPS):
        dxh, dxu, dxv = (lon_difference(x) for x in (h, u, v))
        dyh, dyu, dyv = (lat_difference(x) for x in (h, u, v))
        new_u = (u + turn * v) - dxh - east * dxu - north * dyu
        new_v = (v - turn * u) - dyh - east * dxv - north * dyv
        new_h = h - depth * (dxu + dyv) - east * dxh - north * dyh
        h, u, v = (jnp.where(present, x, 0.0) for x in (new_h, new_u, new_v))
    own = slice(HALO, HALO + rows)
    for f, value in enumerate((4.0 * h, u, v)):
        increment[0, f] = value[own]
    copies.append(pltpu.make_async_copy(increment, increment_hbm, sems.at[2]))
    copies[-1].start()
    for copy in copies:
        copy.wait()


def combine(group, band, core, shares, halves, coef, scale, bands):
    fields, extended, lon = coef.shape
    rows = extended - 2 * HALO
    rank = halves[0].shape[1]
    return pl.pallas_call(
        functools.partial(combine_kernel, scale, len(shares), bands),
        out_shape=(
            jax.ShapeDtypeStruct((1, fields, rows, lon), jnp.float32),
            jax.ShapeDtypeStruct((1, rank), jnp.float32),
            jax.ShapeDtypeStruct((1, 2 * rank), jnp.float32),
        ),
        in_specs=[SMEM] * 3 + [VMEM] * (len(shares) + 5),
        out_specs=(HBM,) * 3,
        scratch_shapes=[
            pltpu.VMEM((1, fields, rows, lon), jnp.float32),
            pltpu.VMEM((1, rank), jnp.float32),
            pltpu.VMEM((1, 2 * rank), jnp.float32),
            pltpu.VMEM((fields, extended, lon), jnp.float32),
            pltpu.SemaphoreType.DMA((3,)),
        ],
        compiler_params=pltpu.CompilerParams(vmem_limit_bytes=8 * MIB),
        name="combine",
    )(group, band, core, *shares, *halves, coef)


def from_ahead(x, axis, by):
    count = lax.axis_size(axis)
    return lax.ppermute(x, axis, [((i + by) % count, i) for i in range(count)])


def added_over(x, axis):
    others = [from_ahead(x, axis, by) for by in range(1, lax.axis_size(axis))]
    return functools.reduce(jnp.add, others, x)


def body(
    sketch, test_sketch, checkpoints, checkpoint_step, station_row, station_column, station_value
):
    rank, fields, rows, lon = sketch.shape
    bands = lax.axis_size(LAT)
    groups = lax.axis_size("tm")
    total_rows = rows * bands
    observed = station_row.shape[1] * bands
    band = lax.axis_index(LAT).astype(jnp.int32).reshape(1)
    core = lax.axis_index("lat_2").astype(jnp.int32).reshape(1)
    group = lax.axis_index("tm").astype(jnp.int32).reshape(1)

    outer, inner, outer_base, inner_base, base = pack(sketch, checkpoints, checkpoint_step, core)
    across_chips = [pair for i in range(1, bands - 1, 2) for pair in ((i, i + 1), (i + 1, i))]
    inside_chip = [(0, 1), (1, 0)]
    far_outer = lax.ppermute(outer, LAT, across_chips)
    far_outer_base = lax.ppermute(outer_base, LAT, across_chips)
    far_inner_base = lax.ppermute(inner_base, "lat_2", inside_chip)
    far_inner = lax.ppermute(inner, "lat_2", inside_chip)
    field, cost = observe(
        band, base, station_row, station_column, station_value, (total_rows, observed, groups)
    )
    scale = map_scale / math.sqrt(rank * fields * total_rows * lon)
    back, coef, own = sweep(
        band, core, test_sketch, base, far_outer_base, far_inner_base, outer, inner, field, cost, scale, bands
    )
    far_outer, far_inner, share = join(core, back, own, far_outer, far_inner, scale)
    for axis in ("lat_2", "lat_1", "lat_0"):
        share = added_over(share, axis)
    shares = [share] + [from_ahead(share, "tm", by) for by in range(1, groups)]
    increment, adjoint, total_cost = combine(
        group, band, core, shares, (outer, inner, far_outer, far_inner), coef, 1.0 / math.sqrt(rank), bands
    )
    return (increment, adjoint, total_cost[0, 0])


def solution(mesh):
    torus = Mesh(mesh.devices.reshape(mesh.shape["tm"], 4, 4, 2), ("tm", "lat_0", "lat_1", "lat_2"))
    in_specs = (
        P("tm", None, LAT, None),
        P("tm", None, LAT, None),
        P("tm", None, LAT, None),
        P("tm"),
        P("tm", LAT),
        P("tm", LAT),
        P("tm", LAT),
    )
    out_specs = (P("tm", None, LAT, None), P("tm", None), P())
    return jax.shard_map(body, mesh=torus, in_specs=in_specs, out_specs=out_specs, check_vma=False)
```

profile of v0, /device:TPU:0, one launch (start us, length us, event | category | flops | bytes accessed | tf_op | source)
XLA Modules:
  0.0 94.9 jit_solution(7417139175095635692)
XLA Ops:
  1.3 1.9 %copy-done = bf16[64,3,8,1024]{3,2,1,0:T(8,128)(2,1)S(1)} copy-done((bf16[64,3,8,1024]{3,2,1,0:T(8,128)(2,1)S(1)}, bf16[64,3,8,1024]{3,2,1,0:T(8,128)(2,1)}, u32[]{:S(2)}) %copy-start) | copy-done | bytes 3145752
  4.1 1.8 %pack.1 = (bf16[12,64,1024]{2,1,0:T(8,128)(2,1)S(1)}, bf16[12,64,1024]{2,1,0:T(8,128)(2,1)S(1)}, bf16[16,1024]{1,0:T(8,128)(2,1)S(1)}, bf16[16,1024]{1,0:T(8,128)(2,1)S(1)}, f32[3,8,1024]{2,1,0:T(8,128)S(1)}) custom-call(s32[1]{0:T(128)S(6)} %copy.10.step_ref, s32[1]{0:T(128)} %bitcast.2.core_ref, bf16[64,3,8,1024]{3,2,1,0:T(8,128)(2,1)S(1)} %copy-done, ...), custom_call_target="tpu_custom_call" | custom-call | tf_op jit(solution)/shard_map/pack/pallas_call | solution.py:89
  5.9 1.8 %collective-permute-start.2 = (bf16[12,64,1024]{2,1,0:T(8,128)(2,1)S(1)}, bf16[12,64,1024]{2,1,0:T(8,128)(2,1)}, u32[]{:S(2)}, u32[]{:S(2)}) collective-permute-start(bf16[12,64,1024]{2,1,0:T(8,128)(2,1)S(1)} %get-tuple-element.22.outer_ref.refs_4_), channel_id=1, source_target_pairs={{1,2},{2,1},{3,4},{4,3},{5,6},{6,5},{7,8},{8,7},{9,10},{10,9},{11,... | collective-permute-start | bytes 4718600 | tf_op jit(solution)/shard_map/ppermute | solution.py:496
  7.8 1.9 %collective-permute-start.3 = (bf16[12,64,1024]{2,1,0:T(8,128)(2,1)S(1)}, bf16[12,64,1024]{2,1,0:T(8,128)(2,1)}, u32[]{:S(2)}, u32[]{:S(2)}) collective-permute-start(bf16[12,64,1024]{2,1,0:T(8,128)(2,1)S(1)} %get-tuple-element.23.inner_ref.refs_5_), channel_id=1, source_target_pairs={{0,1},{1,0},{2,3},{3,2},{4,5},{5,4},{6,7},{7,6},{8,9},{9,8},{10,11... | collective-permute-start | bytes 4718600 | tf_op jit(solution)/shard_map/ppermute | solution.py:499
  10.4 3.2 %collective-permute-start.1 = (bf16[16,1024]{1,0:T(8,128)(2,1)S(1)}, bf16[16,1024]{1,0:T(8,128)(2,1)S(1)}, u32[]{:S(2)}, u32[]{:S(2)}) collective-permute-start(bf16[16,1024]{1,0:T(8,128)(2,1)S(1)} %get-tuple-element.21), channel_id=1, source_target_pairs={{0,1},{1,0},{2,3},{3,2},{4,5},{5,4},{6,7},{7,6},{8,9},{9,8},{10,11... | collective-permute-start | bytes 98312 | tf_op jit(solution)/shard_map/ppermute | solution.py:498
  14.4 1.9 %copy-done.9 = bf16[64,3,8,1024]{3,2,1,0:T(8,128)(2,1)S(1)} copy-done((bf16[64,3,8,1024]{3,2,1,0:T(8,128)(2,1)S(1)}, bf16[64,3,8,1024]{3,2,1,0:T(8,128)(2,1)}, u32[]{:S(2)}) %copy-start.9) | copy-done | bytes 3145752
  16.3 24.7 %sweep.1 = (bf16[48,128,1024]{2,1,0:T(8,128)(2,1)S(1)}, f32[3,16,1024]{2,1,0:T(8,128)S(1)}, f32[72,64]{1,0:T(8,128)S(1)}) custom-call(s32[1]{0:T(128)} %bitcast.1.band_ref, s32[1]{0:T(128)} %bitcast.2.core_ref, bf16[64,3,8,1024]{3,2,1,0:T(8,128)(2,1)S(1)} %copy-done.9, f32[3,8,1024]{2,1,0:T(8,128)S(1)} %get-tuple-element.19.base_ref, ...), custom_call_target="tpu_custom_call" | custom-call | flops 2000000000 | bytes 30000000 | tf_op jit(solution)/shard_map/sweep/pallas_call | solution.py:280
  41.1 4.7 %join.1 = (bf16[12,64,1024]{2,1,0:T(8,128)(2,1)S(1)}, bf16[12,64,1024]{2,1,0:T(8,128)(2,1)S(1)}, f32[40,128]{1,0:T(8,128)S(1)}) custom-call(s32[1]{0:T(128)} %bitcast.2.core_ref, bf16[48,128,1024]{2,1,0:T(8,128)(2,1)S(1)} %get-tuple-element.26.back_ref, f32[72,64]{1,0:T(8,128)S(1)} %get-tuple-element.27.own_ref, ...), custom_call_target="tpu_custom_call" | custom-call | tf_op jit(solution)/shard_map/join/pallas_call | solution.py:337
  45.8 1.2 %copy-done.1 = bf16[12,64,1024]{2,1,0:T(8,128)(2,1)} copy-done((bf16[12,64,1024]{2,1,0:T(8,128)(2,1)}, bf16[12,64,1024]{2,1,0:T(8,128)(2,1)S(1)}, u32[]{:S(2)}) %copy-start.1) | copy-done | bytes 1572888
  48.1 13.6 %collective-permute-start.4 = (f32[40,128]{1,0:T(8,128)S(1)}, f32[40,128]{1,0:T(8,128)S(1)}, u32[]{:S(2)}, u32[]{:S(2)}) collective-permute-start(f32[40,128]{1,0:T(8,128)S(1)} %get-tuple-element.28), channel_id=1, source_target_pairs={{1,0},{0,1},{3,2},{2,3},{5,4},{4,5},{7,6},{6,7},{9,8},{8,9},{11,10... | collective-permute-start | bytes 61448 | tf_op jit(solution)/shard_map/ppermute | solution.py:473
  62.6 2.0 %collective-permute-start.7 = (f32[40,128]{1,0:T(8,128)S(1)}, f32[40,128]{1,0:T(8,128)S(1)}, u32[]{:S(2)}, u32[]{:S(2)}) collective-permute-start(f32[40,128]{1,0:T(8,128)S(1)} %add.29), channel_id=1, source_target_pairs={{6,0},{0,2},{2,4},{4,6},{7,1},{1,3},{3,5},{5,7},{14,8},{8,10},{10,... | collective-permute-start | bytes 61448 | tf_op jit(solution)/shard_map/ppermute | solution.py:473
  64.6 4.5 %collective-permute-start.6 = (f32[40,128]{1,0:T(8,128)S(1)}, f32[40,128]{1,0:T(8,128)S(1)}, u32[]{:S(2)}, u32[]{:S(2)}) collective-permute-start(f32[40,128]{1,0:T(8,128)S(1)} %add.29), channel_id=1, source_target_pairs={{4,0},{6,2},{0,4},{2,6},{5,1},{7,3},{1,5},{3,7},{12,8},{14,10},{8,... | collective-permute-start | bytes 61448 | tf_op jit(solution)/shard_map/ppermute | solution.py:473
  69.4 1.7 %collective-permute-done.6 = f32[40,128]{1,0:T(8,128)S(1)} collective-permute-done((f32[40,128]{1,0:T(8,128)S(1)}, f32[40,128]{1,0:T(8,128)S(1)}, u32[]{:S(2)}, u32[]{:S(2)}) %collective-permute-start.6) | collective-permute-done | bytes 20512 | tf_op jit(solution)/shard_map/ppermute | solution.py:473
  71.1 1.8 %collective-permute-done.5 = f32[40,128]{1,0:T(8,128)S(1)} collective-permute-done((f32[40,128]{1,0:T(8,128)S(1)}, f32[40,128]{1,0:T(8,128)S(1)}, u32[]{:S(2)}, u32[]{:S(2)}) %collective-permute-start.5) | collective-permute-done | bytes 20512 | tf_op jit(solution)/shard_map/ppermute | solution.py:473
  72.9 2.0 %collective-permute-start.10 = (f32[40,128]{1,0:T(8,128)S(1)}, f32[40,128]{1,0:T(8,128)S(1)}, u32[]{:S(2)}, u32[]{:S(2)}) collective-permute-start(f32[40,128]{1,0:T(8,128)S(1)} %add_add_fusion.1), channel_id=1, source_target_pairs={{24,0},{0,8},{8,16},{16,24},{25,1},{1,9},{9,17},{17,25},{26,2},{2,... | collective-permute-start | bytes 61448 | tf_op jit(solution)/shard_map/ppermute | solution.py:473
  74.9 2.0 %collective-permute-start.9 = (f32[40,128]{1,0:T(8,128)S(1)}, f32[40,128]{1,0:T(8,128)S(1)}, u32[]{:S(2)}, u32[]{:S(2)}) collective-permute-start(f32[40,128]{1,0:T(8,128)S(1)} %add_add_fusion.1), channel_id=1, source_target_pairs={{16,0},{24,8},{0,16},{8,24},{17,1},{25,9},{1,17},{9,25},{18,2},{26... | collective-permute-start | bytes 61448 | tf_op jit(solution)/shard_map/ppermute | solution.py:473
  76.9 2.5 %collective-permute-start.8 = (f32[40,128]{1,0:T(8,128)S(1)}, f32[40,128]{1,0:T(8,128)S(1)}, u32[]{:S(2)}, u32[]{:S(2)}) collective-permute-start(f32[40,128]{1,0:T(8,128)S(1)} %add_add_fusion.1), channel_id=1, source_target_pairs={{8,0},{16,8},{24,16},{0,24},{9,1},{17,9},{25,17},{1,25},{10,2},{18... | collective-permute-start | bytes 61448 | tf_op jit(solution)/shard_map/ppermute | solution.py:473
  81.0 1.5 %collective-permute-start.13 = (f32[40,128]{1,0:T(8,128)S(1)}, f32[40,128]{1,0:T(8,128)S(1)}, u32[]{:S(2)}, u32[]{:S(2)}) collective-permute-start(f32[40,128]{1,0:T(8,128)S(1)} %add_add_fusion.refs_0_), channel_id=1, source_target_pairs={{96,0},{0,32},{32,64},{64,96},{97,1},{1,33},{33,65},{65,97},{98,2}... | collective-permute-start | bytes 61448 | tf_op jit(solution)/shard_map/ppermute | solution.py:473
  82.5 2.7 %collective-permute-start.12 = (f32[40,128]{1,0:T(8,128)S(1)}, f32[40,128]{1,0:T(8,128)S(1)}, u32[]{:S(2)}, u32[]{:S(2)}) collective-permute-start(f32[40,128]{1,0:T(8,128)S(1)} %add_add_fusion.refs_0_), channel_id=1, source_target_pairs={{64,0},{96,32},{0,64},{32,96},{65,1},{97,33},{1,65},{33,97},{66,2}... | collective-permute-start | bytes 61448 | tf_op jit(solution)/shard_map/ppermute | solution.py:473
  85.2 1.4 %collective-permute-start.11 = (f32[40,128]{1,0:T(8,128)S(1)}, f32[40,128]{1,0:T(8,128)S(1)}, u32[]{:S(2)}, u32[]{:S(2)}) collective-permute-start(f32[40,128]{1,0:T(8,128)S(1)} %add_add_fusion.refs_0_), channel_id=1, source_target_pairs={{32,0},{64,32},{96,64},{0,96},{33,1},{65,33},{97,65},{1,97},{34,2}... | collective-permute-start | bytes 61448 | tf_op jit(solution)/shard_map/ppermute | solution.py:473
  87.7 1.2 %collective-permute-done.11.refs_1_ = f32[40,128]{1,0:T(8,128)S(1)} collective-permute-done((f32[40,128]{1,0:T(8,128)S(1)}, f32[40,128]{1,0:T(8,128)S(1)}, u32[]{:S(2)}, u32[]{:S(2)}) %collective-permute-start.11) | collective-permute-done | bytes 20512 | tf_op jit(solution)/shard_map/ppermute | solution.py:473
  89.0 1.4 %copy-done.2 = bf16[12,64,1024]{2,1,0:T(8,128)(2,1)S(1)} copy-done((bf16[12,64,1024]{2,1,0:T(8,128)(2,1)S(1)}, bf16[12,64,1024]{2,1,0:T(8,128)(2,1)}, u32[]{:S(2)}) %copy-start.2) | copy-done | bytes 1572888
  90.4 1.4 %copy-done.4 = bf16[12,64,1024]{2,1,0:T(8,128)(2,1)S(1)} copy-done((bf16[12,64,1024]{2,1,0:T(8,128)(2,1)S(1)}, bf16[12,64,1024]{2,1,0:T(8,128)(2,1)}, u32[]{:S(2)}) %copy-start.4) | copy-done | bytes 1572888
  91.8 2.9 %combine.1 = (f32[1,3,8,1024]{3,2,1,0:T(8,128)}, f32[1,64]{1,0:T(1,128)}, f32[1,128]{1,0:T(1,128)}) custom-call(s32[1]{0:T(128)} %bitcast.group_ref, s32[1]{0:T(128)} %bitcast.1.band_ref, s32[1]{0:T(128)} %bitcast.2.core_ref, f32[40,128]{1,0:T(8,128)S(1)} %add_add_fusion.refs_0_, f32[40,128]{1,0:T(8,128)S(1)} %collective-permute-done.11.refs_1_, ...), custom_call_target="tpu_custom_call" | custom-call | tf_op jit(solution)/shard_map/combine/pallas_call | solution.py:450
  (32 shorter events, 7.3 us)
Async XLA Ops:
  1.3 1.9 %copy-start = (bf16[64,3,8,1024]{3,2,1,0:T(8,128)(2,1)S(1)}, bf16[64,3,8,1024]{3,2,1,0:T(8,128)(2,1)}, u32[]{:S(2)}) copy-start(bf16[64,3,8,1024]{3,2,1,0:T(8,128)(2,1)} %sketch_hbm.1) | copy-start | bytes 9437188
  3.2 0.9 copy-start.5
  4.1 9.5 %copy-start.6 = (s32[1,128]{1,0:T(1,128)S(1)}, s32[1,128]{1,0:T(1,128)}, u32[]{:S(2)}) copy-start(s32[1,128]{1,0:T(1,128)} %row_ref.1) | copy-start | bytes 1540
  4.1 9.5 %copy-start.7 = (s32[1,128]{1,0:T(1,128)S(1)}, s32[1,128]{1,0:T(1,128)}, u32[]{:S(2)}) copy-start(s32[1,128]{1,0:T(1,128)} %column_ref.1) | copy-start | bytes 1540
  4.1 9.5 %copy-start.8 = (f32[1,128]{1,0:T(1,128)S(1)}, f32[1,128]{1,0:T(1,128)}, u32[]{:S(2)}) copy-start(f32[1,128]{1,0:T(1,128)} %value_ref.1) | copy-start | bytes 1540
  5.9 35.1 %collective-permute-start.2 = (bf16[12,64,1024]{2,1,0:T(8,128)(2,1)S(1)}, bf16[12,64,1024]{2,1,0:T(8,128)(2,1)}, u32[]{:S(2)}, u32[]{:S(2)}) collective-permute-start(bf16[12,64,1024]{2,1,0:T(8,128)(2,1)S(1)} %get-tuple-element.22.outer_ref.refs_4_), channel_id=1, source_target_pairs={{1,2},{2,1},{3,4},{4,3},{5,6},{6,5},{7,8},{8,7},{9,10},{10,9},{11,... | collective-permute-start | bytes 4718600 | tf_op jit(solution)/shard_map/ppermute | solution.py:496
  7.8 33.3 %collective-permute-start.3 = (bf16[12,64,1024]{2,1,0:T(8,128)(2,1)S(1)}, bf16[12,64,1024]{2,1,0:T(8,128)(2,1)}, u32[]{:S(2)}, u32[]{:S(2)}) collective-permute-start(bf16[12,64,1024]{2,1,0:T(8,128)(2,1)S(1)} %get-tuple-element.23.inner_ref.refs_5_), channel_id=1, source_target_pairs={{0,1},{1,0},{2,3},{3,2},{4,5},{5,4},{6,7},{7,6},{8,9},{9,8},{10,11... | collective-permute-start | bytes 4718600 | tf_op jit(solution)/shard_map/ppermute | solution.py:499
  9.7 4.4 %collective-permute-start = (bf16[16,1024]{1,0:T(8,128)(2,1)S(1)}, bf16[16,1024]{1,0:T(8,128)(2,1)S(1)}, u32[]{:S(2)}, u32[]{:S(2)}) collective-permute-start(bf16[16,1024]{1,0:T(8,128)(2,1)S(1)} %get-tuple-element.20), channel_id=1, source_target_pairs={{1,2},{2,1},{3,4},{4,3},{5,6},{6,5},{7,8},{8,7},{9,10},{10,9},{11,... | collective-permute-start | bytes 98312 | tf_op jit(solution)/shard_map/ppermute | solution.py:497
  10.4 4.1 %collective-permute-start.1 = (bf16[16,1024]{1,0:T(8,128)(2,1)S(1)}, bf16[16,1024]{1,0:T(8,128)(2,1)S(1)}, u32[]{:S(2)}, u32[]{:S(2)}) collective-permute-start(bf16[16,1024]{1,0:T(8,128)(2,1)S(1)} %get-tuple-element.21), channel_id=1, source_target_pairs={{0,1},{1,0},{2,3},{3,2},{4,5},{5,4},{6,7},{7,6},{8,9},{9,8},{10,11... | collective-permute-start | bytes 98312 | tf_op jit(solution)/shard_map/ppermute | solution.py:498
  14.4 1.9 %copy-start.9 = (bf16[64,3,8,1024]{3,2,1,0:T(8,128)(2,1)S(1)}, bf16[64,3,8,1024]{3,2,1,0:T(8,128)(2,1)}, u32[]{:S(2)}) copy-start(bf16[64,3,8,1024]{3,2,1,0:T(8,128)(2,1)} %test_hbm.1) | copy-start | bytes 9437188
  45.8 1.2 %copy-start.1 = (bf16[12,64,1024]{2,1,0:T(8,128)(2,1)}, bf16[12,64,1024]{2,1,0:T(8,128)(2,1)S(1)}, u32[]{:S(2)}) copy-start(bf16[12,64,1024]{2,1,0:T(8,128)(2,1)S(1)} %get-tuple-element.29.refs_6_) | copy-start | bytes 4718596
  47.0 1.1 %copy-start.3 = (bf16[12,64,1024]{2,1,0:T(8,128)(2,1)}, bf16[12,64,1024]{2,1,0:T(8,128)(2,1)S(1)}, u32[]{:S(2)}) copy-start(bf16[12,64,1024]{2,1,0:T(8,128)(2,1)S(1)} %get-tuple-element.30.refs_7_) | copy-start | bytes 4718596
  48.1 14.5 %collective-permute-start.4 = (f32[40,128]{1,0:T(8,128)S(1)}, f32[40,128]{1,0:T(8,128)S(1)}, u32[]{:S(2)}, u32[]{:S(2)}) collective-permute-start(f32[40,128]{1,0:T(8,128)S(1)} %get-tuple-element.28), channel_id=1, source_target_pairs={{1,0},{0,1},{3,2},{2,3},{5,4},{4,5},{7,6},{6,7},{9,8},{8,9},{11,10... | collective-permute-start | bytes 61448 | tf_op jit(solution)/shard_map/ppermute | solution.py:473
  62.6 6.8 %collective-permute-start.7 = (f32[40,128]{1,0:T(8,128)S(1)}, f32[40,128]{1,0:T(8,128)S(1)}, u32[]{:S(2)}, u32[]{:S(2)}) collective-permute-start(f32[40,128]{1,0:T(8,128)S(1)} %add.29), channel_id=1, source_target_pairs={{6,0},{0,2},{2,4},{4,6},{7,1},{1,3},{3,5},{5,7},{14,8},{8,10},{10,... | collective-permute-start | bytes 61448 | tf_op jit(solution)/shard_map/ppermute | solution.py:473
  64.6 6.5 %collective-permute-start.6 = (f32[40,128]{1,0:T(8,128)S(1)}, f32[40,128]{1,0:T(8,128)S(1)}, u32[]{:S(2)}, u32[]{:S(2)}) collective-permute-start(f32[40,128]{1,0:T(8,128)S(1)} %add.29), channel_id=1, source_target_pairs={{4,0},{6,2},{0,4},{2,6},{5,1},{7,3},{1,5},{3,7},{12,8},{14,10},{8,... | collective-permute-start | bytes 61448 | tf_op jit(solution)/shard_map/ppermute | solution.py:473
  69.1 3.8 %collective-permute-start.5 = (f32[40,128]{1,0:T(8,128)S(1)}, f32[40,128]{1,0:T(8,128)S(1)}, u32[]{:S(2)}, u32[]{:S(2)}) collective-permute-start(f32[40,128]{1,0:T(8,128)S(1)} %add.29), channel_id=1, source_target_pairs={{2,0},{4,2},{6,4},{0,6},{3,1},{5,3},{7,5},{1,7},{10,8},{12,10},{14... | collective-permute-start | bytes 61448 | tf_op jit(solution)/shard_map/ppermute | solution.py:473
  72.9 6.6 %collective-permute-start.10 = (f32[40,128]{1,0:T(8,128)S(1)}, f32[40,128]{1,0:T(8,128)S(1)}, u32[]{:S(2)}, u32[]{:S(2)}) collective-permute-start(f32[40,128]{1,0:T(8,128)S(1)} %add_add_fusion.1), channel_id=1, source_target_pairs={{24,0},{0,8},{8,16},{16,24},{25,1},{1,9},{9,17},{17,25},{26,2},{2,... | collective-permute-start | bytes 61448 | tf_op jit(solution)/shard_map/ppermute | solution.py:473
  74.9 5.3 %collective-permute-start.9 = (f32[40,128]{1,0:T(8,128)S(1)}, f32[40,128]{1,0:T(8,128)S(1)}, u32[]{:S(2)}, u32[]{:S(2)}) collective-permute-start(f32[40,128]{1,0:T(8,128)S(1)} %add_add_fusion.1), channel_id=1, source_target_pairs={{16,0},{24,8},{0,16},{8,24},{17,1},{25,9},{1,17},{9,25},{18,2},{26... | collective-permute-start | bytes 61448 | tf_op jit(solution)/shard_map/ppermute | solution.py:473
  76.9 4.0 %collective-permute-start.8 = (f32[40,128]{1,0:T(8,128)S(1)}, f32[40,128]{1,0:T(8,128)S(1)}, u32[]{:S(2)}, u32[]{:S(2)}) collective-permute-start(f32[40,128]{1,0:T(8,128)S(1)} %add_add_fusion.1), channel_id=1, source_target_pairs={{8,0},{16,8},{24,16},{0,24},{9,1},{17,9},{25,17},{1,25},{10,2},{18... | collective-permute-start | bytes 61448 | tf_op jit(solution)/shard_map/ppermute | solution.py:473
  81.0 5.7 %collective-permute-start.13 = (f32[40,128]{1,0:T(8,128)S(1)}, f32[40,128]{1,0:T(8,128)S(1)}, u32[]{:S(2)}, u32[]{:S(2)}) collective-permute-start(f32[40,128]{1,0:T(8,128)S(1)} %add_add_fusion.refs_0_), channel_id=1, source_target_pairs={{96,0},{0,32},{32,64},{64,96},{97,1},{1,33},{33,65},{65,97},{98,2}... | collective-permute-start | bytes 61448 | tf_op jit(solution)/shard_map/ppermute | solution.py:473
  82.5 5.3 %collective-permute-start.12 = (f32[40,128]{1,0:T(8,128)S(1)}, f32[40,128]{1,0:T(8,128)S(1)}, u32[]{:S(2)}, u32[]{:S(2)}) collective-permute-start(f32[40,128]{1,0:T(8,128)S(1)} %add_add_fusion.refs_0_), channel_id=1, source_target_pairs={{64,0},{96,32},{0,64},{32,96},{65,1},{97,33},{1,65},{33,97},{66,2}... | collective-permute-start | bytes 61448 | tf_op jit(solution)/shard_map/ppermute | solution.py:473
  85.2 3.8 %collective-permute-start.11 = (f32[40,128]{1,0:T(8,128)S(1)}, f32[40,128]{1,0:T(8,128)S(1)}, u32[]{:S(2)}, u32[]{:S(2)}) collective-permute-start(f32[40,128]{1,0:T(8,128)S(1)} %add_add_fusion.refs_0_), channel_id=1, source_target_pairs={{32,0},{64,32},{96,64},{0,96},{33,1},{65,33},{97,65},{1,97},{34,2}... | collective-permute-start | bytes 61448 | tf_op jit(solution)/shard_map/ppermute | solution.py:473
  89.0 1.4 %copy-start.2 = (bf16[12,64,1024]{2,1,0:T(8,128)(2,1)S(1)}, bf16[12,64,1024]{2,1,0:T(8,128)(2,1)}, u32[]{:S(2)}) copy-start(bf16[12,64,1024]{2,1,0:T(8,128)(2,1)} %copy-done.1) | copy-start | bytes 4718596
  90.4 1.4 %copy-start.4 = (bf16[12,64,1024]{2,1,0:T(8,128)(2,1)S(1)}, bf16[12,64,1024]{2,1,0:T(8,128)(2,1)}, u32[]{:S(2)}) copy-start(bf16[12,64,1024]{2,1,0:T(8,128)(2,1)} %copy-done.3) | copy-start | bytes 4718596
where the time goes:
time: 95.2 us; the launch traced here: 94.9 us
  starting transfers between devices  40 us (42%)
  Pallas kernels  34.7 us (36%)
  local copies, waits for them, and re-layouts  9.84 us (10%)
  waiting for transfers between devices  8.81 us (9%)
  between operations  1.55 us (2%)
    ppermute x10, starting transfers between devices, from_ahead(): return lax.ppermute(x, axis, [((i + by) % count, i) for i in range(count)])  32.3 us
    pallas_call x1, Pallas kernels, sweep(): pl.pallas_call(functools.partial(sweep_kernel, scale, bands), out_shape=(...  24.7 us
    unnamed x20, local copies, waits for them, and re-layouts  9.84 us
    ppermute x10, waiting for transfers between devices, from_ahead(): return lax.ppermute(x, axis, [((i + by) % count, i) for i in range(count)])  8.45 us
    pallas_call x1, Pallas kernels, join(): pl.pallas_call(functools.partial(join_kernel, scale), out_shape=(received...  4.74 us
    ppermute x1, starting transfers between devices, body(): far_inner_base = lax.ppermute(inner_base, 'lat_2', inside_chip)  3.2 us
    pallas_call x1, Pallas kernels, combine(): pl.pallas_call(functools.partial(combine_kernel, scale, len(shares), band...  2.94 us
    ppermute x1, starting transfers between devices, body(): far_inner = lax.ppermute(inner, 'lat_2', inside_chip)  1.93 us
  transfers between devices with their start and end apart: 14, of which 9 were waited for; matrix products, arithmetic and copies ran while one was open for 0% of the time, Pallas kernels for 27%

commit v1 on v0

--- a/solution.py
+++ b/solution.py
@@ -41,64 +41,68 @@
     return lax.dot_general(a, b, (((1,), (1,)), ((), ())), preferred_element_type=jnp.float32)
 
 
-def pack_kernel(
-    step_ref, core_ref, sketch_hbm, base_hbm, outer_ref, inner_ref, outer_base, inner_base, base_ref, sketch, base, sems
-):
-    chunks = sketch.shape[0] // KC
+def on_hbm(x):
+    return pltpu.with_memory_space_constraint(x, pltpu.HBM)
+
+
+def pick_kernel(step_ref, core_ref, base_hbm, outer_base, inner_base, base_ref, base, sems):
+    fields = base.shape[0]
+    copy = pltpu.make_async_copy(base_hbm.at[step_ref[0]], base, sems.at[0])
+    copy.start()
+    copy.wait()
+    values = base[...].astype(jnp.float32)
+    base_ref[...] = values
+    pad = jnp.zeros((16 - fields * HALO, values.shape[-1]), jnp.float32)
+    for core in range(2):
+        low, high = (outer_base, inner_base) if core == 0 else (inner_base, outer_base)
+
+        @pl.when(core_ref[0] == core)
+        def _(low=low, high=high):
+            for ref, at in ((low, 0), (high, HALO)):
+                rows = [values[f, at : at + HALO] for f in range(fields)]
+                ref[...] = jnp.concatenate([*rows, pad], axis=0).astype(jnp.bfloat16)
+
+
+def pick(checkpoints, checkpoint_step, core):
+    _, fields, rows, lon = checkpoints.shape
+    lines = jax.ShapeDtypeStruct((16, lon), jnp.bfloat16)
+    return pl.pallas_call(
+        pick_kernel,
+        out_shape=(lines, lines, jax.ShapeDtypeStruct((fields, rows, lon), jnp.float32)),
+        in_specs=[SMEM, SMEM, HBM],
+        out_specs=(VMEM,) * 3,
+        scratch_shapes=[pltpu.VMEM((fields, rows, lon), jnp.bfloat16), pltpu.SemaphoreType.DMA((1,))],
+        compiler_params=pltpu.CompilerParams(vmem_limit_bytes=8 * MIB),
+        name="pick",
+    )(checkpoint_step, core, on_hbm(checkpoints))
+
+
+def pack_kernel(core_ref, sketch, first, second, outer_ref, inner_ref):
     fields = sketch.shape[1]
-
-    def copy(c):
-        at = pl.ds(c * KC, KC)
-        return pltpu.make_async_copy(sketch_hbm.at[at], sketch.at[at], sems.at[c])
-
-    base_copy = pltpu.make_async_copy(base_hbm.at[step_ref[0]], base, sems.at[chunks])
-    for c in range(chunks):
-        copy(c).start()
-    base_copy.start()
-    for c in range(chunks):
-        copy(c).wait()
-        for core in range(2):
-            low, high = (outer_ref, inner_ref) if core == 0 else (inner_ref, outer_ref)
-
-            @pl.when(core_ref[0] == core)
-            def _(c=c, low=low, high=high):
+    for core in range(2):
+        low, high = (outer_ref, inner_ref) if core == 0 else (inner_ref, outer_ref)
+
+        @pl.when(core_ref[0] == core)
+        def _(low=low, high=high):
+            for c in range(sketch.shape[0] // KC):
                 for f in range(fields):
                     part = jnp.swapaxes(sketch[c * KC : (c + 1) * KC, f].astype(jnp.float32), 0, 1)
                     part = part.astype(jnp.bfloat16)
                     for ref, rows in ((low, part[:HALO]), (high, part[HALO:])):
                         ref[f * HALO : (f + 1) * HALO, c * KC : (c + 1) * KC] = rows
 
-    base_copy.wait()
-    values = base[...].astype(jnp.float32)
-    base_ref[...] = values
-    pad = jnp.zeros((16 - fields * HALO, values.shape[-1]), jnp.float32)
-    for core in range(2):
-        low, high = (outer_base, inner_base) if core == 0 else (inner_base, outer_base)
-
-        @pl.when(core_ref[0] == core)
-        def _(low=low, high=high):
-            for ref, at in ((low, 0), (high, HALO)):
-                rows = [values[f, at : at + HALO] for f in range(fields)]
-                ref[...] = jnp.concatenate([*rows, pad], axis=0).astype(jnp.bfloat16)
-
-
-def pack(sketch, checkpoints, checkpoint_step, core):
+
+def pack(sketch, core, *first):
     rank, fields, rows, lon = sketch.shape
     half = jax.ShapeDtypeStruct((fields * HALO, rank, lon), jnp.bfloat16)
-    lines = jax.ShapeDtypeStruct((16, lon), jnp.bfloat16)
     return pl.pallas_call(
         pack_kernel,
-        out_shape=(half, half, lines, lines, jax.ShapeDtypeStruct((fields, rows, lon), jnp.float32)),
-        in_specs=[SMEM, SMEM, HBM, HBM],
-        out_specs=(VMEM,) * 5,
-        scratch_shapes=[
-            pltpu.VMEM(sketch.shape, jnp.bfloat16),
-            pltpu.VMEM((fields, rows, lon), jnp.bfloat16),
-            pltpu.SemaphoreType.DMA((rank // KC + 1,)),
-        ],
-        compiler_params=pltpu.CompilerParams(vmem_limit_bytes=12 * MIB),
+        out_shape=(half, half),
+        in_specs=[SMEM, VMEM, VMEM, VMEM],
+        out_specs=(VMEM,) * 2,
+        compiler_params=pltpu.CompilerParams(vmem_limit_bytes=8 * MIB),
         name="pack",
-    )(checkpoint_step, core, sketch, checkpoints)
+    )(core, sketch, *first)
 
 
 def observe_kernel(scales, band_ref, base_ref, row_ref, column_ref, value_ref, field_ref, cost_ref):
@@ -296,31 +300,28 @@
         compiler_params=pltpu.CompilerParams(vmem_limit_bytes=24 * MIB),
         cost_estimate=pl.CostEstimate(flops=2_000_000_000, bytes_accessed=30_000_000, transcendentals=0),
         name="sweep",
-    )(band, core, test_sketch, base, outer_base, inner_base, outer, inner, field, cost)
-
-
-def join_kernel(scale, core_ref, back_ref, own_ref, outer_hbm, inner_hbm, outer_ref, inner_ref, share_ref, sems):
+    )(band, core, on_hbm(test_sketch), base, outer_base, inner_base, outer, inner, field, cost)
+
+
+def join_kernel(scale, core_ref, back_ref, own_ref, outer_hbm, inner_hbm, share_ref, outer, inner, sems):
     rank = own_ref.shape[1]
     extended = back_ref.shape[0] // 3
     core = core_ref[0]
-    size = outer_ref.shape[0]
     pieces = 3
-    step = size // pieces
-    sides = ((inner_hbm, inner_ref, 1 - core), (outer_hbm, outer_ref, core))
-
-    def copy(n, side):
+    step = outer.shape[0] // pieces
+    sides = ((inner_hbm, inner, 1 - core), (outer_hbm, outer, core))
+
+    def copy(s, n):
         at = pl.ds(n * step, step)
-        return pltpu.make_async_copy(side[0].at[at], side[1].at[at], sems.at[n])
-
-    for s, side in enumerate(sides):
+        return pltpu.make_async_copy(sides[s][0].at[at], sides[s][1].at[at], sems.at[s * pieces + n])
+
+    for s in range(2):
         for n in range(pieces):
-            at = pl.ds(n * step, step)
-            pltpu.make_async_copy(side[0].at[at], side[1].at[at], sems.at[s * pieces + n]).start()
+            copy(s, n).start()
     share = jnp.zeros((2 * rank, rank), jnp.float32)
     for s, side in enumerate(sides):
         for n in range(pieces):
-            at = pl.ds(n * step, step)
-            pltpu.make_async_copy(side[0].at[at], side[1].at[at], sems.at[s * pieces + n]).wait()
+            copy(s, n).wait()
             for i in range(n * step, (n + 1) * step):
                 f, r = i // HALO, i % HALO
                 share += across(back_ref[f * extended + side[2] * (extended - HALO) + r], side[1][i])
@@ -333,16 +334,19 @@
 
 def join(core, back, own, outer, inner, scale):
     rank = own.shape[1]
-    received = jax.ShapeDtypeStruct(outer.shape, outer.dtype)
     return pl.pallas_call(
         functools.partial(join_kernel, scale),
-        out_shape=(received, received, jax.ShapeDtypeStruct((rank // 2 + 8, 2 * rank), jnp.float32)),
+        out_shape=jax.ShapeDtypeStruct((rank // 2 + 8, 2 * rank), jnp.float32),
         in_specs=[SMEM, VMEM, VMEM, HBM, HBM],
-        out_specs=(VMEM,) * 3,
-        scratch_shapes=[pltpu.SemaphoreType.DMA((6,))],
+        out_specs=VMEM,
+        scratch_shapes=[
+            pltpu.VMEM(outer.shape, outer.dtype),
+            pltpu.VMEM(inner.shape, inner.dtype),
+            pltpu.SemaphoreType.DMA((6,)),
+        ],
         compiler_params=pltpu.CompilerParams(vmem_limit_bytes=8 * MIB),
         name="join",
-    )(core, back, own, outer, inner)
+    )(core, back, own, on_hbm(outer), on_hbm(inner))
 
 
 def combine_kernel(
@@ -358,8 +362,8 @@
     (
         outer_ref,
         inner_ref,
-        far_outer_ref,
-        far_inner_ref,
+        far_outer_hbm,
+        far_inner_hbm,
         coef_ref,
         increment_hbm,
         adjoint_hbm,
@@ -368,8 +372,16 @@
         adjoint,
         cost_out,
         combined,
+        far_outer_ref,
+        far_inner_ref,
         sems,
     ) = refs[groups:]
+    arrivals = [
+        pltpu.make_async_copy(far_outer_hbm, far_outer_ref, sems.at[3]),
+        pltpu.make_async_copy(far_inner_hbm, far_inner_ref, sems.at[4]),
+    ]
+    for copy in arrivals:
+        copy.start()
     half = shares[0].shape[0] - 8
     rank = 2 * half
     fields, extended, lon = coef_ref.shape
@@ -410,7 +422,9 @@
         (far_outer_ref, core * (extended - HALO)),
         (far_inner_ref, (1 - core) * (extended - HALO)),
     )
-    for ref, first in places:
+    for n, (ref, first) in enumerate(places):
+        if n >= 2:
+            arrivals[n - 2].wait()
         for f in range(fields):
             for r in range(HALO):
                 part = lax.dot_general(
@@ -454,18 +468,20 @@
             jax.ShapeDtypeStruct((1, rank), jnp.float32),
             jax.ShapeDtypeStruct((1, 2 * rank), jnp.float32),
         ),
-        in_specs=[SMEM] * 3 + [VMEM] * (len(shares) + 5),
+        in_specs=[SMEM] * 3 + [VMEM] * (len(shares) + 2) + [HBM] * 2 + [VMEM],
         out_specs=(HBM,) * 3,
         scratch_shapes=[
             pltpu.VMEM((1, fields, rows, lon), jnp.float32),
             pltpu.VMEM((1, rank), jnp.float32),
             pltpu.VMEM((1, 2 * rank), jnp.float32),
             pltpu.VMEM((fields, extended, lon), jnp.float32),
-            pltpu.SemaphoreType.DMA((3,)),
+            pltpu.VMEM(halves[2].shape, halves[2].dtype),
+            pltpu.VMEM(halves[3].shape, halves[3].dtype),
+            pltpu.SemaphoreType.DMA((5,)),
         ],
         compiler_params=pltpu.CompilerParams(vmem_limit_bytes=8 * MIB),
         name="combine",
-    )(group, band, core, *shares, *halves, coef)
+    )(group, band, core, *shares, *halves[:2], *(on_hbm(x) for x in halves[2:]), coef)
 
 
 def from_ahead(x, axis, by):
@@ -490,12 +506,13 @@
     core = lax.axis_index("lat_2").astype(jnp.int32).reshape(1)
     group = lax.axis_index("tm").astype(jnp.int32).reshape(1)
 
-    outer, inner, outer_base, inner_base, base = pack(sketch, checkpoints, checkpoint_step, core)
+    outer_base, inner_base, base = pick(checkpoints, checkpoint_step, core)
     across_chips = [pair for i in range(1, bands - 1, 2) for pair in ((i, i + 1), (i + 1, i))]
     inside_chip = [(0, 1), (1, 0)]
-    far_outer = lax.ppermute(outer, LAT, across_chips)
     far_outer_base = lax.ppermute(outer_base, LAT, across_chips)
     far_inner_base = lax.ppermute(inner_base, "lat_2", inside_chip)
+    outer, inner = pack(sketch, core, far_outer_base, far_inner_base)
+    far_outer = lax.ppermute(outer, LAT, across_chips)
     far_inner = lax.ppermute(inner, "lat_2", inside_chip)
     field, cost = observe(
         band, base, station_row, station_column, station_value, (total_rows, observed, groups)
@@ -504,7 +521,7 @@
     back, coef, own = sweep(
         band, core, test_sketch, base, far_outer_base, far_inner_base, outer, inner, field, cost, scale, bands
     )
-    far_outer, far_inner, share = join(core, back, own, far_outer, far_inner, scale)
+    share = join(core, back, own, far_outer, far_inner, scale)
     for axis in ("lat_2", "lat_1", "lat_0"):
         share = added_over(share, axis)
     shares = [share] + [from_ahead(share, "tm", by) for by in range(1, groups)]

time: 95.2 us -> 79.5 us (0.84)
  starting transfers between devices: 40 us -> 24.7 us
  local copies, waits for them, and re-layouts: 9.84 us -> 1.91 us
  waiting for transfers between devices: 8.81 us -> 13.4 us
  Pallas kernels: 34.7 us -> 37.7 us
    ppermute x10, starting transfers between devices: 32.3 us -> 16.4 us  [from_ahead(): return lax.ppermute(x, axis, [((i + by) % count, i) for i in range(count)])]
    unnamed x20 -> x8, local copies, waits for them, and re-layouts: 9.84 us -> 1.91 us
    ppermute x10, waiting for transfers between devices: 8.45 us -> 12.5 us  [from_ahead(): return lax.ppermute(x, axis, [((i + by) % count, i) for i in range(count)])]
    pallas_call x1, Pallas kernels: 2.94 us -> 4.68 us  [combine(): pl.pallas_call(functools.partial(combine_kernel, scale, len(shares), band...]
    pallas_call x2 -> x3, Pallas kernels: 6.57 us -> 7.14 us  [the longest x1 4.74 us: join(): pl.pallas_call(functools.partial(join_kernel, scale), out_shape=jax.Shape...]
  transfers between devices with their start and end apart: 14 -> 14, of which waited for: 9 -> 8; matrix products, arithmetic and copies ran while one was open for 0% -> 0% of each run, Pallas kernels for 27% -> 33%
where the time goes in v1:
time: 79.5 us; the launch traced here: 79.2 us
  Pallas kernels  37.7 us (47%)
  starting transfers between devices  24.7 us (31%)
  waiting for transfers between devices  13.4 us (17%)
  local copies, waits for them, and re-layouts  1.91 us (2%)
  between operations  1.55 us (2%)
    pallas_call x1, Pallas kernels, sweep(): pl.pallas_call(functools.partial(sweep_kernel, scale, bands), out_shape=(...  25.4 us
    ppermute x10, starting transfers between devices, from_ahead(): return lax.ppermute(x, axis, [((i + by) % count, i) for i in range(count)])  16.4 us
    ppermute x10, waiting for transfers between devices, from_ahead(): return lax.ppermute(x, axis, [((i + by) % count, i) for i in range(count)])  12.5 us
    pallas_call x1, Pallas kernels, join(): pl.pallas_call(functools.partial(join_kernel, scale), out_shape=jax.Shape...  4.74 us
    pallas_call x1, Pallas kernels, combine(): pl.pallas_call(functools.partial(combine_kernel, scale, len(shares), band...  4.68 us
    ppermute x1, starting transfers between devices, body(): far_inner_base = lax.ppermute(inner_base, 'lat_2', inside_chip)  3.1 us
    ppermute x1, starting transfers between devices, body(): far_inner = lax.ppermute(inner, 'lat_2', inside_chip)  2.69 us
    unnamed x8, local copies, waits for them, and re-layouts  1.91 us
  transfers between devices with their start and end apart: 14, of which 8 were waited for; matrix products, arithmetic and copies ran while one was open for 0% of the time, Pallas kernels for 33%

profile of v1, /device:TPU:0, one launch (start us, length us, event | category | flops | bytes accessed | tf_op | source)
XLA Modules:
  0.0 79.2 jit_solution(9251955086754165846)
XLA Ops:
  1.3 0.8 %pick.1 = (bf16[16,1024]{1,0:T(8,128)(2,1)S(1)}, bf16[16,1024]{1,0:T(8,128)(2,1)S(1)}, f32[3,8,1024]{2,1,0:T(8,128)S(1)}) custom-call(s32[1]{0:T(128)S(6)} %copy.10.step_ref, s32[1]{0:T(128)} %bitcast.2.core_ref, bf16[4,3,8,1024]{3,2,1,0:T(8,128)(2,1)} %base_hbm.1), custom_call_target="tpu_custom_call" | custom-call | tf_op jit(solution)/shard_map/pick/pallas_call | solution.py:69
  2.1 0.7 collective-permute-start
  2.8 3.1 %collective-permute-start.1 = (bf16[16,1024]{1,0:T(8,128)(2,1)S(1)}, bf16[16,1024]{1,0:T(8,128)(2,1)S(1)}, u32[]{:S(2)}, u32[]{:S(2)}) collective-permute-start(bf16[16,1024]{1,0:T(8,128)(2,1)S(1)} %get-tuple-element.18), channel_id=1, source_target_pairs={{0,1},{1,0},{2,3},{3,2},{4,5},{5,4},{6,7},{7,6},{8,9},{9,8},{10,11... | collective-permute-start | bytes 98312 | tf_op jit(solution)/shard_map/ppermute | solution.py:513
  5.9 0.9 %collective-permute-done.1.second.inner_base = bf16[16,1024]{1,0:T(8,128)(2,1)S(1)} collective-permute-done((bf16[16,1024]{1,0:T(8,128)(2,1)S(1)}, bf16[16,1024]{1,0:T(8,128)(2,1)S(1)}, u32[]{:S(2)}, u32[]{:S(2)}) %collective-permute-start.1) | collective-permute-done | bytes 32800 | tf_op jit(solution)/shard_map/ppermute | solution.py:513
  6.8 1.9 %copy-done = bf16[64,3,8,1024]{3,2,1,0:T(8,128)(2,1)S(1)} copy-done((bf16[64,3,8,1024]{3,2,1,0:T(8,128)(2,1)S(1)}, bf16[64,3,8,1024]{3,2,1,0:T(8,128)(2,1)}, u32[]{:S(2)}) %copy-start) | copy-done | bytes 3145752
  8.7 1.6 %pack.1 = (bf16[12,64,1024]{2,1,0:T(8,128)(2,1)S(1)}, bf16[12,64,1024]{2,1,0:T(8,128)(2,1)S(1)}) custom-call(s32[1]{0:T(128)} %bitcast.2.core_ref, bf16[64,3,8,1024]{3,2,1,0:T(8,128)(2,1)S(1)} %copy-done, bf16[16,1024]{1,0:T(8,128)(2,1)S(1)} %collective-permute-done.first.outer_base, bf16[16,1024]{1,0:T(8,128)(2,1)S(1)} %collective-permute-done.1.second.inner_base), custom_call_target="tpu_custom_call" | custom-call | tf_op jit(solution)/shard_map/pack/pallas_call | solution.py:98
  10.3 1.8 %collective-permute-start.2 = (bf16[12,64,1024]{2,1,0:T(8,128)(2,1)S(1)}, bf16[12,64,1024]{2,1,0:T(8,128)(2,1)}, u32[]{:S(2)}, u32[]{:S(2)}) collective-permute-start(bf16[12,64,1024]{2,1,0:T(8,128)(2,1)S(1)} %get-tuple-element.19.outer_ref.refs_4_), channel_id=1, source_target_pairs={{1,2},{2,1},{3,4},{4,3},{5,6},{6,5},{7,8},{8,7},{9,10},{10,9},{11,... | collective-permute-start | bytes 4718600 | tf_op jit(solution)/shard_map/ppermute | solution.py:515
  12.1 2.7 %collective-permute-start.3 = (bf16[12,64,1024]{2,1,0:T(8,128)(2,1)S(1)}, bf16[12,64,1024]{2,1,0:T(8,128)(2,1)}, u32[]{:S(2)}, u32[]{:S(2)}) collective-permute-start(bf16[12,64,1024]{2,1,0:T(8,128)(2,1)S(1)} %get-tuple-element.20.inner_ref.refs_5_), channel_id=1, source_target_pairs={{0,1},{1,0},{2,3},{3,2},{4,5},{5,4},{6,7},{7,6},{8,9},{9,8},{10,11... | collective-permute-start | bytes 4718600 | tf_op jit(solution)/shard_map/ppermute | solution.py:516
  15.3 25.4 %sweep.1 = (bf16[48,128,1024]{2,1,0:T(8,128)(2,1)S(1)}, f32[3,16,1024]{2,1,0:T(8,128)S(1)}, f32[72,64]{1,0:T(8,128)S(1)}) custom-call(s32[1]{0:T(128)} %bitcast.1.band_ref, s32[1]{0:T(128)} %bitcast.2.core_ref, bf16[64,3,8,1024]{3,2,1,0:T(8,128)(2,1)} %test_hbm.1, f32[3,8,1024]{2,1,0:T(8,128)S(1)} %get-tuple-element.16.base_ref, ...), custom_call_target="tpu_custom_call" | custom-call | flops 2000000000 | bytes 30000000 | tf_op jit(solution)/shard_map/sweep/pallas_call | solution.py:284
  40.7 4.7 %join.1 = f32[40,128]{1,0:T(8,128)S(1)} custom-call(s32[1]{0:T(128)} %bitcast.2.core_ref, bf16[48,128,1024]{2,1,0:T(8,128)(2,1)S(1)} %get-tuple-element.23.back_ref, f32[72,64]{1,0:T(8,128)S(1)} %get-tuple-element.24.own_ref, bf16[12,64,1024]{2,1,0:T(8,128)(2,1)} %collective-permute-done.2.outer_hbm.refs_6_, ...), custom_call_target="tpu_custom_call" | custom-call | tf_op jit(solution)/shard_map/join/pallas_call | solution.py:337
  45.6 1.1 %collective-permute-done.4 = f32[40,128]{1,0:T(8,128)S(1)} collective-permute-done((f32[40,128]{1,0:T(8,128)S(1)}, f32[40,128]{1,0:T(8,128)S(1)}, u32[]{:S(2)}, u32[]{:S(2)}) %collective-permute-start.4) | collective-permute-done | bytes 20512 | tf_op jit(solution)/shard_map/ppermute | solution.py:489
  46.7 5.1 %collective-permute-start.5 = (f32[40,128]{1,0:T(8,128)S(1)}, f32[40,128]{1,0:T(8,128)S(1)}, u32[]{:S(2)}, u32[]{:S(2)}) collective-permute-start(f32[40,128]{1,0:T(8,128)S(1)} %add.29), channel_id=1, source_target_pairs={{2,0},{4,2},{6,4},{0,6},{3,1},{5,3},{7,5},{1,7},{10,8},{12,10},{14... | collective-permute-start | bytes 61448 | tf_op jit(solution)/shard_map/ppermute | solution.py:489
  51.9 0.9 %collective-permute-start.7 = (f32[40,128]{1,0:T(8,128)S(1)}, f32[40,128]{1,0:T(8,128)S(1)}, u32[]{:S(2)}, u32[]{:S(2)}) collective-permute-start(f32[40,128]{1,0:T(8,128)S(1)} %add.29), channel_id=1, source_target_pairs={{6,0},{0,2},{2,4},{4,6},{7,1},{1,3},{3,5},{5,7},{14,8},{8,10},{10,... | collective-permute-start | bytes 61448 | tf_op jit(solution)/shard_map/ppermute | solution.py:489
  52.8 0.5 collective-permute-done.5
  53.4 3.8 %collective-permute-done.6 = f32[40,128]{1,0:T(8,128)S(1)} collective-permute-done((f32[40,128]{1,0:T(8,128)S(1)}, f32[40,128]{1,0:T(8,128)S(1)}, u32[]{:S(2)}, u32[]{:S(2)}) %collective-permute-start.6) | collective-permute-done | bytes 20512 | tf_op jit(solution)/shard_map/ppermute | solution.py:489
  57.2 2.0 %collective-permute-start.10 = (f32[40,128]{1,0:T(8,128)S(1)}, f32[40,128]{1,0:T(8,128)S(1)}, u32[]{:S(2)}, u32[]{:S(2)}) collective-permute-start(f32[40,128]{1,0:T(8,128)S(1)} %add_add_fusion.1), channel_id=1, source_target_pairs={{24,0},{0,8},{8,16},{16,24},{25,1},{1,9},{9,17},{17,25},{26,2},{2,... | collective-permute-start | bytes 61448 | tf_op jit(solution)/shard_map/ppermute | solution.py:489
  59.2 1.3 %collective-permute-start.8 = (f32[40,128]{1,0:T(8,128)S(1)}, f32[40,128]{1,0:T(8,128)S(1)}, u32[]{:S(2)}, u32[]{:S(2)}) collective-permute-start(f32[40,128]{1,0:T(8,128)S(1)} %add_add_fusion.1), channel_id=1, source_target_pairs={{8,0},{16,8},{24,16},{0,24},{9,1},{17,9},{25,17},{1,25},{10,2},{18... | collective-permute-start | bytes 61448 | tf_op jit(solution)/shard_map/ppermute | solution.py:489
  60.5 2.4 %collective-permute-start.9 = (f32[40,128]{1,0:T(8,128)S(1)}, f32[40,128]{1,0:T(8,128)S(1)}, u32[]{:S(2)}, u32[]{:S(2)}) collective-permute-start(f32[40,128]{1,0:T(8,128)S(1)} %add_add_fusion.1), channel_id=1, source_target_pairs={{16,0},{24,8},{0,16},{8,24},{17,1},{25,9},{1,17},{9,25},{18,2},{26... | collective-permute-start | bytes 61448 | tf_op jit(solution)/shard_map/ppermute | solution.py:489
  62.9 2.8 %collective-permute-done.9 = f32[40,128]{1,0:T(8,128)S(1)} collective-permute-done((f32[40,128]{1,0:T(8,128)S(1)}, f32[40,128]{1,0:T(8,128)S(1)}, u32[]{:S(2)}, u32[]{:S(2)}) %collective-permute-start.9) | collective-permute-done | bytes 20512 | tf_op jit(solution)/shard_map/ppermute | solution.py:489
  65.8 2.8 %collective-permute-start.11 = (f32[40,128]{1,0:T(8,128)S(1)}, f32[40,128]{1,0:T(8,128)S(1)}, u32[]{:S(2)}, u32[]{:S(2)}) collective-permute-start(f32[40,128]{1,0:T(8,128)S(1)} %add_add_fusion.refs_0_), channel_id=1, source_target_pairs={{32,0},{64,32},{96,64},{0,96},{33,1},{65,33},{97,65},{1,97},{34,2}... | collective-permute-start | bytes 61448 | tf_op jit(solution)/shard_map/ppermute | solution.py:489
  68.6 0.8 %collective-permute-start.12 = (f32[40,128]{1,0:T(8,128)S(1)}, f32[40,128]{1,0:T(8,128)S(1)}, u32[]{:S(2)}, u32[]{:S(2)}) collective-permute-start(f32[40,128]{1,0:T(8,128)S(1)} %add_add_fusion.refs_0_), channel_id=1, source_target_pairs={{64,0},{96,32},{0,64},{32,96},{65,1},{97,33},{1,65},{33,97},{66,2}... | collective-permute-start | bytes 61448 | tf_op jit(solution)/shard_map/ppermute | solution.py:489
  69.4 0.9 %collective-permute-start.13 = (f32[40,128]{1,0:T(8,128)S(1)}, f32[40,128]{1,0:T(8,128)S(1)}, u32[]{:S(2)}, u32[]{:S(2)}) collective-permute-start(f32[40,128]{1,0:T(8,128)S(1)} %add_add_fusion.refs_0_), channel_id=1, source_target_pairs={{96,0},{0,32},{32,64},{64,96},{97,1},{1,33},{33,65},{65,97},{98,2}... | collective-permute-start | bytes 61448 | tf_op jit(solution)/shard_map/ppermute | solution.py:489
  70.3 3.6 %collective-permute-done.12.refs_2_ = f32[40,128]{1,0:T(8,128)S(1)} collective-permute-done((f32[40,128]{1,0:T(8,128)S(1)}, f32[40,128]{1,0:T(8,128)S(1)}, u32[]{:S(2)}, u32[]{:S(2)}) %collective-permute-start.12) | collective-permute-done | bytes 20512 | tf_op jit(solution)/shard_map/ppermute | solution.py:489
  74.4 4.7 %combine.1 = (f32[1,3,8,1024]{3,2,1,0:T(8,128)}, f32[1,64]{1,0:T(1,128)}, f32[1,128]{1,0:T(1,128)}) custom-call(s32[1]{0:T(128)} %bitcast.group_ref, s32[1]{0:T(128)} %bitcast.1.band_ref, s32[1]{0:T(128)} %bitcast.2.core_ref, f32[40,128]{1,0:T(8,128)S(1)} %add_add_fusion.refs_0_, f32[40,128]{1,0:T(8,128)S(1)} %collective-permute-done.11.refs_1_, ...), custom_call_target="tpu_custom_call" | custom-call | tf_op jit(solution)/shard_map/combine/pallas_call | solution.py:464
  (21 shorter events, 1.3 us)
Async XLA Ops:
  2.1 3.8 %collective-permute-start = (bf16[16,1024]{1,0:T(8,128)(2,1)S(1)}, bf16[16,1024]{1,0:T(8,128)(2,1)S(1)}, u32[]{:S(2)}, u32[]{:S(2)}) collective-permute-start(bf16[16,1024]{1,0:T(8,128)(2,1)S(1)} %get-tuple-element.17), channel_id=1, source_target_pairs={{1,2},{2,1},{3,4},{4,3},{5,6},{6,5},{7,8},{8,7},{9,10},{10,9},{11,... | collective-permute-start | bytes 98312 | tf_op jit(solution)/shard_map/ppermute | solution.py:512
  2.8 12.0 %copy-start.1 = (s32[1,128]{1,0:T(1,128)S(1)}, s32[1,128]{1,0:T(1,128)}, u32[]{:S(2)}) copy-start(s32[1,128]{1,0:T(1,128)} %row_ref.1) | copy-start | bytes 1540
  2.8 12.0 %copy-start.2 = (s32[1,128]{1,0:T(1,128)S(1)}, s32[1,128]{1,0:T(1,128)}, u32[]{:S(2)}) copy-start(s32[1,128]{1,0:T(1,128)} %column_ref.1) | copy-start | bytes 1540
  2.8 12.0 %copy-start.3 = (f32[1,128]{1,0:T(1,128)S(1)}, f32[1,128]{1,0:T(1,128)}, u32[]{:S(2)}) copy-start(f32[1,128]{1,0:T(1,128)} %value_ref.1) | copy-start | bytes 1540
  2.8 4.0 %collective-permute-start.1 = (bf16[16,1024]{1,0:T(8,128)(2,1)S(1)}, bf16[16,1024]{1,0:T(8,128)(2,1)S(1)}, u32[]{:S(2)}, u32[]{:S(2)}) collective-permute-start(bf16[16,1024]{1,0:T(8,128)(2,1)S(1)} %get-tuple-element.18), channel_id=1, source_target_pairs={{0,1},{1,0},{2,3},{3,2},{4,5},{5,4},{6,7},{7,6},{8,9},{9,8},{10,11... | collective-permute-start | bytes 98312 | tf_op jit(solution)/shard_map/ppermute | solution.py:513
  6.8 1.9 %copy-start = (bf16[64,3,8,1024]{3,2,1,0:T(8,128)(2,1)S(1)}, bf16[64,3,8,1024]{3,2,1,0:T(8,128)(2,1)}, u32[]{:S(2)}) copy-start(bf16[64,3,8,1024]{3,2,1,0:T(8,128)(2,1)} %sketch.1) | copy-start | bytes 9437188
  10.3 30.5 %collective-permute-start.2 = (bf16[12,64,1024]{2,1,0:T(8,128)(2,1)S(1)}, bf16[12,64,1024]{2,1,0:T(8,128)(2,1)}, u32[]{:S(2)}, u32[]{:S(2)}) collective-permute-start(bf16[12,64,1024]{2,1,0:T(8,128)(2,1)S(1)} %get-tuple-element.19.outer_ref.refs_4_), channel_id=1, source_target_pairs={{1,2},{2,1},{3,4},{4,3},{5,6},{6,5},{7,8},{8,7},{9,10},{10,9},{11,... | collective-permute-start | bytes 4718600 | tf_op jit(solution)/shard_map/ppermute | solution.py:515
  12.1 28.6 %collective-permute-start.3 = (bf16[12,64,1024]{2,1,0:T(8,128)(2,1)S(1)}, bf16[12,64,1024]{2,1,0:T(8,128)(2,1)}, u32[]{:S(2)}, u32[]{:S(2)}) collective-permute-start(bf16[12,64,1024]{2,1,0:T(8,128)(2,1)S(1)} %get-tuple-element.20.inner_ref.refs_5_), channel_id=1, source_target_pairs={{0,1},{1,0},{2,3},{3,2},{4,5},{5,4},{6,7},{7,6},{8,9},{9,8},{10,11... | collective-permute-start | bytes 4718600 | tf_op jit(solution)/shard_map/ppermute | solution.py:516
  45.5 1.3 %collective-permute-start.4 = (f32[40,128]{1,0:T(8,128)S(1)}, f32[40,128]{1,0:T(8,128)S(1)}, u32[]{:S(2)}, u32[]{:S(2)}) collective-permute-start(f32[40,128]{1,0:T(8,128)S(1)} %join.1), channel_id=1, source_target_pairs={{1,0},{0,1},{3,2},{2,3},{5,4},{4,5},{7,6},{6,7},{9,8},{8,9},{11,10... | collective-permute-start | bytes 61448 | tf_op jit(solution)/shard_map/ppermute | solution.py:489
  46.7 6.6 %collective-permute-start.5 = (f32[40,128]{1,0:T(8,128)S(1)}, f32[40,128]{1,0:T(8,128)S(1)}, u32[]{:S(2)}, u32[]{:S(2)}) collective-permute-start(f32[40,128]{1,0:T(8,128)S(1)} %add.29), channel_id=1, source_target_pairs={{2,0},{4,2},{6,4},{0,6},{3,1},{5,3},{7,5},{1,7},{10,8},{12,10},{14... | collective-permute-start | bytes 61448 | tf_op jit(solution)/shard_map/ppermute | solution.py:489
  51.9 5.3 %collective-permute-start.6 = (f32[40,128]{1,0:T(8,128)S(1)}, f32[40,128]{1,0:T(8,128)S(1)}, u32[]{:S(2)}, u32[]{:S(2)}) collective-permute-start(f32[40,128]{1,0:T(8,128)S(1)} %add.29), channel_id=1, source_target_pairs={{4,0},{6,2},{0,4},{2,6},{5,1},{7,3},{1,5},{3,7},{12,8},{14,10},{8,... | collective-permute-start | bytes 61448 | tf_op jit(solution)/shard_map/ppermute | solution.py:489
  51.9 5.3 %collective-permute-start.7 = (f32[40,128]{1,0:T(8,128)S(1)}, f32[40,128]{1,0:T(8,128)S(1)}, u32[]{:S(2)}, u32[]{:S(2)}) collective-permute-start(f32[40,128]{1,0:T(8,128)S(1)} %add.29), channel_id=1, source_target_pairs={{6,0},{0,2},{2,4},{4,6},{7,1},{1,3},{3,5},{5,7},{14,8},{8,10},{10,... | collective-permute-start | bytes 61448 | tf_op jit(solution)/shard_map/ppermute | solution.py:489
  57.2 5.7 %collective-permute-start.10 = (f32[40,128]{1,0:T(8,128)S(1)}, f32[40,128]{1,0:T(8,128)S(1)}, u32[]{:S(2)}, u32[]{:S(2)}) collective-permute-start(f32[40,128]{1,0:T(8,128)S(1)} %add_add_fusion.1), channel_id=1, source_target_pairs={{24,0},{0,8},{8,16},{16,24},{25,1},{1,9},{9,17},{17,25},{26,2},{2,... | collective-permute-start | bytes 61448 | tf_op jit(solution)/shard_map/ppermute | solution.py:489
  59.2 3.8 %collective-permute-start.8 = (f32[40,128]{1,0:T(8,128)S(1)}, f32[40,128]{1,0:T(8,128)S(1)}, u32[]{:S(2)}, u32[]{:S(2)}) collective-permute-start(f32[40,128]{1,0:T(8,128)S(1)} %add_add_fusion.1), channel_id=1, source_target_pairs={{8,0},{16,8},{24,16},{0,24},{9,1},{17,9},{25,17},{1,25},{10,2},{18... | collective-permute-start | bytes 61448 | tf_op jit(solution)/shard_map/ppermute | solution.py:489
  60.5 5.3 %collective-permute-start.9 = (f32[40,128]{1,0:T(8,128)S(1)}, f32[40,128]{1,0:T(8,128)S(1)}, u32[]{:S(2)}, u32[]{:S(2)}) collective-permute-start(f32[40,128]{1,0:T(8,128)S(1)} %add_add_fusion.1), channel_id=1, source_target_pairs={{16,0},{24,8},{0,16},{8,24},{17,1},{25,9},{1,17},{9,25},{18,2},{26... | collective-permute-start | bytes 61448 | tf_op jit(solution)/shard_map/ppermute | solution.py:489
  65.8 4.5 %collective-permute-start.11 = (f32[40,128]{1,0:T(8,128)S(1)}, f32[40,128]{1,0:T(8,128)S(1)}, u32[]{:S(2)}, u32[]{:S(2)}) collective-permute-start(f32[40,128]{1,0:T(8,128)S(1)} %add_add_fusion.refs_0_), channel_id=1, source_target_pairs={{32,0},{64,32},{96,64},{0,96},{33,1},{65,33},{97,65},{1,97},{34,2}... | collective-permute-start | bytes 61448 | tf_op jit(solution)/shard_map/ppermute | solution.py:489
  68.6 5.3 %collective-permute-start.12 = (f32[40,128]{1,0:T(8,128)S(1)}, f32[40,128]{1,0:T(8,128)S(1)}, u32[]{:S(2)}, u32[]{:S(2)}) collective-permute-start(f32[40,128]{1,0:T(8,128)S(1)} %add_add_fusion.refs_0_), channel_id=1, source_target_pairs={{64,0},{96,32},{0,64},{32,96},{65,1},{97,33},{1,65},{33,97},{66,2}... | collective-permute-start | bytes 61448 | tf_op jit(solution)/shard_map/ppermute | solution.py:489
  69.4 5.0 %collective-permute-start.13 = (f32[40,128]{1,0:T(8,128)S(1)}, f32[40,128]{1,0:T(8,128)S(1)}, u32[]{:S(2)}, u32[]{:S(2)}) collective-permute-start(f32[40,128]{1,0:T(8,128)S(1)} %add_add_fusion.refs_0_), channel_id=1, source_target_pairs={{96,0},{0,32},{32,64},{64,96},{97,1},{1,33},{33,65},{65,97},{98,2}... | collective-permute-start | bytes 61448 | tf_op jit(solution)/shard_map/ppermute | solution.py:489

commit v2 on v1

--- a/solution.py
+++ b/solution.py
@@ -77,14 +77,23 @@
     )(checkpoint_step, core, on_hbm(checkpoints))
 
 
-def pack_kernel(core_ref, sketch, first, second, outer_ref, inner_ref):
+def pack_kernel(core_ref, sketch_hbm, outer_ref, inner_ref, sketch, sems):
+    chunks = sketch.shape[0] // KC
     fields = sketch.shape[1]
-    for core in range(2):
-        low, high = (outer_ref, inner_ref) if core == 0 else (inner_ref, outer_ref)
-
-        @pl.when(core_ref[0] == core)
-        def _(low=low, high=high):
-            for c in range(sketch.shape[0] // KC):
+
+    def copy(c):
+        at = pl.ds(c * KC, KC)
+        return pltpu.make_async_copy(sketch_hbm.at[at], sketch.at[at], sems.at[c])
+
+    for c in range(chunks):
+        copy(c).start()
+    for c in range(chunks):
+        copy(c).wait()
+        for core in range(2):
+            low, high = (outer_ref, inner_ref) if core == 0 else (inner_ref, outer_ref)
+
+            @pl.when(core_ref[0] == core)
+            def _(c=c, low=low, high=high):
                 for f in range(fields):
                     part = jnp.swapaxes(sketch[c * KC : (c + 1) * KC, f].astype(jnp.float32), 0, 1)
                     part = part.astype(jnp.bfloat16)
@@ -92,17 +101,18 @@
                         ref[f * HALO : (f + 1) * HALO, c * KC : (c + 1) * KC] = rows
 
 
-def pack(sketch, core, *first):
+def pack(sketch, core):
     rank, fields, rows, lon = sketch.shape
     half = jax.ShapeDtypeStruct((fields * HALO, rank, lon), jnp.bfloat16)
     return pl.pallas_call(
         pack_kernel,
         out_shape=(half, half),
-        in_specs=[SMEM, VMEM, VMEM, VMEM],
+        in_specs=[SMEM, HBM],
         out_specs=(VMEM,) * 2,
+        scratch_shapes=[pltpu.VMEM(sketch.shape, sketch.dtype), pltpu.SemaphoreType.DMA((rank // KC,))],
         compiler_params=pltpu.CompilerParams(vmem_limit_bytes=8 * MIB),
         name="pack",
-    )(core, sketch, *first)
+    )(core, on_hbm(sketch))
 
 
 def observe_kernel(scales, band_ref, base_ref, row_ref, column_ref, value_ref, field_ref, cost_ref):
@@ -148,7 +158,6 @@
 
 
 def sweep_kernel(
-    scale,
     bands,
     band_ref,
     core_ref,
@@ -162,7 +171,7 @@
     cost_ref,
     back_ref,
     coef_ref,
-    share_ref,
+    tail_ref,
     test,
     one,
     two,
@@ -221,7 +230,20 @@
         beside = (edge + north * h, north * u, north * v + deep)
         return mine, beside
 
-    def backward_step(source, target, first, last, at):
+    def keep(target, c, e, f, half, total):
+        target[e, f, pl.ds(half * 8, 8)] = total
+
+    def keep_parts(target, c, e, f, half, total):
+        if f == 0:
+            total = 0.25 * total
+        upper = total.astype(jnp.bfloat16)
+        lower = (total - upper.astype(jnp.float32)).astype(jnp.bfloat16)
+        at = c * KC + half * 8
+        back_ref[f * extended + e, pl.ds(at, 8)] = upper
+        back_ref[f * extended + e, pl.ds(rank + at, 8)] = lower
+
+    def backward_step(source, target, first, last, c, half, store):
+        at = pl.ds(half * 8, 8)
         before = here = mine = None
         for e in range(first - 1, last + 2):
             after_mine, after = terms(source, e + 1, at) if e + 1 <= last else (None, None)
@@ -231,7 +253,7 @@
                     total = after[f] if total is None else total + after[f]
                 if before is not None:
                     total = -before[f] if total is None else total - before[f]
-                target[e, f, at] = total
+                store(target, c, e, f, half, total)
             before, here, mine = here, after, after_mine
 
     def chunk_body(c, carry):
@@ -245,48 +267,33 @@
                     one[HALO + r, f, at] = 4.0 * part[r] if f == 0 else part[r]
             source, target = one, two
             for step in range(STEPS):
-                backward_step(source, target, HALO - step, HALO + rows - 1 + step, at)
+                store = keep if step < STEPS - 1 else keep_parts
+                backward_step(source, target, HALO - step, HALO + rows - 1 + step, c, half, store)
                 source, target = target, source
-        for e in range(extended):
-            for f in range(fields):
-                value = one[e, f]
-                if f == 0:
-                    value = 0.25 * value
-                upper = value.astype(jnp.bfloat16)
-                lower = (value - upper.astype(jnp.float32)).astype(jnp.bfloat16)
-                back_ref[f * extended + e, pl.ds(c * KC, KC)] = upper
-                back_ref[f * extended + e, pl.ds(rank + c * KC, KC)] = lower
         return carry
 
     lax.fori_loop(0, rank // KC, chunk_body, 0)
 
-    share = jnp.zeros((2 * rank, rank), jnp.float32)
     forced = jnp.zeros((3 * rows, rank), jnp.float32)
     line = lax.broadcasted_iota(jnp.int32, (3 * rows, rank), 0) % rows
     field = field_ref[...].astype(jnp.bfloat16)
     for ref, first in ((outer_ref, core), (inner_ref, 1 - core)):
-        for f in range(fields):
-            for r in range(HALO):
-                columns = ref[f * HALO + r]
-                share += across(back_ref[f * extended + HALO + first * HALO + r], columns)
-                if f == 0:
-                    forced += jnp.where(line == first * HALO + r, across(field, columns), 0.0)
-    share = (share[:rank] + share[rank:]) * scale
-    share_ref[:rank] = share
+        for r in range(HALO):
+            forced += jnp.where(line == first * HALO + r, across(field, ref[r]), 0.0)
     lane = lax.broadcasted_iota(jnp.int32, (8, rank), 0)
     forced = jnp.sum(forced, axis=0, keepdims=True)
-    share_ref[rank:] = jnp.where(lane == 0, forced, jnp.where(lane == 1, cost_ref[0:1, :rank], 0.0))
-
-
-def sweep(band, core, test_sketch, base, outer_base, inner_base, outer, inner, field, cost, scale, bands):
+    tail_ref[...] = jnp.where(lane == 0, forced, jnp.where(lane == 1, cost_ref[0:1, :rank], 0.0))
+
+
+def sweep(band, core, test_sketch, base, outer_base, inner_base, outer, inner, field, cost, bands):
     rank, fields, rows, lon = test_sketch.shape
     extended = rows + 2 * HALO
     return pl.pallas_call(
-        functools.partial(sweep_kernel, scale, bands),
+        functools.partial(sweep_kernel, bands),
         out_shape=(
             jax.ShapeDtypeStruct((fields * extended, 2 * rank, lon), jnp.bfloat16),
             jax.ShapeDtypeStruct((fields, extended, lon), jnp.float32),
-            jax.ShapeDtypeStruct((rank + 8, rank), jnp.float32),
+            jax.ShapeDtypeStruct((8, rank), jnp.float32),
         ),
         in_specs=[SMEM, SMEM, HBM] + [VMEM] * 7,
         out_specs=(VMEM,) * 3,
@@ -303,8 +310,10 @@
     )(band, core, on_hbm(test_sketch), base, outer_base, inner_base, outer, inner, field, cost)
 
 
-def join_kernel(scale, core_ref, back_ref, own_ref, outer_hbm, inner_hbm, share_ref, outer, inner, sems):
-    rank = own_ref.shape[1]
+def join_kernel(
+    scale, core_ref, back_ref, tail_ref, outer_ref, inner_ref, outer_hbm, inner_hbm, share_ref, outer, inner, sems
+):
+    rank = tail_ref.shape[1]
     extended = back_ref.shape[0] // 3
     core = core_ref[0]
     pieces = 3
@@ -319,25 +328,29 @@
         for n in range(pieces):
             copy(s, n).start()
     share = jnp.zeros((2 * rank, rank), jnp.float32)
+    for ref, first in ((outer_ref, core), (inner_ref, 1 - core)):
+        for i in range(outer.shape[0]):
+            f, r = i // HALO, i % HALO
+            share += across(back_ref[f * extended + HALO + first * HALO + r], ref[i])
     for s, side in enumerate(sides):
         for n in range(pieces):
             copy(s, n).wait()
             for i in range(n * step, (n + 1) * step):
                 f, r = i // HALO, i % HALO
                 share += across(back_ref[f * extended + side[2] * (extended - HALO) + r], side[1][i])
-    share = own_ref[:rank] + (share[:rank] + share[rank:]) * scale
+    share = (share[:rank] + share[rank:]) * scale
     half = rank // 2
     share_ref[:half] = jnp.concatenate([share[:half], share[half:]], axis=1)
-    tail = own_ref[rank:]
+    tail = tail_ref[...]
     share_ref[half:] = jnp.concatenate([tail, tail], axis=1)
 
 
-def join(core, back, own, outer, inner, scale):
-    rank = own.shape[1]
+def join(core, back, tail, outer, inner, far_outer, far_inner, scale):
+    rank = tail.shape[1]
     return pl.pallas_call(
         functools.partial(join_kernel, scale),
         out_shape=jax.ShapeDtypeStruct((rank // 2 + 8, 2 * rank), jnp.float32),
-        in_specs=[SMEM, VMEM, VMEM, HBM, HBM],
+        in_specs=[SMEM, VMEM, VMEM, VMEM, VMEM, HBM, HBM],
         out_specs=VMEM,
         scratch_shapes=[
             pltpu.VMEM(outer.shape, outer.dtype),
@@ -346,7 +359,7 @@
         ],
         compiler_params=pltpu.CompilerParams(vmem_limit_bytes=8 * MIB),
         name="join",
-    )(core, back, own, on_hbm(outer), on_hbm(inner))
+    )(core, back, tail, outer, inner, on_hbm(far_outer), on_hbm(far_inner))
 
 
 def combine_kernel(
@@ -511,17 +524,20 @@
     inside_chip = [(0, 1), (1, 0)]
     far_outer_base = lax.ppermute(outer_base, LAT, across_chips)
     far_inner_base = lax.ppermute(inner_base, "lat_2", inside_chip)
-    outer, inner = pack(sketch, core, far_outer_base, far_inner_base)
+    outer, inner = pack(sketch, core)
+    outer, inner, far_outer_base, far_inner_base = lax.optimization_barrier(
+        (outer, inner, far_outer_base, far_inner_base)
+    )
     far_outer = lax.ppermute(outer, LAT, across_chips)
     far_inner = lax.ppermute(inner, "lat_2", inside_chip)
     field, cost = observe(
         band, base, station_row, station_column, station_value, (total_rows, observed, groups)
     )
     scale = map_scale / math.sqrt(rank * fields * total_rows * lon)
-    back, coef, own = sweep(
-        band, core, test_sketch, base, far_outer_base, far_inner_base, outer, inner, field, cost, scale, bands
-    )
-    share = join(core, back, own, far_outer, far_inner, scale)
+    back, coef, tail = sweep(
+        band, core, test_sketch, base, far_outer_base, far_inner_base, outer, inner, field, cost, bands
+    )
+    share = join(core, back, tail, outer, inner, far_outer, far_inner, scale)
     for axis in ("lat_2", "lat_1", "lat_0"):
         share = added_over(share, axis)
     shares = [share] + [from_ahead(share, "tm", by) for by in range(1, groups)]

time: 79.5 us -> 77 us (0.969)
  Pallas kernels: 37.7 us -> 39.9 us
  starting transfers between devices: 24.7 us -> 22.8 us
  local copies, waits for them, and re-layouts: 1.91 us -> 0.02 us
  waiting for transfers between devices: 13.4 us -> 12.5 us
    pallas_call x1, Pallas kernels: 4.74 us -> 7.77 us  [join(): pl.pallas_call(functools.partial(join_kernel, scale), out_shape=jax.Shape...]
    unnamed x8 -> x6, local copies, waits for them, and re-layouts: 1.91 us -> 0.02 us
    ppermute x10, starting transfers between devices: 16.4 us -> 15.2 us  [from_ahead(): return lax.ppermute(x, axis, [((i + by) % count, i) for i in range(count)])]
    pallas_call x2, Pallas kernels: 27 us -> 26.1 us  [the longest x1 23.4 us: sweep(): pl.pallas_call(functools.partial(sweep_kernel, bands), out_shape=(jax.Sha...]
    ppermute x1, waiting for transfers between devices: 0.86 us -> 0.01 us  [body(): far_inner_base = lax.ppermute(inner_base, 'lat_2', inside_chip)]
  transfers between devices with their start and end apart: 14 -> 14, of which waited for: 8 -> 7; matrix products, arithmetic and copies ran while one was open for 0% -> 0% of each run, Pallas kernels for 33% -> 35%
where the time goes in v2:
time: 77 us; the launch traced here: 76.8 us
  Pallas kernels  39.9 us (52%)
  starting transfers between devices  22.8 us (30%)
  waiting for transfers between devices  12.5 us (16%)
  between operations  1.56 us (2%)
    pallas_call x1, Pallas kernels, sweep(): pl.pallas_call(functools.partial(sweep_kernel, bands), out_shape=(jax.Sha...  23.4 us
    ppermute x10, starting transfers between devices, from_ahead(): return lax.ppermute(x, axis, [((i + by) % count, i) for i in range(count)])  15.2 us
    ppermute x10, waiting for transfers between devices, from_ahead(): return lax.ppermute(x, axis, [((i + by) % count, i) for i in range(count)])  12.5 us
    pallas_call x1, Pallas kernels, join(): pl.pallas_call(functools.partial(join_kernel, scale), out_shape=jax.Shape...  7.77 us
    pallas_call x1, Pallas kernels, combine(): pl.pallas_call(functools.partial(combine_kernel, scale, len(shares), band...  4.68 us
    ppermute x1, starting transfers between devices, body(): far_inner_base = lax.ppermute(inner_base, 'lat_2', inside_chip)  3.1 us
    pallas_call x1, Pallas kernels, pack(): pl.pallas_call(pack_kernel, out_shape=(half, half), in_specs=[SMEM, HBM],...  2.65 us
    ppermute x1, starting transfers between devices, body(): far_inner = lax.ppermute(inner, 'lat_2', inside_chip)  2.03 us
  transfers between devices with their start and end apart: 14, of which 7 were waited for; matrix products, arithmetic and copies ran while one was open for 0% of the time, Pallas kernels for 35%

profile of v2, /device:TPU:0, one launch (start us, length us, event | category | flops | bytes accessed | tf_op | source)
XLA Modules:
  0.0 76.8 jit_solution(17391617876911540164)
XLA Ops:
  1.3 0.8 %pick.1 = (bf16[16,1024]{1,0:T(8,128)(2,1)S(1)}, bf16[16,1024]{1,0:T(8,128)(2,1)S(1)}, f32[3,8,1024]{2,1,0:T(8,128)S(1)}) custom-call(s32[1]{0:T(128)S(6)} %copy.10.step_ref, s32[1]{0:T(128)} %bitcast.2.core_ref, bf16[4,3,8,1024]{3,2,1,0:T(8,128)(2,1)} %base_hbm.1), custom_call_target="tpu_custom_call" | custom-call | tf_op jit(solution)/shard_map/pick/pallas_call | solution.py:69
  2.1 0.7 collective-permute-start
  2.8 3.1 %collective-permute-start.1 = (bf16[16,1024]{1,0:T(8,128)(2,1)S(1)}, bf16[16,1024]{1,0:T(8,128)(2,1)S(1)}, u32[]{:S(2)}, u32[]{:S(2)}) collective-permute-start(bf16[16,1024]{1,0:T(8,128)(2,1)S(1)} %get-tuple-element.24), channel_id=1, source_target_pairs={{0,1},{1,0},{2,3},{3,2},{4,5},{5,4},{6,7},{7,6},{8,9},{9,8},{10,11... | collective-permute-start | bytes 98312 | tf_op jit(solution)/shard_map/ppermute | solution.py:526
  5.9 2.6 %pack.1 = (bf16[12,64,1024]{2,1,0:T(8,128)(2,1)S(1)}, bf16[12,64,1024]{2,1,0:T(8,128)(2,1)S(1)}) custom-call(s32[1]{0:T(128)} %bitcast.2.core_ref, bf16[64,3,8,1024]{3,2,1,0:T(8,128)(2,1)} %sketch_hbm.1), custom_call_target="tpu_custom_call" | custom-call | tf_op jit(solution)/shard_map/pack/pallas_call | solution.py:107
  8.6 1.8 %collective-permute-start.2 = (bf16[12,64,1024]{2,1,0:T(8,128)(2,1)S(1)}, bf16[12,64,1024]{2,1,0:T(8,128)(2,1)}, u32[]{:S(2)}, u32[]{:S(2)}) collective-permute-start(bf16[12,64,1024]{2,1,0:T(8,128)(2,1)S(1)} %get-tuple-element.27.outer_ref.refs_4_), channel_id=1, source_target_pairs={{1,2},{2,1},{3,4},{4,3},{5,6},{6,5},{7,8},{8,7},{9,10},{10,9},{11,... | collective-permute-start | bytes 4718600 | tf_op jit(solution)/shard_map/ppermute | solution.py:531
  10.4 2.0 %collective-permute-start.3 = (bf16[12,64,1024]{2,1,0:T(8,128)(2,1)S(1)}, bf16[12,64,1024]{2,1,0:T(8,128)(2,1)}, u32[]{:S(2)}, u32[]{:S(2)}) collective-permute-start(bf16[12,64,1024]{2,1,0:T(8,128)(2,1)S(1)} %get-tuple-element.28.inner_ref.refs_5_), channel_id=1, source_target_pairs={{0,1},{1,0},{2,3},{3,2},{4,5},{5,4},{6,7},{7,6},{8,9},{9,8},{10,11... | collective-permute-start | bytes 4718600 | tf_op jit(solution)/shard_map/ppermute | solution.py:532
  12.5 0.5 observe.1
  13.0 23.4 %sweep.1 = (bf16[48,128,1024]{2,1,0:T(8,128)(2,1)S(1)}, f32[3,16,1024]{2,1,0:T(8,128)S(1)}, f32[8,64]{1,0:T(8,128)S(1)}) custom-call(s32[1]{0:T(128)} %bitcast.1.band_ref, s32[1]{0:T(128)} %bitcast.2.core_ref, bf16[64,3,8,1024]{3,2,1,0:T(8,128)(2,1)} %test_hbm.1, f32[3,8,1024]{2,1,0:T(8,128)S(1)} %get-tuple-element.20.base_ref, ...), custom_call_target="tpu_custom_call" | custom-call | flops 2000000000 | bytes 30000000 | tf_op jit(solution)/shard_map/sweep/pallas_call | solution.py:291
  36.4 7.8 %join.1 = f32[40,128]{1,0:T(8,128)S(1)} custom-call(s32[1]{0:T(128)} %bitcast.2.core_ref, bf16[48,128,1024]{2,1,0:T(8,128)(2,1)S(1)} %get-tuple-element.31.back_ref, f32[8,64]{1,0:T(8,128)S(1)} %get-tuple-element.32.tail_ref, bf16[12,64,1024]{2,1,0:T(8,128)(2,1)S(1)} %get-tuple-element.27.outer_ref.refs_4_, ...), custom_call_target="tpu_custom_call" | custom-call | tf_op jit(solution)/shard_map/join/pallas_call | solution.py:350
  44.4 1.1 %collective-permute-done.4 = f32[40,128]{1,0:T(8,128)S(1)} collective-permute-done((f32[40,128]{1,0:T(8,128)S(1)}, f32[40,128]{1,0:T(8,128)S(1)}, u32[]{:S(2)}, u32[]{:S(2)}) %collective-permute-start.4) | collective-permute-done | bytes 20512 | tf_op jit(solution)/shard_map/ppermute | solution.py:502
  45.5 4.0 %collective-permute-start.5 = (f32[40,128]{1,0:T(8,128)S(1)}, f32[40,128]{1,0:T(8,128)S(1)}, u32[]{:S(2)}, u32[]{:S(2)}) collective-permute-start(f32[40,128]{1,0:T(8,128)S(1)} %add.29), channel_id=1, source_target_pairs={{2,0},{4,2},{6,4},{0,6},{3,1},{5,3},{7,5},{1,7},{10,8},{12,10},{14... | collective-permute-start | bytes 61448 | tf_op jit(solution)/shard_map/ppermute | solution.py:502
  49.4 0.9 %collective-permute-start.7 = (f32[40,128]{1,0:T(8,128)S(1)}, f32[40,128]{1,0:T(8,128)S(1)}, u32[]{:S(2)}, u32[]{:S(2)}) collective-permute-start(f32[40,128]{1,0:T(8,128)S(1)} %add.29), channel_id=1, source_target_pairs={{6,0},{0,2},{2,4},{4,6},{7,1},{1,3},{3,5},{5,7},{14,8},{8,10},{10,... | collective-permute-start | bytes 61448 | tf_op jit(solution)/shard_map/ppermute | solution.py:502
  50.4 0.5 collective-permute-done.5
  50.9 3.8 %collective-permute-done.6 = f32[40,128]{1,0:T(8,128)S(1)} collective-permute-done((f32[40,128]{1,0:T(8,128)S(1)}, f32[40,128]{1,0:T(8,128)S(1)}, u32[]{:S(2)}, u32[]{:S(2)}) %collective-permute-start.6) | collective-permute-done | bytes 20512 | tf_op jit(solution)/shard_map/ppermute | solution.py:502
  54.7 2.0 %collective-permute-start.10 = (f32[40,128]{1,0:T(8,128)S(1)}, f32[40,128]{1,0:T(8,128)S(1)}, u32[]{:S(2)}, u32[]{:S(2)}) collective-permute-start(f32[40,128]{1,0:T(8,128)S(1)} %add_add_fusion.1), channel_id=1, source_target_pairs={{24,0},{0,8},{8,16},{16,24},{25,1},{1,9},{9,17},{17,25},{26,2},{2,... | collective-permute-start | bytes 61448 | tf_op jit(solution)/shard_map/ppermute | solution.py:502
  56.7 1.3 %collective-permute-start.8 = (f32[40,128]{1,0:T(8,128)S(1)}, f32[40,128]{1,0:T(8,128)S(1)}, u32[]{:S(2)}, u32[]{:S(2)}) collective-permute-start(f32[40,128]{1,0:T(8,128)S(1)} %add_add_fusion.1), channel_id=1, source_target_pairs={{8,0},{16,8},{24,16},{0,24},{9,1},{17,9},{25,17},{1,25},{10,2},{18... | collective-permute-start | bytes 61448 | tf_op jit(solution)/shard_map/ppermute | solution.py:502
  58.1 2.4 %collective-permute-start.9 = (f32[40,128]{1,0:T(8,128)S(1)}, f32[40,128]{1,0:T(8,128)S(1)}, u32[]{:S(2)}, u32[]{:S(2)}) collective-permute-start(f32[40,128]{1,0:T(8,128)S(1)} %add_add_fusion.1), channel_id=1, source_target_pairs={{16,0},{24,8},{0,16},{8,24},{17,1},{25,9},{1,17},{9,25},{18,2},{26... | collective-permute-start | bytes 61448 | tf_op jit(solution)/shard_map/ppermute | solution.py:502
  60.5 2.8 %collective-permute-done.9 = f32[40,128]{1,0:T(8,128)S(1)} collective-permute-done((f32[40,128]{1,0:T(8,128)S(1)}, f32[40,128]{1,0:T(8,128)S(1)}, u32[]{:S(2)}, u32[]{:S(2)}) %collective-permute-start.9) | collective-permute-done | bytes 20512 | tf_op jit(solution)/shard_map/ppermute | solution.py:502
  63.3 2.8 %collective-permute-start.11 = (f32[40,128]{1,0:T(8,128)S(1)}, f32[40,128]{1,0:T(8,128)S(1)}, u32[]{:S(2)}, u32[]{:S(2)}) collective-permute-start(f32[40,128]{1,0:T(8,128)S(1)} %add_add_fusion.refs_0_), channel_id=1, source_target_pairs={{32,0},{64,32},{96,64},{0,96},{33,1},{65,33},{97,65},{1,97},{34,2}... | collective-permute-start | bytes 61448 | tf_op jit(solution)/shard_map/ppermute | solution.py:502
  66.2 0.8 %collective-permute-start.12 = (f32[40,128]{1,0:T(8,128)S(1)}, f32[40,128]{1,0:T(8,128)S(1)}, u32[]{:S(2)}, u32[]{:S(2)}) collective-permute-start(f32[40,128]{1,0:T(8,128)S(1)} %add_add_fusion.refs_0_), channel_id=1, source_target_pairs={{64,0},{96,32},{0,64},{32,96},{65,1},{97,33},{1,65},{33,97},{66,2}... | collective-permute-start | bytes 61448 | tf_op jit(solution)/shard_map/ppermute | solution.py:502
  67.0 0.9 %collective-permute-start.13 = (f32[40,128]{1,0:T(8,128)S(1)}, f32[40,128]{1,0:T(8,128)S(1)}, u32[]{:S(2)}, u32[]{:S(2)}) collective-permute-start(f32[40,128]{1,0:T(8,128)S(1)} %add_add_fusion.refs_0_), channel_id=1, source_target_pairs={{96,0},{0,32},{32,64},{64,96},{97,1},{1,33},{33,65},{65,97},{98,2}... | collective-permute-start | bytes 61448 | tf_op jit(solution)/shard_map/ppermute | solution.py:502
  67.9 3.6 %collective-permute-done.12.refs_2_ = f32[40,128]{1,0:T(8,128)S(1)} collective-permute-done((f32[40,128]{1,0:T(8,128)S(1)}, f32[40,128]{1,0:T(8,128)S(1)}, u32[]{:S(2)}, u32[]{:S(2)}) %collective-permute-start.12) | collective-permute-done | bytes 20512 | tf_op jit(solution)/shard_map/ppermute | solution.py:502
  71.5 0.5 collective-permute-done.13.refs_3_
  72.0 4.7 %combine.1 = (f32[1,3,8,1024]{3,2,1,0:T(8,128)}, f32[1,64]{1,0:T(1,128)}, f32[1,128]{1,0:T(1,128)}) custom-call(s32[1]{0:T(128)} %bitcast.group_ref, s32[1]{0:T(128)} %bitcast.1.band_ref, s32[1]{0:T(128)} %bitcast.2.core_ref, f32[40,128]{1,0:T(8,128)S(1)} %add_add_fusion.refs_0_, f32[40,128]{1,0:T(8,128)S(1)} %collective-permute-done.11.refs_1_, ...), custom_call_target="tpu_custom_call" | custom-call | tf_op jit(solution)/shard_map/combine/pallas_call | solution.py:477
  (19 shorter events, 0.3 us)
Async XLA Ops:
  2.1 6.5 %collective-permute-start = (bf16[16,1024]{1,0:T(8,128)(2,1)S(1)}, bf16[16,1024]{1,0:T(8,128)(2,1)S(1)}, u32[]{:S(2)}, u32[]{:S(2)}) collective-permute-start(bf16[16,1024]{1,0:T(8,128)(2,1)S(1)} %get-tuple-element.23), channel_id=1, source_target_pairs={{1,2},{2,1},{3,4},{4,3},{5,6},{6,5},{7,8},{8,7},{9,10},{10,9},{11,... | collective-permute-start | bytes 98312 | tf_op jit(solution)/shard_map/ppermute | solution.py:525
  2.8 9.7 %copy-start = (s32[1,128]{1,0:T(1,128)S(1)}, s32[1,128]{1,0:T(1,128)}, u32[]{:S(2)}) copy-start(s32[1,128]{1,0:T(1,128)} %row_ref.1) | copy-start | bytes 1540
  2.8 9.7 %copy-start.1 = (s32[1,128]{1,0:T(1,128)S(1)}, s32[1,128]{1,0:T(1,128)}, u32[]{:S(2)}) copy-start(s32[1,128]{1,0:T(1,128)} %column_ref.1) | copy-start | bytes 1540
  2.8 9.7 %copy-start.2 = (f32[1,128]{1,0:T(1,128)S(1)}, f32[1,128]{1,0:T(1,128)}, u32[]{:S(2)}) copy-start(f32[1,128]{1,0:T(1,128)} %value_ref.1) | copy-start | bytes 1540
  2.8 5.8 %collective-permute-start.1 = (bf16[16,1024]{1,0:T(8,128)(2,1)S(1)}, bf16[16,1024]{1,0:T(8,128)(2,1)S(1)}, u32[]{:S(2)}, u32[]{:S(2)}) collective-permute-start(bf16[16,1024]{1,0:T(8,128)(2,1)S(1)} %get-tuple-element.24), channel_id=1, source_target_pairs={{0,1},{1,0},{2,3},{3,2},{4,5},{5,4},{6,7},{7,6},{8,9},{9,8},{10,11... | collective-permute-start | bytes 98312 | tf_op jit(solution)/shard_map/ppermute | solution.py:526
  8.6 27.8 %collective-permute-start.2 = (bf16[12,64,1024]{2,1,0:T(8,128)(2,1)S(1)}, bf16[12,64,1024]{2,1,0:T(8,128)(2,1)}, u32[]{:S(2)}, u32[]{:S(2)}) collective-permute-start(bf16[12,64,1024]{2,1,0:T(8,128)(2,1)S(1)} %get-tuple-element.27.outer_ref.refs_4_), channel_id=1, source_target_pairs={{1,2},{2,1},{3,4},{4,3},{5,6},{6,5},{7,8},{8,7},{9,10},{10,9},{11,... | collective-permute-start | bytes 4718600 | tf_op jit(solution)/shard_map/ppermute | solution.py:531
  10.4 26.0 %collective-permute-start.3 = (bf16[12,64,1024]{2,1,0:T(8,128)(2,1)S(1)}, bf16[12,64,1024]{2,1,0:T(8,128)(2,1)}, u32[]{:S(2)}, u32[]{:S(2)}) collective-permute-start(bf16[12,64,1024]{2,1,0:T(8,128)(2,1)S(1)} %get-tuple-element.28.inner_ref.refs_5_), channel_id=1, source_target_pairs={{0,1},{1,0},{2,3},{3,2},{4,5},{5,4},{6,7},{7,6},{8,9},{9,8},{10,11... | collective-permute-start | bytes 4718600 | tf_op jit(solution)/shard_map/ppermute | solution.py:532
  44.2 1.3 %collective-permute-start.4 = (f32[40,128]{1,0:T(8,128)S(1)}, f32[40,128]{1,0:T(8,128)S(1)}, u32[]{:S(2)}, u32[]{:S(2)}) collective-permute-start(f32[40,128]{1,0:T(8,128)S(1)} %join.1), channel_id=1, source_target_pairs={{1,0},{0,1},{3,2},{2,3},{5,4},{4,5},{7,6},{6,7},{9,8},{8,9},{11,10... | collective-permute-start | bytes 61448 | tf_op jit(solution)/shard_map/ppermute | solution.py:502
  45.5 5.4 %collective-permute-start.5 = (f32[40,128]{1,0:T(8,128)S(1)}, f32[40,128]{1,0:T(8,128)S(1)}, u32[]{:S(2)}, u32[]{:S(2)}) collective-permute-start(f32[40,128]{1,0:T(8,128)S(1)} %add.29), channel_id=1, source_target_pairs={{2,0},{4,2},{6,4},{0,6},{3,1},{5,3},{7,5},{1,7},{10,8},{12,10},{14... | collective-permute-start | bytes 61448 | tf_op jit(solution)/shard_map/ppermute | solution.py:502
  49.4 5.3 %collective-permute-start.6 = (f32[40,128]{1,0:T(8,128)S(1)}, f32[40,128]{1,0:T(8,128)S(1)}, u32[]{:S(2)}, u32[]{:S(2)}) collective-permute-start(f32[40,128]{1,0:T(8,128)S(1)} %add.29), channel_id=1, source_target_pairs={{4,0},{6,2},{0,4},{2,6},{5,1},{7,3},{1,5},{3,7},{12,8},{14,10},{8,... | collective-permute-start | bytes 61448 | tf_op jit(solution)/shard_map/ppermute | solution.py:502
  49.4 5.3 %collective-permute-start.7 = (f32[40,128]{1,0:T(8,128)S(1)}, f32[40,128]{1,0:T(8,128)S(1)}, u32[]{:S(2)}, u32[]{:S(2)}) collective-permute-start(f32[40,128]{1,0:T(8,128)S(1)} %add.29), channel_id=1, source_target_pairs={{6,0},{0,2},{2,4},{4,6},{7,1},{1,3},{3,5},{5,7},{14,8},{8,10},{10,... | collective-permute-start | bytes 61448 | tf_op jit(solution)/shard_map/ppermute | solution.py:502
  54.7 5.7 %collective-permute-start.10 = (f32[40,128]{1,0:T(8,128)S(1)}, f32[40,128]{1,0:T(8,128)S(1)}, u32[]{:S(2)}, u32[]{:S(2)}) collective-permute-start(f32[40,128]{1,0:T(8,128)S(1)} %add_add_fusion.1), channel_id=1, source_target_pairs={{24,0},{0,8},{8,16},{16,24},{25,1},{1,9},{9,17},{17,25},{26,2},{2,... | collective-permute-start | bytes 61448 | tf_op jit(solution)/shard_map/ppermute | solution.py:502
  56.7 3.8 %collective-permute-start.8 = (f32[40,128]{1,0:T(8,128)S(1)}, f32[40,128]{1,0:T(8,128)S(1)}, u32[]{:S(2)}, u32[]{:S(2)}) collective-permute-start(f32[40,128]{1,0:T(8,128)S(1)} %add_add_fusion.1), channel_id=1, source_target_pairs={{8,0},{16,8},{24,16},{0,24},{9,1},{17,9},{25,17},{1,25},{10,2},{18... | collective-permute-start | bytes 61448 | tf_op jit(solution)/shard_map/ppermute | solution.py:502
  58.1 5.3 %collective-permute-start.9 = (f32[40,128]{1,0:T(8,128)S(1)}, f32[40,128]{1,0:T(8,128)S(1)}, u32[]{:S(2)}, u32[]{:S(2)}) collective-permute-start(f32[40,128]{1,0:T(8,128)S(1)} %add_add_fusion.1), channel_id=1, source_target_pairs={{16,0},{24,8},{0,16},{8,24},{17,1},{25,9},{1,17},{9,25},{18,2},{26... | collective-permute-start | bytes 61448 | tf_op jit(solution)/shard_map/ppermute | solution.py:502
  63.3 4.5 %collective-permute-start.11 = (f32[40,128]{1,0:T(8,128)S(1)}, f32[40,128]{1,0:T(8,128)S(1)}, u32[]{:S(2)}, u32[]{:S(2)}) collective-permute-start(f32[40,128]{1,0:T(8,128)S(1)} %add_add_fusion.refs_0_), channel_id=1, source_target_pairs={{32,0},{64,32},{96,64},{0,96},{33,1},{65,33},{97,65},{1,97},{34,2}... | collective-permute-start | bytes 61448 | tf_op jit(solution)/shard_map/ppermute | solution.py:502
  66.2 5.3 %collective-permute-start.12 = (f32[40,128]{1,0:T(8,128)S(1)}, f32[40,128]{1,0:T(8,128)S(1)}, u32[]{:S(2)}, u32[]{:S(2)}) collective-permute-start(f32[40,128]{1,0:T(8,128)S(1)} %add_add_fusion.refs_0_), channel_id=1, source_target_pairs={{64,0},{96,32},{0,64},{32,96},{65,1},{97,33},{1,65},{33,97},{66,2}... | collective-permute-start | bytes 61448 | tf_op jit(solution)/shard_map/ppermute | solution.py:502
  67.0 5.0 %collective-permute-start.13 = (f32[40,128]{1,0:T(8,128)S(1)}, f32[40,128]{1,0:T(8,128)S(1)}, u32[]{:S(2)}, u32[]{:S(2)}) collective-permute-start(f32[40,128]{1,0:T(8,128)S(1)} %add_add_fusion.refs_0_), channel_id=1, source_target_pairs={{96,0},{0,32},{32,64},{64,96},{97,1},{1,33},{33,65},{65,97},{98,2}... | collective-permute-start | bytes 61448 | tf_op jit(solution)/shard_map/ppermute | solution.py:502

commit v3 on v2

--- a/solution.py
+++ b/solution.py
@@ -87,18 +87,23 @@
 
     for c in range(chunks):
         copy(c).start()
-    for c in range(chunks):
+    def chunk_body(c, carry):
         copy(c).wait()
+        at = pl.ds(c * KC, KC)
         for core in range(2):
             low, high = (outer_ref, inner_ref) if core == 0 else (inner_ref, outer_ref)
 
             @pl.when(core_ref[0] == core)
-            def _(c=c, low=low, high=high):
+            def _(low=low, high=high):
                 for f in range(fields):
-                    part = jnp.swapaxes(sketch[c * KC : (c + 1) * KC, f].astype(jnp.float32), 0, 1)
+                    part = jnp.swapaxes(sketch[at, f].astype(jnp.float32), 0, 1)
                     part = part.astype(jnp.bfloat16)
                     for ref, rows in ((low, part[:HALO]), (high, part[HALO:])):
-                        ref[f * HALO : (f + 1) * HALO, c * KC : (c + 1) * KC] = rows
+                        ref[f * HALO : (f + 1) * HALO, at] = rows
+
+        return carry
+
+    lax.fori_loop(0, chunks, chunk_body, 0)
 
 
 def pack(sketch, core):
@@ -202,9 +207,12 @@
         coef[f, e] = jnp.broadcast_to(line, (8, lon))
         coef_ref[f, pl.ds(e, 1)] = line
 
-    for f in range(fields):
-        for r in range(rows):
-            put(f, HALO + r, base_ref[f, r : r + 1])
+    def own_row(r, carry):
+        for f in range(fields):
+            put(f, HALO + r, base_ref[f, pl.ds(r, 1)])
+        return carry
+
+    lax.fori_loop(0, rows, own_row, 0)
     for ref, first in ((outer_base, core), (inner_base, 1 - core)):
         values = ref[...].astype(jnp.float32)
         for f in range(fields):
@@ -328,16 +336,21 @@
         for n in range(pieces):
             copy(s, n).start()
     share = jnp.zeros((2 * rank, rank), jnp.float32)
-    for ref, first in ((outer_ref, core), (inner_ref, 1 - core)):
-        for i in range(outer.shape[0]):
-            f, r = i // HALO, i % HALO
-            share += across(back_ref[f * extended + HALO + first * HALO + r], ref[i])
+
+    def products(places, share):
+        def one_field(f, share):
+            for ref, first in places:
+                for r in range(HALO):
+                    share += across(back_ref[f * extended + first + r], ref[f * HALO + r])
+            return share
+
+        return lax.fori_loop(0, back_ref.shape[0] // extended, one_field, share)
+
+    share = products(((outer_ref, HALO + core * HALO), (inner_ref, 2 * HALO - core * HALO)), share)
     for s, side in enumerate(sides):
         for n in range(pieces):
             copy(s, n).wait()
-            for i in range(n * step, (n + 1) * step):
-                f, r = i // HALO, i % HALO
-                share += across(back_ref[f * extended + side[2] * (extended - HALO) + r], side[1][i])
+        share = products(((side[1], side[2] * (extended - HALO)),), share)
     share = (share[:rank] + share[rank:]) * scale
     half = rank // 2
     share_ref[:half] = jnp.concatenate([share[:half], share[half:]], axis=1)
@@ -360,6 +373,31 @@
         compiler_params=pltpu.CompilerParams(vmem_limit_bytes=8 * MIB),
         name="join",
     )(core, back, tail, outer, inner, on_hbm(far_outer), on_hbm(far_inner))
+
+
+def fetch_kernel(outer_hbm, inner_hbm, share_ref, outer_ref, inner_ref, sems):
+    copies = [
+        pltpu.make_async_copy(outer_hbm, outer_ref, sems.at[0]),
+        pltpu.make_async_copy(inner_hbm, inner_ref, sems.at[1]),
+    ]
+    for copy in copies:
+        copy.start()
+    for copy in copies:
+        copy.wait()
+
+
+def fetch(outer, inner, share):
+    received = jax.ShapeDtypeStruct(outer.shape, outer.dtype)
+    return pl.pallas_call(
+        fetch_kernel,
+        out_shape=(received, received),
+        in_specs=[HBM, HBM, VMEM],
+        out_specs=(VMEM, VMEM),
+        scratch_shapes=[pltpu.SemaphoreType.DMA((2,))],
+        compiler_params=pltpu.CompilerParams(vmem_limit_bytes=4 * MIB),
+        cost_estimate=pl.CostEstimate(flops=0, bytes_accessed=6_300_000, transcendentals=0),
+        name="fetch",
+    )(on_hbm(outer), on_hbm(inner), share)
 
 
 def combine_kernel(
@@ -375,8 +413,8 @@
     (
         outer_ref,
         inner_ref,
-        far_outer_hbm,
-        far_inner_hbm,
+        far_outer_ref,
+        far_inner_ref,
         coef_ref,
         increment_hbm,
         adjoint_hbm,
@@ -385,16 +423,8 @@
         adjoint,
         cost_out,
         combined,
-        far_outer_ref,
-        far_inner_ref,
         sems,
     ) = refs[groups:]
-    arrivals = [
-        pltpu.make_async_copy(far_outer_hbm, far_outer_ref, sems.at[3]),
-        pltpu.make_async_copy(far_inner_hbm, far_inner_ref, sems.at[4]),
-    ]
-    for copy in arrivals:
-        copy.start()
     half = shares[0].shape[0] - 8
     rank = 2 * half
     fields, extended, lon = coef_ref.shape
@@ -435,35 +465,42 @@
         (far_outer_ref, core * (extended - HALO)),
         (far_inner_ref, (1 - core) * (extended - HALO)),
     )
-    for n, (ref, first) in enumerate(places):
-        if n >= 2:
-            arrivals[n - 2].wait()
-        for f in range(fields):
+
+    def one_field(f, carry):
+        for ref, first in places:
             for r in range(HALO):
                 part = lax.dot_general(
                     factor, ref[f * HALO + r], (((1,), (0,)), ((), ())), preferred_element_type=jnp.float32
                 )
                 combined[f, pl.ds(first + r, 1)] = jnp.sum(part, axis=0, keepdims=True)
+        return carry
+
+    lax.fori_loop(0, fields, one_field, 0)
 
     latitude = band_ref[0] * rows - HALO + lax.broadcasted_iota(jnp.int32, (extended, lon), 0)
     present = (latitude >= 0) & (latitude < rows * bands)
     turn = 0.5 * coriolis_coef * (2.0 * (latitude.astype(jnp.float32) + 0.5) / (rows * bands) - 1.0)
-    depth, east, north = (coef_ref[f] for f in range(3))
-    h, u, v = 0.25 * combined[0], combined[1], combined[2]
+    combined[0] = 0.25 * combined[0]
 
     def lat_difference(x):
         return pltpu.roll(x, extended - 1, 0) - pltpu.roll(x, 1, 0)
 
-    for _ in range(STEPS):
+    def step(_, carry):
+        depth, east, north = (coef_ref[f] for f in range(3))
+        h, u, v = (combined[f] for f in range(3))
         dxh, dxu, dxv = (lon_difference(x) for x in (h, u, v))
         dyh, dyu, dyv = (lat_difference(x) for x in (h, u, v))
         new_u = (u + turn * v) - dxh - east * dxu - north * dyu
         new_v = (v - turn * u) - dyh - east * dxv - north * dyv
         new_h = h - depth * (dxu + dyv) - east * dxh - north * dyh
-        h, u, v = (jnp.where(present, x, 0.0) for x in (new_h, new_u, new_v))
-    own = slice(HALO, HALO + rows)
-    for f, value in enumerate((4.0 * h, u, v)):
-        increment[0, f] = value[own]
+        for f, x in enumerate((new_h, new_u, new_v)):
+            combined[f] = jnp.where(present, x, 0.0)
+        return carry
+
+    lax.fori_loop(0, STEPS, step, 0)
+    for f in range(fields):
+        value = combined[f, HALO : HALO + rows]
+        increment[0, f] = 4.0 * value if f == 0 else value
     copies.append(pltpu.make_async_copy(increment, increment_hbm, sems.at[2]))
     copies[-1].start()
     for copy in copies:
@@ -481,20 +518,18 @@
             jax.ShapeDtypeStruct((1, rank), jnp.float32),
             jax.ShapeDtypeStruct((1, 2 * rank), jnp.float32),
         ),
-        in_specs=[SMEM] * 3 + [VMEM] * (len(shares) + 2) + [HBM] * 2 + [VMEM],
+        in_specs=[SMEM] * 3 + [VMEM] * (len(shares) + 5),
         out_specs=(HBM,) * 3,
         scratch_shapes=[
             pltpu.VMEM((1, fields, rows, lon), jnp.float32),
             pltpu.VMEM((1, rank), jnp.float32),
             pltpu.VMEM((1, 2 * rank), jnp.float32),
             pltpu.VMEM((fields, extended, lon), jnp.float32),
-            pltpu.VMEM(halves[2].shape, halves[2].dtype),
-            pltpu.VMEM(halves[3].shape, halves[3].dtype),
-            pltpu.SemaphoreType.DMA((5,)),
+            pltpu.SemaphoreType.DMA((3,)),
         ],
         compiler_params=pltpu.CompilerParams(vmem_limit_bytes=8 * MIB),
         name="combine",
-    )(group, band, core, *shares, *halves[:2], *(on_hbm(x) for x in halves[2:]), coef)
+    )(group, band, core, *shares, *halves, coef)
 
 
 def from_ahead(x, axis, by):
@@ -540,6 +575,7 @@
     share = join(core, back, tail, outer, inner, far_outer, far_inner, scale)
     for axis in ("lat_2", "lat_1", "lat_0"):
         share = added_over(share, axis)
+    far_outer, far_inner = fetch(far_outer, far_inner, share)
     shares = [share] + [from_ahead(share, "tm", by) for by in range(1, groups)]
     increment, adjoint, total_cost = combine(
         group, band, core, shares, (outer, inner, far_outer, far_inner), coef, 1.0 / math.sqrt(rank), bands

time: 77 us -> 72.3 us (0.939)
  Pallas kernels: 39.9 us -> 37.3 us
  waiting for transfers between devices: 12.5 us -> 10.6 us
    pallas_call x1, Pallas kernels: 7.77 us -> 4.74 us  [join(): pl.pallas_call(functools.partial(join_kernel, scale), out_shape=jax.Shape...]
    pallas_call x0 -> x1, Pallas kernels: none -> 1.9 us  [fetch(): pl.pallas_call(fetch_kernel, out_shape=(received, received), in_specs=[HB...]
    ppermute x10, waiting for transfers between devices: 12.5 us -> 10.6 us  [from_ahead(): return lax.ppermute(x, axis, [((i + by) % count, i) for i in range(count)])]
    pallas_call x1, Pallas kernels: 4.68 us -> 3.34 us  [combine(): pl.pallas_call(functools.partial(combine_kernel, scale, len(shares), band...]
  transfers between devices with their start and end apart: 14 -> 14, of which waited for: 7 -> 7; matrix products, arithmetic and copies ran while one was open for 0% -> 0% of each run, Pallas kernels for 35% -> 39%
where the time goes in v3:
time: 72.3 us; the launch traced here: 72.1 us
  Pallas kernels  37.3 us (52%)
  starting transfers between devices  22.6 us (31%)
  waiting for transfers between devices  10.6 us (15%)
  between operations  1.42 us (2%)
    pallas_call x1, Pallas kernels, sweep(): pl.pallas_call(functools.partial(sweep_kernel, bands), out_shape=(jax.Sha...  23.4 us
    ppermute x10, starting transfers between devices, from_ahead(): return lax.ppermute(x, axis, [((i + by) % count, i) for i in range(count)])  15.2 us
    ppermute x10, waiting for transfers between devices, from_ahead(): return lax.ppermute(x, axis, [((i + by) % count, i) for i in range(count)])  10.6 us
    pallas_call x1, Pallas kernels, join(): pl.pallas_call(functools.partial(join_kernel, scale), out_shape=jax.Shape...  4.74 us
    pallas_call x1, Pallas kernels, combine(): pl.pallas_call(functools.partial(combine_kernel, scale, len(shares), band...  3.34 us
    ppermute x1, starting transfers between devices, body(): far_inner_base = lax.ppermute(inner_base, 'lat_2', inside_chip)  3.1 us
    pallas_call x1, Pallas kernels, pack(): pl.pallas_call(pack_kernel, out_shape=(half, half), in_specs=[SMEM, HBM],...  2.68 us
    pallas_call x1, Pallas kernels, fetch(): pl.pallas_call(fetch_kernel, out_shape=(received, received), in_specs=[HB...  1.9 us
  transfers between devices with their start and end apart: 14, of which 7 were waited for; matrix products, arithmetic and copies ran while one was open for 0% of the time, Pallas kernels for 39%

profile of v3, /device:TPU:0, one launch (start us, length us, event | category | flops | bytes accessed | tf_op | source)
XLA Modules:
  0.0 72.1 jit_solution(11444797826359843409)
XLA Ops:
  1.3 0.8 %pick.1 = (bf16[16,1024]{1,0:T(8,128)(2,1)S(1)}, bf16[16,1024]{1,0:T(8,128)(2,1)S(1)}, f32[3,8,1024]{2,1,0:T(8,128)S(1)}) custom-call(s32[1]{0:T(128)S(6)} %copy.10.step_ref, s32[1]{0:T(128)} %bitcast.2.core_ref, bf16[4,3,8,1024]{3,2,1,0:T(8,128)(2,1)} %base_hbm.1), custom_call_target="tpu_custom_call" | custom-call | tf_op jit(solution)/shard_map/pick/pallas_call | solution.py:69
  2.1 0.7 collective-permute-start
  2.8 3.1 %collective-permute-start.1 = (bf16[16,1024]{1,0:T(8,128)(2,1)S(1)}, bf16[16,1024]{1,0:T(8,128)(2,1)S(1)}, u32[]{:S(2)}, u32[]{:S(2)}) collective-permute-start(bf16[16,1024]{1,0:T(8,128)(2,1)S(1)} %get-tuple-element.26), channel_id=1, source_target_pairs={{0,1},{1,0},{2,3},{3,2},{4,5},{5,4},{6,7},{7,6},{8,9},{9,8},{10,11... | collective-permute-start | bytes 98312 | tf_op jit(solution)/shard_map/ppermute | solution.py:561
  5.9 2.7 %pack.1 = (bf16[12,64,1024]{2,1,0:T(8,128)(2,1)S(1)}, bf16[12,64,1024]{2,1,0:T(8,128)(2,1)S(1)}) custom-call(s32[1]{0:T(128)} %bitcast.2.core_ref, bf16[64,3,8,1024]{3,2,1,0:T(8,128)(2,1)} %sketch_hbm.1), custom_call_target="tpu_custom_call" | custom-call | tf_op jit(solution)/shard_map/pack/pallas_call | solution.py:112
  8.6 1.8 %collective-permute-start.2 = (bf16[12,64,1024]{2,1,0:T(8,128)(2,1)S(1)}, bf16[12,64,1024]{2,1,0:T(8,128)(2,1)}, u32[]{:S(2)}, u32[]{:S(2)}) collective-permute-start(bf16[12,64,1024]{2,1,0:T(8,128)(2,1)S(1)} %get-tuple-element.29.outer_ref.refs_4_), channel_id=1, source_target_pairs={{1,2},{2,1},{3,4},{4,3},{5,6},{6,5},{7,8},{8,7},{9,10},{10,9},{11,... | collective-permute-start | bytes 4718600 | tf_op jit(solution)/shard_map/ppermute | solution.py:566
  10.5 1.9 %collective-permute-start.3 = (bf16[12,64,1024]{2,1,0:T(8,128)(2,1)S(1)}, bf16[12,64,1024]{2,1,0:T(8,128)(2,1)}, u32[]{:S(2)}, u32[]{:S(2)}) collective-permute-start(bf16[12,64,1024]{2,1,0:T(8,128)(2,1)S(1)} %get-tuple-element.30.inner_ref.refs_5_), channel_id=1, source_target_pairs={{0,1},{1,0},{2,3},{3,2},{4,5},{5,4},{6,7},{7,6},{8,9},{9,8},{10,11... | collective-permute-start | bytes 4718600 | tf_op jit(solution)/shard_map/ppermute | solution.py:567
  12.8 23.4 %sweep.1 = (bf16[48,128,1024]{2,1,0:T(8,128)(2,1)S(1)}, f32[3,16,1024]{2,1,0:T(8,128)S(1)}, f32[8,64]{1,0:T(8,128)S(1)}) custom-call(s32[1]{0:T(128)} %bitcast.1.band_ref, s32[1]{0:T(128)} %bitcast.2.core_ref, bf16[64,3,8,1024]{3,2,1,0:T(8,128)(2,1)} %test_hbm.1, f32[3,8,1024]{2,1,0:T(8,128)S(1)} %get-tuple-element.22.base_ref, ...), custom_call_target="tpu_custom_call" | custom-call | flops 2000000000 | bytes 30000000 | tf_op jit(solution)/shard_map/sweep/pallas_call | solution.py:299
  36.2 4.7 %join.1 = f32[40,128]{1,0:T(8,128)S(1)} custom-call(s32[1]{0:T(128)} %bitcast.2.core_ref, bf16[48,128,1024]{2,1,0:T(8,128)(2,1)S(1)} %get-tuple-element.33.back_ref, f32[8,64]{1,0:T(8,128)S(1)} %get-tuple-element.34.tail_ref, bf16[12,64,1024]{2,1,0:T(8,128)(2,1)S(1)} %get-tuple-element.29.outer_ref.refs_4_, ...), custom_call_target="tpu_custom_call" | custom-call | tf_op jit(solution)/shard_map/join/pallas_call | solution.py:363
  41.1 1.1 %collective-permute-done.4 = f32[40,128]{1,0:T(8,128)S(1)} collective-permute-done((f32[40,128]{1,0:T(8,128)S(1)}, f32[40,128]{1,0:T(8,128)S(1)}, u32[]{:S(2)}, u32[]{:S(2)}) %collective-permute-start.4) | collective-permute-done | bytes 20512 | tf_op jit(solution)/shard_map/ppermute | solution.py:537
  42.2 3.9 %collective-permute-start.5 = (f32[40,128]{1,0:T(8,128)S(1)}, f32[40,128]{1,0:T(8,128)S(1)}, u32[]{:S(2)}, u32[]{:S(2)}) collective-permute-start(f32[40,128]{1,0:T(8,128)S(1)} %add.29), channel_id=1, source_target_pairs={{2,0},{4,2},{6,4},{0,6},{3,1},{5,3},{7,5},{1,7},{10,8},{12,10},{14... | collective-permute-start | bytes 61448 | tf_op jit(solution)/shard_map/ppermute | solution.py:537
  46.2 0.9 %collective-permute-start.7 = (f32[40,128]{1,0:T(8,128)S(1)}, f32[40,128]{1,0:T(8,128)S(1)}, u32[]{:S(2)}, u32[]{:S(2)}) collective-permute-start(f32[40,128]{1,0:T(8,128)S(1)} %add.29), channel_id=1, source_target_pairs={{6,0},{0,2},{2,4},{4,6},{7,1},{1,3},{3,5},{5,7},{14,8},{8,10},{10,... | collective-permute-start | bytes 61448 | tf_op jit(solution)/shard_map/ppermute | solution.py:537
  47.1 0.5 collective-permute-done.5
  47.6 3.8 %collective-permute-done.6 = f32[40,128]{1,0:T(8,128)S(1)} collective-permute-done((f32[40,128]{1,0:T(8,128)S(1)}, f32[40,128]{1,0:T(8,128)S(1)}, u32[]{:S(2)}, u32[]{:S(2)}) %collective-permute-start.6) | collective-permute-done | bytes 20512 | tf_op jit(solution)/shard_map/ppermute | solution.py:537
  51.5 2.0 %collective-permute-start.10 = (f32[40,128]{1,0:T(8,128)S(1)}, f32[40,128]{1,0:T(8,128)S(1)}, u32[]{:S(2)}, u32[]{:S(2)}) collective-permute-start(f32[40,128]{1,0:T(8,128)S(1)} %add_add_fusion.1), channel_id=1, source_target_pairs={{24,0},{0,8},{8,16},{16,24},{25,1},{1,9},{9,17},{17,25},{26,2},{2,... | collective-permute-start | bytes 61448 | tf_op jit(solution)/shard_map/ppermute | solution.py:537
  53.5 1.3 %collective-permute-start.8 = (f32[40,128]{1,0:T(8,128)S(1)}, f32[40,128]{1,0:T(8,128)S(1)}, u32[]{:S(2)}, u32[]{:S(2)}) collective-permute-start(f32[40,128]{1,0:T(8,128)S(1)} %add_add_fusion.1), channel_id=1, source_target_pairs={{8,0},{16,8},{24,16},{0,24},{9,1},{17,9},{25,17},{1,25},{10,2},{18... | collective-permute-start | bytes 61448 | tf_op jit(solution)/shard_map/ppermute | solution.py:537
  54.8 2.4 %collective-permute-start.9 = (f32[40,128]{1,0:T(8,128)S(1)}, f32[40,128]{1,0:T(8,128)S(1)}, u32[]{:S(2)}, u32[]{:S(2)}) collective-permute-start(f32[40,128]{1,0:T(8,128)S(1)} %add_add_fusion.1), channel_id=1, source_target_pairs={{16,0},{24,8},{0,16},{8,24},{17,1},{25,9},{1,17},{9,25},{18,2},{26... | collective-permute-start | bytes 61448 | tf_op jit(solution)/shard_map/ppermute | solution.py:537
  57.2 2.8 %collective-permute-done.9 = f32[40,128]{1,0:T(8,128)S(1)} collective-permute-done((f32[40,128]{1,0:T(8,128)S(1)}, f32[40,128]{1,0:T(8,128)S(1)}, u32[]{:S(2)}, u32[]{:S(2)}) %collective-permute-start.9) | collective-permute-done | bytes 20512 | tf_op jit(solution)/shard_map/ppermute | solution.py:537
  60.1 2.8 %collective-permute-start.11 = (f32[40,128]{1,0:T(8,128)S(1)}, f32[40,128]{1,0:T(8,128)S(1)}, u32[]{:S(2)}, u32[]{:S(2)}) collective-permute-start(f32[40,128]{1,0:T(8,128)S(1)} %add_add_fusion.share_ref.refs_0_), channel_id=1, source_target_pairs={{32,0},{64,32},{96,64},{0,96},{33,1},{65,33},{97,65},{1,97},{34,2}... | collective-permute-start | bytes 61448 | tf_op jit(solution)/shard_map/ppermute | solution.py:537
  62.9 0.8 %collective-permute-start.12 = (f32[40,128]{1,0:T(8,128)S(1)}, f32[40,128]{1,0:T(8,128)S(1)}, u32[]{:S(2)}, u32[]{:S(2)}) collective-permute-start(f32[40,128]{1,0:T(8,128)S(1)} %add_add_fusion.share_ref.refs_0_), channel_id=1, source_target_pairs={{64,0},{96,32},{0,64},{32,96},{65,1},{97,33},{1,65},{33,97},{66,2}... | collective-permute-start | bytes 61448 | tf_op jit(solution)/shard_map/ppermute | solution.py:537
  63.7 0.9 %collective-permute-start.13 = (f32[40,128]{1,0:T(8,128)S(1)}, f32[40,128]{1,0:T(8,128)S(1)}, u32[]{:S(2)}, u32[]{:S(2)}) collective-permute-start(f32[40,128]{1,0:T(8,128)S(1)} %add_add_fusion.share_ref.refs_0_), channel_id=1, source_target_pairs={{96,0},{0,32},{32,64},{64,96},{97,1},{1,33},{33,65},{65,97},{98,2}... | collective-permute-start | bytes 61448 | tf_op jit(solution)/shard_map/ppermute | solution.py:537
  64.6 1.9 %fetch.1 = (bf16[12,64,1024]{2,1,0:T(8,128)(2,1)S(1)}, bf16[12,64,1024]{2,1,0:T(8,128)(2,1)S(1)}) custom-call(bf16[12,64,1024]{2,1,0:T(8,128)(2,1)} %collective-permute-done.2.outer_hbm, bf16[12,64,1024]{2,1,0:T(8,128)(2,1)} %collective-permute-done.3.inner_hbm, f32[40,128]{1,0:T(8,128)S(1)} %add_add_fusion.share_ref.refs_0_), custom_call_target="tpu_custom_call" | custom-call | bytes 6300000 | tf_op jit(solution)/shard_map/fetch/pallas_call | solution.py:391
  66.5 1.7 %collective-permute-done.12.refs_2_ = f32[40,128]{1,0:T(8,128)S(1)} collective-permute-done((f32[40,128]{1,0:T(8,128)S(1)}, f32[40,128]{1,0:T(8,128)S(1)}, u32[]{:S(2)}, u32[]{:S(2)}) %collective-permute-start.12) | collective-permute-done | bytes 20512 | tf_op jit(solution)/shard_map/ppermute | solution.py:537
  68.2 0.5 collective-permute-done.13.refs_3_
  68.7 3.3 %combine.1 = (f32[1,3,8,1024]{3,2,1,0:T(8,128)}, f32[1,64]{1,0:T(1,128)}, f32[1,128]{1,0:T(1,128)}) custom-call(s32[1]{0:T(128)} %bitcast.group_ref, s32[1]{0:T(128)} %bitcast.1.band_ref, s32[1]{0:T(128)} %bitcast.2.core_ref, f32[40,128]{1,0:T(8,128)S(1)} %add_add_fusion.share_ref.refs_0_, f32[40,128]{1,0:T(8,128)S(1)} %collective-permute-done.11.refs_1_, ...), custom_call_target="tpu_custom_call" | custom-call | tf_op jit(solution)/shard_map/combine/pallas_call | solution.py:514
  (20 shorter events, 0.7 us)
Async XLA Ops:
  2.1 6.5 %collective-permute-start = (bf16[16,1024]{1,0:T(8,128)(2,1)S(1)}, bf16[16,1024]{1,0:T(8,128)(2,1)S(1)}, u32[]{:S(2)}, u32[]{:S(2)}) collective-permute-start(bf16[16,1024]{1,0:T(8,128)(2,1)S(1)} %get-tuple-element.25), channel_id=1, source_target_pairs={{1,2},{2,1},{3,4},{4,3},{5,6},{6,5},{7,8},{8,7},{9,10},{10,9},{11,... | collective-permute-start | bytes 98312 | tf_op jit(solution)/shard_map/ppermute | solution.py:560
  2.8 9.5 %copy-start = (s32[1,128]{1,0:T(1,128)S(1)}, s32[1,128]{1,0:T(1,128)}, u32[]{:S(2)}) copy-start(s32[1,128]{1,0:T(1,128)} %row_ref.1) | copy-start | bytes 1540
  2.8 9.5 %copy-start.1 = (s32[1,128]{1,0:T(1,128)S(1)}, s32[1,128]{1,0:T(1,128)}, u32[]{:S(2)}) copy-start(s32[1,128]{1,0:T(1,128)} %column_ref.1) | copy-start | bytes 1540
  2.8 9.5 %copy-start.2 = (f32[1,128]{1,0:T(1,128)S(1)}, f32[1,128]{1,0:T(1,128)}, u32[]{:S(2)}) copy-start(f32[1,128]{1,0:T(1,128)} %value_ref.1) | copy-start | bytes 1540
  2.8 5.8 %collective-permute-start.1 = (bf16[16,1024]{1,0:T(8,128)(2,1)S(1)}, bf16[16,1024]{1,0:T(8,128)(2,1)S(1)}, u32[]{:S(2)}, u32[]{:S(2)}) collective-permute-start(bf16[16,1024]{1,0:T(8,128)(2,1)S(1)} %get-tuple-element.26), channel_id=1, source_target_pairs={{0,1},{1,0},{2,3},{3,2},{4,5},{5,4},{6,7},{7,6},{8,9},{9,8},{10,11... | collective-permute-start | bytes 98312 | tf_op jit(solution)/shard_map/ppermute | solution.py:561
  8.6 27.6 %collective-permute-start.2 = (bf16[12,64,1024]{2,1,0:T(8,128)(2,1)S(1)}, bf16[12,64,1024]{2,1,0:T(8,128)(2,1)}, u32[]{:S(2)}, u32[]{:S(2)}) collective-permute-start(bf16[12,64,1024]{2,1,0:T(8,128)(2,1)S(1)} %get-tuple-element.29.outer_ref.refs_4_), channel_id=1, source_target_pairs={{1,2},{2,1},{3,4},{4,3},{5,6},{6,5},{7,8},{8,7},{9,10},{10,9},{11,... | collective-permute-start | bytes 4718600 | tf_op jit(solution)/shard_map/ppermute | solution.py:566
  10.5 25.7 %collective-permute-start.3 = (bf16[12,64,1024]{2,1,0:T(8,128)(2,1)S(1)}, bf16[12,64,1024]{2,1,0:T(8,128)(2,1)}, u32[]{:S(2)}, u32[]{:S(2)}) collective-permute-start(bf16[12,64,1024]{2,1,0:T(8,128)(2,1)S(1)} %get-tuple-element.30.inner_ref.refs_5_), channel_id=1, source_target_pairs={{0,1},{1,0},{2,3},{3,2},{4,5},{5,4},{6,7},{7,6},{8,9},{9,8},{10,11... | collective-permute-start | bytes 4718600 | tf_op jit(solution)/shard_map/ppermute | solution.py:567
  41.0 1.3 %collective-permute-start.4 = (f32[40,128]{1,0:T(8,128)S(1)}, f32[40,128]{1,0:T(8,128)S(1)}, u32[]{:S(2)}, u32[]{:S(2)}) collective-permute-start(f32[40,128]{1,0:T(8,128)S(1)} %join.1), channel_id=1, source_target_pairs={{1,0},{0,1},{3,2},{2,3},{5,4},{4,5},{7,6},{6,7},{9,8},{8,9},{11,10... | collective-permute-start | bytes 61448 | tf_op jit(solution)/shard_map/ppermute | solution.py:537
  42.2 5.4 %collective-permute-start.5 = (f32[40,128]{1,0:T(8,128)S(1)}, f32[40,128]{1,0:T(8,128)S(1)}, u32[]{:S(2)}, u32[]{:S(2)}) collective-permute-start(f32[40,128]{1,0:T(8,128)S(1)} %add.29), channel_id=1, source_target_pairs={{2,0},{4,2},{6,4},{0,6},{3,1},{5,3},{7,5},{1,7},{10,8},{12,10},{14... | collective-permute-start | bytes 61448 | tf_op jit(solution)/shard_map/ppermute | solution.py:537
  46.2 5.3 %collective-permute-start.6 = (f32[40,128]{1,0:T(8,128)S(1)}, f32[40,128]{1,0:T(8,128)S(1)}, u32[]{:S(2)}, u32[]{:S(2)}) collective-permute-start(f32[40,128]{1,0:T(8,128)S(1)} %add.29), channel_id=1, source_target_pairs={{4,0},{6,2},{0,4},{2,6},{5,1},{7,3},{1,5},{3,7},{12,8},{14,10},{8,... | collective-permute-start | bytes 61448 | tf_op jit(solution)/shard_map/ppermute | solution.py:537
  46.2 5.3 %collective-permute-start.7 = (f32[40,128]{1,0:T(8,128)S(1)}, f32[40,128]{1,0:T(8,128)S(1)}, u32[]{:S(2)}, u32[]{:S(2)}) collective-permute-start(f32[40,128]{1,0:T(8,128)S(1)} %add.29), channel_id=1, source_target_pairs={{6,0},{0,2},{2,4},{4,6},{7,1},{1,3},{3,5},{5,7},{14,8},{8,10},{10,... | collective-permute-start | bytes 61448 | tf_op jit(solution)/shard_map/ppermute | solution.py:537
  51.5 5.7 %collective-permute-start.10 = (f32[40,128]{1,0:T(8,128)S(1)}, f32[40,128]{1,0:T(8,128)S(1)}, u32[]{:S(2)}, u32[]{:S(2)}) collective-permute-start(f32[40,128]{1,0:T(8,128)S(1)} %add_add_fusion.1), channel_id=1, source_target_pairs={{24,0},{0,8},{8,16},{16,24},{25,1},{1,9},{9,17},{17,25},{26,2},{2,... | collective-permute-start | bytes 61448 | tf_op jit(solution)/shard_map/ppermute | solution.py:537
  53.5 3.8 %collective-permute-start.8 = (f32[40,128]{1,0:T(8,128)S(1)}, f32[40,128]{1,0:T(8,128)S(1)}, u32[]{:S(2)}, u32[]{:S(2)}) collective-permute-start(f32[40,128]{1,0:T(8,128)S(1)} %add_add_fusion.1), channel_id=1, source_target_pairs={{8,0},{16,8},{24,16},{0,24},{9,1},{17,9},{25,17},{1,25},{10,2},{18... | collective-permute-start | bytes 61448 | tf_op jit(solution)/shard_map/ppermute | solution.py:537
  54.8 5.3 %collective-permute-start.9 = (f32[40,128]{1,0:T(8,128)S(1)}, f32[40,128]{1,0:T(8,128)S(1)}, u32[]{:S(2)}, u32[]{:S(2)}) collective-permute-start(f32[40,128]{1,0:T(8,128)S(1)} %add_add_fusion.1), channel_id=1, source_target_pairs={{16,0},{24,8},{0,16},{8,24},{17,1},{25,9},{1,17},{9,25},{18,2},{26... | collective-permute-start | bytes 61448 | tf_op jit(solution)/shard_map/ppermute | solution.py:537
  60.1 6.4 %collective-permute-start.11 = (f32[40,128]{1,0:T(8,128)S(1)}, f32[40,128]{1,0:T(8,128)S(1)}, u32[]{:S(2)}, u32[]{:S(2)}) collective-permute-start(f32[40,128]{1,0:T(8,128)S(1)} %add_add_fusion.share_ref.refs_0_), channel_id=1, source_target_pairs={{32,0},{64,32},{96,64},{0,96},{33,1},{65,33},{97,65},{1,97},{34,2}... | collective-permute-start | bytes 61448 | tf_op jit(solution)/shard_map/ppermute | solution.py:537
  62.9 5.3 %collective-permute-start.12 = (f32[40,128]{1,0:T(8,128)S(1)}, f32[40,128]{1,0:T(8,128)S(1)}, u32[]{:S(2)}, u32[]{:S(2)}) collective-permute-start(f32[40,128]{1,0:T(8,128)S(1)} %add_add_fusion.share_ref.refs_0_), channel_id=1, source_target_pairs={{64,0},{96,32},{0,64},{32,96},{65,1},{97,33},{1,65},{33,97},{66,2}... | collective-permute-start | bytes 61448 | tf_op jit(solution)/shard_map/ppermute | solution.py:537
  63.7 5.0 %collective-permute-start.13 = (f32[40,128]{1,0:T(8,128)S(1)}, f32[40,128]{1,0:T(8,128)S(1)}, u32[]{:S(2)}, u32[]{:S(2)}) collective-permute-start(f32[40,128]{1,0:T(8,128)S(1)} %add_add_fusion.share_ref.refs_0_), channel_id=1, source_target_pairs={{96,0},{0,32},{32,64},{64,96},{97,1},{1,33},{33,65},{65,97},{98,2}... | collective-permute-start | bytes 61448 | tf_op jit(solution)/shard_map/ppermute | solution.py:537

commit v4 on v3

--- a/solution.py
+++ b/solution.py
@@ -120,49 +120,32 @@
     )(core, on_hbm(sketch))
 
 
-def observe_kernel(scales, band_ref, base_ref, row_ref, column_ref, value_ref, field_ref, cost_ref):
-    total_rows, observed, groups = scales
-    rows, lon = base_ref.shape[-2:]
-    count = row_ref.shape[-1]
-    station_row = row_ref[...]
-    local = station_row - band_ref[0] * rows
-    at_column = lax.broadcasted_iota(jnp.int32, (lon, count), 0) == column_ref[...]
+def observed(scales, band, height, station_row, station_column, station_value):
+    total_rows, observations, groups = scales
+    rows, lon = height.shape
+    count = station_row.shape[-1]
+    local = station_row - band * rows
+    at_column = lax.broadcasted_iota(jnp.int32, (lon, count), 0) == station_column
     at_column = jnp.where(at_column, 1.0, 0.0).astype(jnp.bfloat16)
     at_row = lax.broadcasted_iota(jnp.int32, (rows, count), 0) == local
     found = lax.dot_general(
-        base_ref[0].astype(jnp.bfloat16), at_column, (((1,), (0,)), ((), ())), preferred_element_type=jnp.float32
+        height.astype(jnp.bfloat16), at_column, (((1,), (0,)), ((), ())), preferred_element_type=jnp.float32
     )
     here = jnp.sum(jnp.where(at_row, found, 0.0), axis=0, keepdims=True)
-    innovation = here - value_ref[...]
+    innovation = here - station_value
     weight = 1.0 + 2.0 * station_row.astype(jnp.float32) / total_rows
     weighted = weight * innovation
-    cost = jnp.sum(weighted * innovation, axis=1, keepdims=True) / (2.0 * groups * observed)
-    cost_ref[...] = jnp.broadcast_to(cost, cost_ref.shape)
-    spread = jnp.where(at_row, weighted / (2.0 * math.sqrt(observed)), 0.0)
+    cost = jnp.sum(weighted * innovation, axis=1, keepdims=True) / (2.0 * groups * observations)
+    spread = jnp.where(at_row, weighted / (2.0 * math.sqrt(observations)), 0.0)
     field = jnp.zeros((rows, lon), jnp.float32)
     for piece in split3(spread):
         field += across(piece, at_column)
-    for n, piece in enumerate(split3(field)):
-        field_ref[n * rows : (n + 1) * rows] = piece.astype(jnp.float32)
-
-
-def observe(band, base, station_row, station_column, station_value, scales):
-    rows, lon = base.shape[-2:]
-    return pl.pallas_call(
-        functools.partial(observe_kernel, scales),
-        out_shape=(
-            jax.ShapeDtypeStruct((3 * rows, lon), jnp.float32),
-            jax.ShapeDtypeStruct((1, 128), jnp.float32),
-        ),
-        in_specs=[SMEM] + [VMEM] * 4,
-        out_specs=(VMEM, VMEM),
-        compiler_params=pltpu.CompilerParams(vmem_limit_bytes=8 * MIB),
-        cost_estimate=pl.CostEstimate(flops=20_000_000, bytes_accessed=1_000_000, transcendentals=0),
-        name="observe",
-    )(band, base, station_row, station_column, station_value)
+    pieces = [piece.astype(jnp.float32) for piece in split3(field)]
+    return jnp.concatenate(pieces, axis=0).astype(jnp.bfloat16), cost
 
 
 def sweep_kernel(
+    scales,
     bands,
     band_ref,
     core_ref,
@@ -172,8 +155,9 @@
     inner_base,
     outer_ref,
     inner_ref,
-    field_ref,
-    cost_ref,
+    station_row_ref,
+    station_column_ref,
+    station_value_ref,
     back_ref,
     coef_ref,
     tail_ref,
@@ -218,6 +202,18 @@
         for f in range(fields):
             for r in range(HALO):
                 put(f, first * (extended - HALO) + r, values[f * HALO + r : f * HALO + r + 1])
+
+    forced = jnp.zeros((3 * rows, rank), jnp.float32)
+    line = lax.broadcasted_iota(jnp.int32, (3 * rows, rank), 0) % rows
+    field, cost = observed(
+        scales, band, base_ref[0], station_row_ref[...], station_column_ref[...], station_value_ref[...]
+    )
+    for ref, first in ((outer_ref, core), (inner_ref, 1 - core)):
+        for r in range(HALO):
+            forced += jnp.where(line == first * HALO + r, across(field, ref[r]), 0.0)
+    lane = lax.broadcasted_iota(jnp.int32, (8, rank), 0)
+    forced = jnp.sum(forced, axis=0, keepdims=True)
+    tail_ref[...] = jnp.where(lane == 0, forced, jnp.where(lane == 1, cost, 0.0))
 
     turns = [
         0.5 * coriolis_coef * (2.0 * (latitude(e).astype(jnp.float32) + 0.5) / (rows * bands) - 1.0)
@@ -282,28 +278,18 @@
 
     lax.fori_loop(0, rank // KC, chunk_body, 0)
 
-    forced = jnp.zeros((3 * rows, rank), jnp.float32)
-    line = lax.broadcasted_iota(jnp.int32, (3 * rows, rank), 0) % rows
-    field = field_ref[...].astype(jnp.bfloat16)
-    for ref, first in ((outer_ref, core), (inner_ref, 1 - core)):
-        for r in range(HALO):
-            forced += jnp.where(line == first * HALO + r, across(field, ref[r]), 0.0)
-    lane = lax.broadcasted_iota(jnp.int32, (8, rank), 0)
-    forced = jnp.sum(forced, axis=0, keepdims=True)
-    tail_ref[...] = jnp.where(lane == 0, forced, jnp.where(lane == 1, cost_ref[0:1, :rank], 0.0))
-
-
-def sweep(band, core, test_sketch, base, outer_base, inner_base, outer, inner, field, cost, bands):
+
+def sweep(band, core, test_sketch, base, outer_base, inner_base, outer, inner, stations, scales, bands):
     rank, fields, rows, lon = test_sketch.shape
     extended = rows + 2 * HALO
     return pl.pallas_call(
-        functools.partial(sweep_kernel, bands),
+        functools.partial(sweep_kernel, scales, bands),
         out_shape=(
             jax.ShapeDtypeStruct((fields * extended, 2 * rank, lon), jnp.bfloat16),
             jax.ShapeDtypeStruct((fields, extended, lon), jnp.float32),
             jax.ShapeDtypeStruct((8, rank), jnp.float32),
         ),
-        in_specs=[SMEM, SMEM, HBM] + [VMEM] * 7,
+        in_specs=[SMEM, SMEM, HBM] + [VMEM] * 8,
         out_specs=(VMEM,) * 3,
         scratch_shapes=[
             pltpu.VMEM(test_sketch.shape, jnp.bfloat16),
@@ -315,11 +301,11 @@
         compiler_params=pltpu.CompilerParams(vmem_limit_bytes=24 * MIB),
         cost_estimate=pl.CostEstimate(flops=2_000_000_000, bytes_accessed=30_000_000, transcendentals=0),
         name="sweep",
-    )(band, core, on_hbm(test_sketch), base, outer_base, inner_base, outer, inner, field, cost)
+    )(band, core, on_hbm(test_sketch), base, outer_base, inner_base, outer, inner, *stations)
 
 
 def join_kernel(
-    scale, core_ref, back_ref, tail_ref, outer_ref, inner_ref, outer_hbm, inner_hbm, share_ref, outer, inner, sems
+    scale, core_ref, back_ref, tail_ref, outer_ref, inner_ref, outer_hbm, inner_hbm, share_ref, outer, inner, sums, sems
 ):
     rank = tail_ref.shape[1]
     extended = back_ref.shape[0] // 3
@@ -335,22 +321,31 @@
     for s in range(2):
         for n in range(pieces):
             copy(s, n).start()
-    share = jnp.zeros((2 * rank, rank), jnp.float32)
-
-    def products(places, share):
-        def one_field(f, share):
-            for ref, first in places:
-                for r in range(HALO):
-                    share += across(back_ref[f * extended + first + r], ref[f * HALO + r])
-            return share
-
-        return lax.fori_loop(0, back_ref.shape[0] // extended, one_field, share)
-
-    share = products(((outer_ref, HALO + core * HALO), (inner_ref, 2 * HALO - core * HALO)), share)
-    for s, side in enumerate(sides):
+    def products(places):
+        total = jnp.zeros((2 * rank, rank), jnp.float32)
+        for ref, first in places:
+            for i in range(ref.shape[0]):
+                total += across(back_ref[i // HALO * extended + first + i % HALO], ref[i])
+        return total
+
+    for at in range(2):
+
+        @pl.when(core == at)
+        def _(at=at):
+            sums[...] = products(((outer_ref, HALO + at * HALO), (inner_ref, 2 * HALO - at * HALO)))
+
+    for s in range(2):
         for n in range(pieces):
             copy(s, n).wait()
-        share = products(((side[1], side[2] * (extended - HALO)),), share)
+    for at in range(2):
+
+        @pl.when(core == at)
+        def _(at=at):
+            sums[...] += products(
+                ((inner, (1 - at) * (extended - HALO)), (outer, at * (extended - HALO)))
+            )
+
+    share = sums[...]
     share = (share[:rank] + share[rank:]) * scale
     half = rank // 2
     share_ref[:half] = jnp.concatenate([share[:half], share[half:]], axis=1)
@@ -368,6 +363,7 @@
         scratch_shapes=[
             pltpu.VMEM(outer.shape, outer.dtype),
             pltpu.VMEM(inner.shape, inner.dtype),
+            pltpu.VMEM((2 * rank, rank), jnp.float32),
             pltpu.SemaphoreType.DMA((6,)),
         ],
         compiler_params=pltpu.CompilerParams(vmem_limit_bytes=8 * MIB),
@@ -549,7 +545,6 @@
     bands = lax.axis_size(LAT)
     groups = lax.axis_size("tm")
     total_rows = rows * bands
-    observed = station_row.shape[1] * bands
     band = lax.axis_index(LAT).astype(jnp.int32).reshape(1)
     core = lax.axis_index("lat_2").astype(jnp.int32).reshape(1)
     group = lax.axis_index("tm").astype(jnp.int32).reshape(1)
@@ -565,12 +560,11 @@
     )
     far_outer = lax.ppermute(outer, LAT, across_chips)
     far_inner = lax.ppermute(inner, "lat_2", inside_chip)
-    field, cost = observe(
-        band, base, station_row, station_column, station_value, (total_rows, observed, groups)
-    )
+    stations = (station_row, station_column, station_value)
+    scales = (total_rows, station_row.shape[1] * bands, groups)
     scale = map_scale / math.sqrt(rank * fields * total_rows * lon)
     back, coef, tail = sweep(
-        band, core, test_sketch, base, far_outer_base, far_inner_base, outer, inner, field, cost, bands
+        band, core, test_sketch, base, far_outer_base, far_inner_base, outer, inner, stations, scales, bands
     )
     share = join(core, back, tail, outer, inner, far_outer, far_inner, scale)
     for axis in ("lat_2", "lat_1", "lat_0"):

time: 72.3 us -> 70.8 us (0.979)
  Pallas kernels: 37.3 us -> 35.7 us
    pallas_call x2 -> x1, Pallas kernels: 23.9 us -> 23 us  [sweep(): pl.pallas_call(functools.partial(sweep_kernel, scales, bands), out_shape=...]
    pallas_call x1, Pallas kernels: 4.74 us -> 3.97 us  [join(): pl.pallas_call(functools.partial(join_kernel, scale), out_shape=jax.Shape...]
where the time goes in v4:
time: 70.8 us; the launch traced here: 70.5 us
  Pallas kernels  35.7 us (50%)
  starting transfers between devices  22.6 us (32%)
  waiting for transfers between devices  10.6 us (15%)
  between operations  1.57 us (2%)
    pallas_call x1, Pallas kernels, sweep(): pl.pallas_call(functools.partial(sweep_kernel, scales, bands), out_shape=...  23 us
    ppermute x10, starting transfers between devices, from_ahead(): return lax.ppermute(x, axis, [((i + by) % count, i) for i in range(count)])  15.1 us
    ppermute x10, waiting for transfers between devices, from_ahead(): return lax.ppermute(x, axis, [((i + by) % count, i) for i in range(count)])  10.6 us
    pallas_call x1, Pallas kernels, join(): pl.pallas_call(functools.partial(join_kernel, scale), out_shape=jax.Shape...  3.97 us
    pallas_call x1, Pallas kernels, combine(): pl.pallas_call(functools.partial(combine_kernel, scale, len(shares), band...  3.34 us
    ppermute x1, starting transfers between devices, body(): far_inner_base = lax.ppermute(inner_base, 'lat_2', inside_chip)  3.1 us
    pallas_call x1, Pallas kernels, pack(): pl.pallas_call(pack_kernel, out_shape=(half, half), in_specs=[SMEM, HBM],...  2.68 us
    pallas_call x1, Pallas kernels, fetch(): pl.pallas_call(fetch_kernel, out_shape=(received, received), in_specs=[HB...  1.9 us
  transfers between devices with their start and end apart: 14, of which 7 were waited for; matrix products, arithmetic and copies ran while one was open for 0% of the time, Pallas kernels for 39%

profile of v4, /device:TPU:0, one launch (start us, length us, event | category | flops | bytes accessed | tf_op | source)
XLA Modules:
  0.0 70.5 jit_solution(15331963354387603007)
XLA Ops:
  1.3 0.8 %pick.1 = (bf16[16,1024]{1,0:T(8,128)(2,1)S(1)}, bf16[16,1024]{1,0:T(8,128)(2,1)S(1)}, f32[3,8,1024]{2,1,0:T(8,128)S(1)}) custom-call(s32[1]{0:T(128)S(6)} %copy.10.step_ref, s32[1]{0:T(128)} %bitcast.2.core_ref, bf16[4,3,8,1024]{3,2,1,0:T(8,128)(2,1)} %base_hbm.1), custom_call_target="tpu_custom_call" | custom-call | tf_op jit(solution)/shard_map/pick/pallas_call | solution.py:69
  2.1 0.7 collective-permute-start
  2.8 3.1 %collective-permute-start.1 = (bf16[16,1024]{1,0:T(8,128)(2,1)S(1)}, bf16[16,1024]{1,0:T(8,128)(2,1)S(1)}, u32[]{:S(2)}, u32[]{:S(2)}) collective-permute-start(bf16[16,1024]{1,0:T(8,128)(2,1)S(1)} %get-tuple-element.24), channel_id=1, source_target_pairs={{0,1},{1,0},{2,3},{3,2},{4,5},{5,4},{6,7},{7,6},{8,9},{9,8},{10,11... | collective-permute-start | bytes 98312 | tf_op jit(solution)/shard_map/ppermute | solution.py:556
  5.9 2.7 %pack.1 = (bf16[12,64,1024]{2,1,0:T(8,128)(2,1)S(1)}, bf16[12,64,1024]{2,1,0:T(8,128)(2,1)S(1)}) custom-call(s32[1]{0:T(128)} %bitcast.2.core_ref, bf16[64,3,8,1024]{3,2,1,0:T(8,128)(2,1)} %sketch_hbm.1), custom_call_target="tpu_custom_call" | custom-call | tf_op jit(solution)/shard_map/pack/pallas_call | solution.py:112
  8.6 1.8 %collective-permute-start.2 = (bf16[12,64,1024]{2,1,0:T(8,128)(2,1)S(1)}, bf16[12,64,1024]{2,1,0:T(8,128)(2,1)}, u32[]{:S(2)}, u32[]{:S(2)}) collective-permute-start(bf16[12,64,1024]{2,1,0:T(8,128)(2,1)S(1)} %get-tuple-element.27.outer_ref.refs_4_), channel_id=1, source_target_pairs={{1,2},{2,1},{3,4},{4,3},{5,6},{6,5},{7,8},{8,7},{9,10},{10,9},{11,... | collective-permute-start | bytes 4718600 | tf_op jit(solution)/shard_map/ppermute | solution.py:561
  10.5 1.8 %collective-permute-start.3 = (bf16[12,64,1024]{2,1,0:T(8,128)(2,1)S(1)}, bf16[12,64,1024]{2,1,0:T(8,128)(2,1)}, u32[]{:S(2)}, u32[]{:S(2)}) collective-permute-start(bf16[12,64,1024]{2,1,0:T(8,128)(2,1)S(1)} %get-tuple-element.28.inner_ref.refs_5_), channel_id=1, source_target_pairs={{0,1},{1,0},{2,3},{3,2},{4,5},{5,4},{6,7},{7,6},{8,9},{9,8},{10,11... | collective-permute-start | bytes 4718600 | tf_op jit(solution)/shard_map/ppermute | solution.py:562
  12.3 23.0 %sweep.1 = (bf16[48,128,1024]{2,1,0:T(8,128)(2,1)S(1)}, f32[3,16,1024]{2,1,0:T(8,128)S(1)}, f32[8,64]{1,0:T(8,128)S(1)}) custom-call(s32[1]{0:T(128)} %bitcast.1.band_ref, s32[1]{0:T(128)} %bitcast.2.core_ref, bf16[64,3,8,1024]{3,2,1,0:T(8,128)(2,1)} %test_hbm.1, f32[3,8,1024]{2,1,0:T(8,128)S(1)} %get-tuple-element.20.base_ref, ...), custom_call_target="tpu_custom_call" | custom-call | flops 2000000000 | bytes 30000000 | tf_op jit(solution)/shard_map/sweep/pallas_call | solution.py:285
  35.3 4.0 %join.1 = f32[40,128]{1,0:T(8,128)S(1)} custom-call(s32[1]{0:T(128)} %bitcast.2.core_ref, bf16[48,128,1024]{2,1,0:T(8,128)(2,1)S(1)} %get-tuple-element.29.back_ref, f32[8,64]{1,0:T(8,128)S(1)} %get-tuple-element.30.tail_ref, bf16[12,64,1024]{2,1,0:T(8,128)(2,1)S(1)} %get-tuple-element.27.outer_ref.refs_4_, ...), custom_call_target="tpu_custom_call" | custom-call | tf_op jit(solution)/shard_map/join/pallas_call | solution.py:358
  39.4 1.2 %collective-permute-done.4 = f32[40,128]{1,0:T(8,128)S(1)} collective-permute-done((f32[40,128]{1,0:T(8,128)S(1)}, f32[40,128]{1,0:T(8,128)S(1)}, u32[]{:S(2)}, u32[]{:S(2)}) %collective-permute-start.4) | collective-permute-done | bytes 20512 | tf_op jit(solution)/shard_map/ppermute | solution.py:533
  40.6 3.9 %collective-permute-start.5 = (f32[40,128]{1,0:T(8,128)S(1)}, f32[40,128]{1,0:T(8,128)S(1)}, u32[]{:S(2)}, u32[]{:S(2)}) collective-permute-start(f32[40,128]{1,0:T(8,128)S(1)} %add.29), channel_id=1, source_target_pairs={{2,0},{4,2},{6,4},{0,6},{3,1},{5,3},{7,5},{1,7},{10,8},{12,10},{14... | collective-permute-start | bytes 61448 | tf_op jit(solution)/shard_map/ppermute | solution.py:533
  44.5 0.9 %collective-permute-start.7 = (f32[40,128]{1,0:T(8,128)S(1)}, f32[40,128]{1,0:T(8,128)S(1)}, u32[]{:S(2)}, u32[]{:S(2)}) collective-permute-start(f32[40,128]{1,0:T(8,128)S(1)} %add.29), channel_id=1, source_target_pairs={{6,0},{0,2},{2,4},{4,6},{7,1},{1,3},{3,5},{5,7},{14,8},{8,10},{10,... | collective-permute-start | bytes 61448 | tf_op jit(solution)/shard_map/ppermute | solution.py:533
  45.4 0.5 collective-permute-done.5
  46.0 3.8 %collective-permute-done.6 = f32[40,128]{1,0:T(8,128)S(1)} collective-permute-done((f32[40,128]{1,0:T(8,128)S(1)}, f32[40,128]{1,0:T(8,128)S(1)}, u32[]{:S(2)}, u32[]{:S(2)}) %collective-permute-start.6) | collective-permute-done | bytes 20512 | tf_op jit(solution)/shard_map/ppermute | solution.py:533
  49.8 2.0 %collective-permute-start.10 = (f32[40,128]{1,0:T(8,128)S(1)}, f32[40,128]{1,0:T(8,128)S(1)}, u32[]{:S(2)}, u32[]{:S(2)}) collective-permute-start(f32[40,128]{1,0:T(8,128)S(1)} %add_add_fusion.1), channel_id=1, source_target_pairs={{24,0},{0,8},{8,16},{16,24},{25,1},{1,9},{9,17},{17,25},{26,2},{2,... | collective-permute-start | bytes 61448 | tf_op jit(solution)/shard_map/ppermute | solution.py:533
  51.8 1.3 %collective-permute-start.8 = (f32[40,128]{1,0:T(8,128)S(1)}, f32[40,128]{1,0:T(8,128)S(1)}, u32[]{:S(2)}, u32[]{:S(2)}) collective-permute-start(f32[40,128]{1,0:T(8,128)S(1)} %add_add_fusion.1), channel_id=1, source_target_pairs={{8,0},{16,8},{24,16},{0,24},{9,1},{17,9},{25,17},{1,25},{10,2},{18... | collective-permute-start | bytes 61448 | tf_op jit(solution)/shard_map/ppermute | solution.py:533
  53.1 2.4 %collective-permute-start.9 = (f32[40,128]{1,0:T(8,128)S(1)}, f32[40,128]{1,0:T(8,128)S(1)}, u32[]{:S(2)}, u32[]{:S(2)}) collective-permute-start(f32[40,128]{1,0:T(8,128)S(1)} %add_add_fusion.1), channel_id=1, source_target_pairs={{16,0},{24,8},{0,16},{8,24},{17,1},{25,9},{1,17},{9,25},{18,2},{26... | collective-permute-start | bytes 61448 | tf_op jit(solution)/shard_map/ppermute | solution.py:533
  55.6 2.8 %collective-permute-done.9 = f32[40,128]{1,0:T(8,128)S(1)} collective-permute-done((f32[40,128]{1,0:T(8,128)S(1)}, f32[40,128]{1,0:T(8,128)S(1)}, u32[]{:S(2)}, u32[]{:S(2)}) %collective-permute-start.9) | collective-permute-done | bytes 20512 | tf_op jit(solution)/shard_map/ppermute | solution.py:533
  58.4 2.8 %collective-permute-start.11 = (f32[40,128]{1,0:T(8,128)S(1)}, f32[40,128]{1,0:T(8,128)S(1)}, u32[]{:S(2)}, u32[]{:S(2)}) collective-permute-start(f32[40,128]{1,0:T(8,128)S(1)} %add_add_fusion.share_ref.refs_0_), channel_id=1, source_target_pairs={{32,0},{64,32},{96,64},{0,96},{33,1},{65,33},{97,65},{1,97},{34,2}... | collective-permute-start | bytes 61448 | tf_op jit(solution)/shard_map/ppermute | solution.py:533
  61.3 0.8 %collective-permute-start.12 = (f32[40,128]{1,0:T(8,128)S(1)}, f32[40,128]{1,0:T(8,128)S(1)}, u32[]{:S(2)}, u32[]{:S(2)}) collective-permute-start(f32[40,128]{1,0:T(8,128)S(1)} %add_add_fusion.share_ref.refs_0_), channel_id=1, source_target_pairs={{64,0},{96,32},{0,64},{32,96},{65,1},{97,33},{1,65},{33,97},{66,2}... | collective-permute-start | bytes 61448 | tf_op jit(solution)/shard_map/ppermute | solution.py:533
  62.0 0.9 %collective-permute-start.13 = (f32[40,128]{1,0:T(8,128)S(1)}, f32[40,128]{1,0:T(8,128)S(1)}, u32[]{:S(2)}, u32[]{:S(2)}) collective-permute-start(f32[40,128]{1,0:T(8,128)S(1)} %add_add_fusion.share_ref.refs_0_), channel_id=1, source_target_pairs={{96,0},{0,32},{32,64},{64,96},{97,1},{1,33},{33,65},{65,97},{98,2}... | collective-permute-start | bytes 61448 | tf_op jit(solution)/shard_map/ppermute | solution.py:533
  62.9 1.9 %fetch.1 = (bf16[12,64,1024]{2,1,0:T(8,128)(2,1)S(1)}, bf16[12,64,1024]{2,1,0:T(8,128)(2,1)S(1)}) custom-call(bf16[12,64,1024]{2,1,0:T(8,128)(2,1)} %collective-permute-done.2.outer_hbm, bf16[12,64,1024]{2,1,0:T(8,128)(2,1)} %collective-permute-done.3.inner_hbm, f32[40,128]{1,0:T(8,128)S(1)} %add_add_fusion.share_ref.refs_0_), custom_call_target="tpu_custom_call" | custom-call | bytes 6300000 | tf_op jit(solution)/shard_map/fetch/pallas_call | solution.py:387
  64.9 1.7 %collective-permute-done.12.refs_2_ = f32[40,128]{1,0:T(8,128)S(1)} collective-permute-done((f32[40,128]{1,0:T(8,128)S(1)}, f32[40,128]{1,0:T(8,128)S(1)}, u32[]{:S(2)}, u32[]{:S(2)}) %collective-permute-start.12) | collective-permute-done | bytes 20512 | tf_op jit(solution)/shard_map/ppermute | solution.py:533
  66.5 0.5 collective-permute-done.13.refs_3_
  67.0 3.3 %combine.1 = (f32[1,3,8,1024]{3,2,1,0:T(8,128)}, f32[1,64]{1,0:T(1,128)}, f32[1,128]{1,0:T(1,128)}) custom-call(s32[1]{0:T(128)} %bitcast.group_ref, s32[1]{0:T(128)} %bitcast.1.band_ref, s32[1]{0:T(128)} %bitcast.2.core_ref, f32[40,128]{1,0:T(8,128)S(1)} %add_add_fusion.share_ref.refs_0_, f32[40,128]{1,0:T(8,128)S(1)} %collective-permute-done.11.refs_1_, ...), custom_call_target="tpu_custom_call" | custom-call | tf_op jit(solution)/shard_map/combine/pallas_call | solution.py:510
  (19 shorter events, 0.2 us)
Async XLA Ops:
  2.1 6.5 %collective-permute-start = (bf16[16,1024]{1,0:T(8,128)(2,1)S(1)}, bf16[16,1024]{1,0:T(8,128)(2,1)S(1)}, u32[]{:S(2)}, u32[]{:S(2)}) collective-permute-start(bf16[16,1024]{1,0:T(8,128)(2,1)S(1)} %get-tuple-element.23), channel_id=1, source_target_pairs={{1,2},{2,1},{3,4},{4,3},{5,6},{6,5},{7,8},{8,7},{9,10},{10,9},{11,... | collective-permute-start | bytes 98312 | tf_op jit(solution)/shard_map/ppermute | solution.py:555
  2.8 9.5 %copy-start = (s32[1,128]{1,0:T(1,128)S(1)}, s32[1,128]{1,0:T(1,128)}, u32[]{:S(2)}) copy-start(s32[1,128]{1,0:T(1,128)} %station_row_ref.1) | copy-start | bytes 1540
  2.8 9.5 %copy-start.1 = (s32[1,128]{1,0:T(1,128)S(1)}, s32[1,128]{1,0:T(1,128)}, u32[]{:S(2)}) copy-start(s32[1,128]{1,0:T(1,128)} %station_column_ref.1) | copy-start | bytes 1540
  2.8 9.5 %copy-start.2 = (f32[1,128]{1,0:T(1,128)S(1)}, f32[1,128]{1,0:T(1,128)}, u32[]{:S(2)}) copy-start(f32[1,128]{1,0:T(1,128)} %station_value_ref.1) | copy-start | bytes 1540
  2.8 5.8 %collective-permute-start.1 = (bf16[16,1024]{1,0:T(8,128)(2,1)S(1)}, bf16[16,1024]{1,0:T(8,128)(2,1)S(1)}, u32[]{:S(2)}, u32[]{:S(2)}) collective-permute-start(bf16[16,1024]{1,0:T(8,128)(2,1)S(1)} %get-tuple-element.24), channel_id=1, source_target_pairs={{0,1},{1,0},{2,3},{3,2},{4,5},{5,4},{6,7},{7,6},{8,9},{9,8},{10,11... | collective-permute-start | bytes 98312 | tf_op jit(solution)/shard_map/ppermute | solution.py:556
  8.6 26.7 %collective-permute-start.2 = (bf16[12,64,1024]{2,1,0:T(8,128)(2,1)S(1)}, bf16[12,64,1024]{2,1,0:T(8,128)(2,1)}, u32[]{:S(2)}, u32[]{:S(2)}) collective-permute-start(bf16[12,64,1024]{2,1,0:T(8,128)(2,1)S(1)} %get-tuple-element.27.outer_ref.refs_4_), channel_id=1, source_target_pairs={{1,2},{2,1},{3,4},{4,3},{5,6},{6,5},{7,8},{8,7},{9,10},{10,9},{11,... | collective-permute-start | bytes 4718600 | tf_op jit(solution)/shard_map/ppermute | solution.py:561
  10.5 24.9 %collective-permute-start.3 = (bf16[12,64,1024]{2,1,0:T(8,128)(2,1)S(1)}, bf16[12,64,1024]{2,1,0:T(8,128)(2,1)}, u32[]{:S(2)}, u32[]{:S(2)}) collective-permute-start(bf16[12,64,1024]{2,1,0:T(8,128)(2,1)S(1)} %get-tuple-element.28.inner_ref.refs_5_), channel_id=1, source_target_pairs={{0,1},{1,0},{2,3},{3,2},{4,5},{5,4},{6,7},{7,6},{8,9},{9,8},{10,11... | collective-permute-start | bytes 4718600 | tf_op jit(solution)/shard_map/ppermute | solution.py:562
  39.3 1.3 %collective-permute-start.4 = (f32[40,128]{1,0:T(8,128)S(1)}, f32[40,128]{1,0:T(8,128)S(1)}, u32[]{:S(2)}, u32[]{:S(2)}) collective-permute-start(f32[40,128]{1,0:T(8,128)S(1)} %join.1), channel_id=1, source_target_pairs={{1,0},{0,1},{3,2},{2,3},{5,4},{4,5},{7,6},{6,7},{9,8},{8,9},{11,10... | collective-permute-start | bytes 61448 | tf_op jit(solution)/shard_map/ppermute | solution.py:533
  40.6 5.4 %collective-permute-start.5 = (f32[40,128]{1,0:T(8,128)S(1)}, f32[40,128]{1,0:T(8,128)S(1)}, u32[]{:S(2)}, u32[]{:S(2)}) collective-permute-start(f32[40,128]{1,0:T(8,128)S(1)} %add.29), channel_id=1, source_target_pairs={{2,0},{4,2},{6,4},{0,6},{3,1},{5,3},{7,5},{1,7},{10,8},{12,10},{14... | collective-permute-start | bytes 61448 | tf_op jit(solution)/shard_map/ppermute | solution.py:533
  44.5 5.3 %collective-permute-start.6 = (f32[40,128]{1,0:T(8,128)S(1)}, f32[40,128]{1,0:T(8,128)S(1)}, u32[]{:S(2)}, u32[]{:S(2)}) collective-permute-start(f32[40,128]{1,0:T(8,128)S(1)} %add.29), channel_id=1, source_target_pairs={{4,0},{6,2},{0,4},{2,6},{5,1},{7,3},{1,5},{3,7},{12,8},{14,10},{8,... | collective-permute-start | bytes 61448 | tf_op jit(solution)/shard_map/ppermute | solution.py:533
  44.5 5.3 %collective-permute-start.7 = (f32[40,128]{1,0:T(8,128)S(1)}, f32[40,128]{1,0:T(8,128)S(1)}, u32[]{:S(2)}, u32[]{:S(2)}) collective-permute-start(f32[40,128]{1,0:T(8,128)S(1)} %add.29), channel_id=1, source_target_pairs={{6,0},{0,2},{2,4},{4,6},{7,1},{1,3},{3,5},{5,7},{14,8},{8,10},{10,... | collective-permute-start | bytes 61448 | tf_op jit(solution)/shard_map/ppermute | solution.py:533
  49.8 5.7 %collective-permute-start.10 = (f32[40,128]{1,0:T(8,128)S(1)}, f32[40,128]{1,0:T(8,128)S(1)}, u32[]{:S(2)}, u32[]{:S(2)}) collective-permute-start(f32[40,128]{1,0:T(8,128)S(1)} %add_add_fusion.1), channel_id=1, source_target_pairs={{24,0},{0,8},{8,16},{16,24},{25,1},{1,9},{9,17},{17,25},{26,2},{2,... | collective-permute-start | bytes 61448 | tf_op jit(solution)/shard_map/ppermute | solution.py:533
  51.8 3.8 %collective-permute-start.8 = (f32[40,128]{1,0:T(8,128)S(1)}, f32[40,128]{1,0:T(8,128)S(1)}, u32[]{:S(2)}, u32[]{:S(2)}) collective-permute-start(f32[40,128]{1,0:T(8,128)S(1)} %add_add_fusion.1), channel_id=1, source_target_pairs={{8,0},{16,8},{24,16},{0,24},{9,1},{17,9},{25,17},{1,25},{10,2},{18... | collective-permute-start | bytes 61448 | tf_op jit(solution)/shard_map/ppermute | solution.py:533
  53.1 5.3 %collective-permute-start.9 = (f32[40,128]{1,0:T(8,128)S(1)}, f32[40,128]{1,0:T(8,128)S(1)}, u32[]{:S(2)}, u32[]{:S(2)}) collective-permute-start(f32[40,128]{1,0:T(8,128)S(1)} %add_add_fusion.1), channel_id=1, source_target_pairs={{16,0},{24,8},{0,16},{8,24},{17,1},{25,9},{1,17},{9,25},{18,2},{26... | collective-permute-start | bytes 61448 | tf_op jit(solution)/shard_map/ppermute | solution.py:533
  58.4 6.4 %collective-permute-start.11 = (f32[40,128]{1,0:T(8,128)S(1)}, f32[40,128]{1,0:T(8,128)S(1)}, u32[]{:S(2)}, u32[]{:S(2)}) collective-permute-start(f32[40,128]{1,0:T(8,128)S(1)} %add_add_fusion.share_ref.refs_0_), channel_id=1, source_target_pairs={{32,0},{64,32},{96,64},{0,96},{33,1},{65,33},{97,65},{1,97},{34,2}... | collective-permute-start | bytes 61448 | tf_op jit(solution)/shard_map/ppermute | solution.py:533
  61.3 5.3 %collective-permute-start.12 = (f32[40,128]{1,0:T(8,128)S(1)}, f32[40,128]{1,0:T(8,128)S(1)}, u32[]{:S(2)}, u32[]{:S(2)}) collective-permute-start(f32[40,128]{1,0:T(8,128)S(1)} %add_add_fusion.share_ref.refs_0_), channel_id=1, source_target_pairs={{64,0},{96,32},{0,64},{32,96},{65,1},{97,33},{1,65},{33,97},{66,2}... | collective-permute-start | bytes 61448 | tf_op jit(solution)/shard_map/ppermute | solution.py:533
  62.0 5.0 %collective-permute-start.13 = (f32[40,128]{1,0:T(8,128)S(1)}, f32[40,128]{1,0:T(8,128)S(1)}, u32[]{:S(2)}, u32[]{:S(2)}) collective-permute-start(f32[40,128]{1,0:T(8,128)S(1)} %add_add_fusion.share_ref.refs_0_), channel_id=1, source_target_pairs={{96,0},{0,32},{32,64},{64,96},{97,1},{1,33},{33,65},{65,97},{98,2}... | collective-permute-start | bytes 61448 | tf_op jit(solution)/shard_map/ppermute | solution.py:533

commit v5 on v4

--- a/solution.py
+++ b/solution.py
@@ -432,8 +432,9 @@
     left = lane < rank
     row = jnp.zeros((1, 2 * rank), jnp.float32)
     cost = jnp.zeros((1, 2 * rank), jnp.float32)
+    places = dict(zip((0, *farthest_first(groups)), shares))
     for ahead in reversed(range(groups)):
-        share = shares[ahead][...]
+        share = places[ahead][...]
         cost += share[half + 1 : half + 2]
         upper = jnp.sum(jnp.where(lane == line, row, 0.0), axis=1, keepdims=True)
         lower = jnp.sum(jnp.where(lane == line + half, row, 0.0), axis=1, keepdims=True)
@@ -533,8 +534,12 @@
     return lax.ppermute(x, axis, [((i + by) % count, i) for i in range(count)])
 
 
+def farthest_first(count):
+    return sorted(range(1, count), key=lambda by: -min(by, count - by))
+
+
 def added_over(x, axis):
-    others = [from_ahead(x, axis, by) for by in range(1, lax.axis_size(axis))]
+    others = [from_ahead(x, axis, by) for by in farthest_first(lax.axis_size(axis))]
     return functools.reduce(jnp.add, others, x)
 
 
@@ -570,7 +575,8 @@
     for axis in ("lat_2", "lat_1", "lat_0"):
         share = added_over(share, axis)
     far_outer, far_inner = fetch(far_outer, far_inner, share)
-    shares = [share] + [from_ahead(share, "tm", by) for by in range(1, groups)]
+    order = farthest_first(groups)
+    shares = [share] + [from_ahead(share, "tm", by) for by in order]
     increment, adjoint, total_cost = combine(
         group, band, core, shares, (outer, inner, far_outer, far_inner), coef, 1.0 / math.sqrt(rank), bands
     )

time: 70.8 us -> 71.9 us (1.016)
  starting transfers between devices: 22.6 us -> 24.1 us
    ppermute x10, starting transfers between devices: 15.1 us -> 16.7 us  [from_ahead(): return lax.ppermute(x, axis, [((i + by) % count, i) for i in range(count)])]
  transfers between devices with their start and end apart: 14 -> 14, of which waited for: 7 -> 7; matrix products, arithmetic and copies ran while one was open for 0% -> 0% of each run, Pallas kernels for 39% -> 38%
where the time goes in v5:
time: 71.9 us; the launch traced here: 71.6 us
  Pallas kernels  35.7 us (50%)
  starting transfers between devices  24.1 us (34%)
  waiting for transfers between devices  10.2 us (14%)
  between operations  1.58 us (2%)
    pallas_call x1, Pallas kernels, sweep(): pl.pallas_call(functools.partial(sweep_kernel, scales, bands), out_shape=...  23 us
    ppermute x10, starting transfers between devices, from_ahead(): return lax.ppermute(x, axis, [((i + by) % count, i) for i in range(count)])  16.7 us
    ppermute x10, waiting for transfers between devices, from_ahead(): return lax.ppermute(x, axis, [((i + by) % count, i) for i in range(count)])  10.2 us
    pallas_call x1, Pallas kernels, join(): pl.pallas_call(functools.partial(join_kernel, scale), out_shape=jax.Shape...  3.97 us
    pallas_call x1, Pallas kernels, combine(): pl.pallas_call(functools.partial(combine_kernel, scale, len(shares), band...  3.34 us
    ppermute x1, starting transfers between devices, body(): far_inner_base = lax.ppermute(inner_base, 'lat_2', inside_chip)  3.1 us
    pallas_call x1, Pallas kernels, pack(): pl.pallas_call(pack_kernel, out_shape=(half, half), in_specs=[SMEM, HBM],...  2.68 us
    pallas_call x1, Pallas kernels, fetch(): pl.pallas_call(fetch_kernel, out_shape=(received, received), in_specs=[HB...  1.9 us
  transfers between devices with their start and end apart: 14, of which 7 were waited for; matrix products, arithmetic and copies ran while one was open for 0% of the time, Pallas kernels for 38%

profile of v5, /device:TPU:0, one launch (start us, length us, event | category | flops | bytes accessed | tf_op | source)
XLA Modules:
  0.0 71.6 jit_solution(8139957986541996060)
XLA Ops:
  1.3 0.8 %pick.1 = (bf16[16,1024]{1,0:T(8,128)(2,1)S(1)}, bf16[16,1024]{1,0:T(8,128)(2,1)S(1)}, f32[3,8,1024]{2,1,0:T(8,128)S(1)}) custom-call(s32[1]{0:T(128)S(6)} %copy.10.step_ref, s32[1]{0:T(128)} %bitcast.2.core_ref, bf16[4,3,8,1024]{3,2,1,0:T(8,128)(2,1)} %base_hbm.1), custom_call_target="tpu_custom_call" | custom-call | tf_op jit(solution)/shard_map/pick/pallas_call | solution.py:69
  2.8 3.1 %collective-permute-start.1 = (bf16[16,1024]{1,0:T(8,128)(2,1)S(1)}, bf16[16,1024]{1,0:T(8,128)(2,1)S(1)}, u32[]{:S(2)}, u32[]{:S(2)}) collective-permute-start(bf16[16,1024]{1,0:T(8,128)(2,1)S(1)} %get-tuple-element.24), channel_id=1, source_target_pairs={{0,1},{1,0},{2,3},{3,2},{4,5},{5,4},{6,7},{7,6},{8,9},{9,8},{10,11... | collective-permute-start | bytes 98312 | tf_op jit(solution)/shard_map/ppermute | solution.py:561
  5.9 2.7 %pack.1 = (bf16[12,64,1024]{2,1,0:T(8,128)(2,1)S(1)}, bf16[12,64,1024]{2,1,0:T(8,128)(2,1)S(1)}) custom-call(s32[1]{0:T(128)} %bitcast.2.core_ref, bf16[64,3,8,1024]{3,2,1,0:T(8,128)(2,1)} %sketch_hbm.1), custom_call_target="tpu_custom_call" | custom-call | tf_op jit(solution)/shard_map/pack/pallas_call | solution.py:112
  8.6 1.8 %collective-permute-start.2 = (bf16[12,64,1024]{2,1,0:T(8,128)(2,1)S(1)}, bf16[12,64,1024]{2,1,0:T(8,128)(2,1)}, u32[]{:S(2)}, u32[]{:S(2)}) collective-permute-start(bf16[12,64,1024]{2,1,0:T(8,128)(2,1)S(1)} %get-tuple-element.27.outer_ref.refs_4_), channel_id=1, source_target_pairs={{1,2},{2,1},{3,4},{4,3},{5,6},{6,5},{7,8},{8,7},{9,10},{10,9},{11,... | collective-permute-start | bytes 4718600 | tf_op jit(solution)/shard_map/ppermute | solution.py:566
  10.5 1.8 %collective-permute-start.3 = (bf16[12,64,1024]{2,1,0:T(8,128)(2,1)S(1)}, bf16[12,64,1024]{2,1,0:T(8,128)(2,1)}, u32[]{:S(2)}, u32[]{:S(2)}) collective-permute-start(bf16[12,64,1024]{2,1,0:T(8,128)(2,1)S(1)} %get-tuple-element.28.inner_ref.refs_5_), channel_id=1, source_target_pairs={{0,1},{1,0},{2,3},{3,2},{4,5},{5,4},{6,7},{7,6},{8,9},{9,8},{10,11... | collective-permute-start | bytes 4718600 | tf_op jit(solution)/shard_map/ppermute | solution.py:567
  12.3 23.0 %sweep.1 = (bf16[48,128,1024]{2,1,0:T(8,128)(2,1)S(1)}, f32[3,16,1024]{2,1,0:T(8,128)S(1)}, f32[8,64]{1,0:T(8,128)S(1)}) custom-call(s32[1]{0:T(128)} %bitcast.1.band_ref, s32[1]{0:T(128)} %bitcast.2.core_ref, bf16[64,3,8,1024]{3,2,1,0:T(8,128)(2,1)} %test_hbm.1, f32[3,8,1024]{2,1,0:T(8,128)S(1)} %get-tuple-element.20.base_ref, ...), custom_call_target="tpu_custom_call" | custom-call | flops 2000000000 | bytes 30000000 | tf_op jit(solution)/shard_map/sweep/pallas_call | solution.py:285
  35.3 4.0 %join.1 = f32[40,128]{1,0:T(8,128)S(1)} custom-call(s32[1]{0:T(128)} %bitcast.2.core_ref, bf16[48,128,1024]{2,1,0:T(8,128)(2,1)S(1)} %get-tuple-element.29.back_ref, f32[8,64]{1,0:T(8,128)S(1)} %get-tuple-element.30.tail_ref, bf16[12,64,1024]{2,1,0:T(8,128)(2,1)S(1)} %get-tuple-element.27.outer_ref.refs_4_, ...), custom_call_target="tpu_custom_call" | custom-call | tf_op jit(solution)/shard_map/join/pallas_call | solution.py:358
  39.4 1.2 %collective-permute-done.4 = f32[40,128]{1,0:T(8,128)S(1)} collective-permute-done((f32[40,128]{1,0:T(8,128)S(1)}, f32[40,128]{1,0:T(8,128)S(1)}, u32[]{:S(2)}, u32[]{:S(2)}) %collective-permute-start.4) | collective-permute-done | bytes 20512 | tf_op jit(solution)/shard_map/ppermute | solution.py:534
  40.6 2.9 %collective-permute-start.5 = (f32[40,128]{1,0:T(8,128)S(1)}, f32[40,128]{1,0:T(8,128)S(1)}, u32[]{:S(2)}, u32[]{:S(2)}) collective-permute-start(f32[40,128]{1,0:T(8,128)S(1)} %add.29), channel_id=1, source_target_pairs={{4,0},{6,2},{0,4},{2,6},{5,1},{7,3},{1,5},{3,7},{12,8},{14,10},{8,... | collective-permute-start | bytes 61448 | tf_op jit(solution)/shard_map/ppermute | solution.py:534
  43.5 1.1 %collective-permute-start.6 = (f32[40,128]{1,0:T(8,128)S(1)}, f32[40,128]{1,0:T(8,128)S(1)}, u32[]{:S(2)}, u32[]{:S(2)}) collective-permute-start(f32[40,128]{1,0:T(8,128)S(1)} %add.29), channel_id=1, source_target_pairs={{2,0},{4,2},{6,4},{0,6},{3,1},{5,3},{7,5},{1,7},{10,8},{12,10},{14... | collective-permute-start | bytes 61448 | tf_op jit(solution)/shard_map/ppermute | solution.py:534
  44.6 0.9 %collective-permute-start.7 = (f32[40,128]{1,0:T(8,128)S(1)}, f32[40,128]{1,0:T(8,128)S(1)}, u32[]{:S(2)}, u32[]{:S(2)}) collective-permute-start(f32[40,128]{1,0:T(8,128)S(1)} %add.29), channel_id=1, source_target_pairs={{6,0},{0,2},{2,4},{4,6},{7,1},{1,3},{3,5},{5,7},{14,8},{8,10},{10,... | collective-permute-start | bytes 61448 | tf_op jit(solution)/shard_map/ppermute | solution.py:534
  45.9 1.5 %collective-permute-done.6 = f32[40,128]{1,0:T(8,128)S(1)} collective-permute-done((f32[40,128]{1,0:T(8,128)S(1)}, f32[40,128]{1,0:T(8,128)S(1)}, u32[]{:S(2)}, u32[]{:S(2)}) %collective-permute-start.6) | collective-permute-done | bytes 20512 | tf_op jit(solution)/shard_map/ppermute | solution.py:534
  47.3 2.2 %collective-permute-done.7 = f32[40,128]{1,0:T(8,128)S(1)} collective-permute-done((f32[40,128]{1,0:T(8,128)S(1)}, f32[40,128]{1,0:T(8,128)S(1)}, u32[]{:S(2)}, u32[]{:S(2)}) %collective-permute-start.7) | collective-permute-done | bytes 20512 | tf_op jit(solution)/shard_map/ppermute | solution.py:534
  49.6 2.0 %collective-permute-start.10 = (f32[40,128]{1,0:T(8,128)S(1)}, f32[40,128]{1,0:T(8,128)S(1)}, u32[]{:S(2)}, u32[]{:S(2)}) collective-permute-start(f32[40,128]{1,0:T(8,128)S(1)} %add_add_fusion.1), channel_id=1, source_target_pairs={{24,0},{0,8},{8,16},{16,24},{25,1},{1,9},{9,17},{17,25},{26,2},{2,... | collective-permute-start | bytes 61448 | tf_op jit(solution)/shard_map/ppermute | solution.py:534
  51.6 3.5 %collective-permute-start.8 = (f32[40,128]{1,0:T(8,128)S(1)}, f32[40,128]{1,0:T(8,128)S(1)}, u32[]{:S(2)}, u32[]{:S(2)}) collective-permute-start(f32[40,128]{1,0:T(8,128)S(1)} %add_add_fusion.1), channel_id=1, source_target_pairs={{16,0},{24,8},{0,16},{8,24},{17,1},{25,9},{1,17},{9,25},{18,2},{26... | collective-permute-start | bytes 61448 | tf_op jit(solution)/shard_map/ppermute | solution.py:534
  55.1 1.0 %collective-permute-start.9 = (f32[40,128]{1,0:T(8,128)S(1)}, f32[40,128]{1,0:T(8,128)S(1)}, u32[]{:S(2)}, u32[]{:S(2)}) collective-permute-start(f32[40,128]{1,0:T(8,128)S(1)} %add_add_fusion.1), channel_id=1, source_target_pairs={{8,0},{16,8},{24,16},{0,24},{9,1},{17,9},{25,17},{1,25},{10,2},{18... | collective-permute-start | bytes 61448 | tf_op jit(solution)/shard_map/ppermute | solution.py:534
  56.1 1.0 %collective-permute-done.8 = f32[40,128]{1,0:T(8,128)S(1)} collective-permute-done((f32[40,128]{1,0:T(8,128)S(1)}, f32[40,128]{1,0:T(8,128)S(1)}, u32[]{:S(2)}, u32[]{:S(2)}) %collective-permute-start.8) | collective-permute-done | bytes 20512 | tf_op jit(solution)/shard_map/ppermute | solution.py:534
  57.1 1.8 %collective-permute-done.9 = f32[40,128]{1,0:T(8,128)S(1)} collective-permute-done((f32[40,128]{1,0:T(8,128)S(1)}, f32[40,128]{1,0:T(8,128)S(1)}, u32[]{:S(2)}, u32[]{:S(2)}) %collective-permute-start.9) | collective-permute-done | bytes 20512 | tf_op jit(solution)/shard_map/ppermute | solution.py:534
  58.9 3.1 %collective-permute-start.11 = (f32[40,128]{1,0:T(8,128)S(1)}, f32[40,128]{1,0:T(8,128)S(1)}, u32[]{:S(2)}, u32[]{:S(2)}) collective-permute-start(f32[40,128]{1,0:T(8,128)S(1)} %add_add_fusion.share_ref.refs_0_), channel_id=1, source_target_pairs={{64,0},{96,32},{0,64},{32,96},{65,1},{97,33},{1,65},{33,97},{66,2}... | collective-permute-start | bytes 61448 | tf_op jit(solution)/shard_map/ppermute | solution.py:534
  62.0 1.1 %collective-permute-start.12 = (f32[40,128]{1,0:T(8,128)S(1)}, f32[40,128]{1,0:T(8,128)S(1)}, u32[]{:S(2)}, u32[]{:S(2)}) collective-permute-start(f32[40,128]{1,0:T(8,128)S(1)} %add_add_fusion.share_ref.refs_0_), channel_id=1, source_target_pairs={{32,0},{64,32},{96,64},{0,96},{33,1},{65,33},{97,65},{1,97},{34,2}... | collective-permute-start | bytes 61448 | tf_op jit(solution)/shard_map/ppermute | solution.py:534
  63.1 0.9 %collective-permute-start.13 = (f32[40,128]{1,0:T(8,128)S(1)}, f32[40,128]{1,0:T(8,128)S(1)}, u32[]{:S(2)}, u32[]{:S(2)}) collective-permute-start(f32[40,128]{1,0:T(8,128)S(1)} %add_add_fusion.share_ref.refs_0_), channel_id=1, source_target_pairs={{96,0},{0,32},{32,64},{64,96},{97,1},{1,33},{33,65},{65,97},{98,2}... | collective-permute-start | bytes 61448 | tf_op jit(solution)/shard_map/ppermute | solution.py:534
  64.0 1.9 %fetch.1 = (bf16[12,64,1024]{2,1,0:T(8,128)(2,1)S(1)}, bf16[12,64,1024]{2,1,0:T(8,128)(2,1)S(1)}) custom-call(bf16[12,64,1024]{2,1,0:T(8,128)(2,1)} %collective-permute-done.2.outer_hbm, bf16[12,64,1024]{2,1,0:T(8,128)(2,1)} %collective-permute-done.3.inner_hbm, f32[40,128]{1,0:T(8,128)S(1)} %add_add_fusion.share_ref.refs_0_), custom_call_target="tpu_custom_call" | custom-call | bytes 6300000 | tf_op jit(solution)/shard_map/fetch/pallas_call | solution.py:387
  66.0 2.2 %collective-permute-done.13.refs_3_ = f32[40,128]{1,0:T(8,128)S(1)} collective-permute-done((f32[40,128]{1,0:T(8,128)S(1)}, f32[40,128]{1,0:T(8,128)S(1)}, u32[]{:S(2)}, u32[]{:S(2)}) %collective-permute-start.13) | collective-permute-done | bytes 20512 | tf_op jit(solution)/shard_map/ppermute | solution.py:534
  68.1 3.3 %combine.1 = (f32[1,3,8,1024]{3,2,1,0:T(8,128)}, f32[1,64]{1,0:T(1,128)}, f32[1,128]{1,0:T(1,128)}) custom-call(s32[1]{0:T(128)} %bitcast.group_ref, s32[1]{0:T(128)} %bitcast.1.band_ref, s32[1]{0:T(128)} %bitcast.2.core_ref, f32[40,128]{1,0:T(8,128)S(1)} %add_add_fusion.share_ref.refs_0_, f32[40,128]{1,0:T(8,128)S(1)} %collective-permute-done.11.refs_1_, ...), custom_call_target="tpu_custom_call" | custom-call | tf_op jit(solution)/shard_map/combine/pallas_call | solution.py:511
  (19 shorter events, 1.2 us)
Async XLA Ops:
  2.1 6.5 %collective-permute-start = (bf16[16,1024]{1,0:T(8,128)(2,1)S(1)}, bf16[16,1024]{1,0:T(8,128)(2,1)S(1)}, u32[]{:S(2)}, u32[]{:S(2)}) collective-permute-start(bf16[16,1024]{1,0:T(8,128)(2,1)S(1)} %get-tuple-element.23), channel_id=1, source_target_pairs={{1,2},{2,1},{3,4},{4,3},{5,6},{6,5},{7,8},{8,7},{9,10},{10,9},{11,... | collective-permute-start | bytes 98312 | tf_op jit(solution)/shard_map/ppermute | solution.py:560
  2.8 9.5 %copy-start = (s32[1,128]{1,0:T(1,128)S(1)}, s32[1,128]{1,0:T(1,128)}, u32[]{:S(2)}) copy-start(s32[1,128]{1,0:T(1,128)} %station_row_ref.1) | copy-start | bytes 1540
  2.8 9.5 %copy-start.1 = (s32[1,128]{1,0:T(1,128)S(1)}, s32[1,128]{1,0:T(1,128)}, u32[]{:S(2)}) copy-start(s32[1,128]{1,0:T(1,128)} %station_column_ref.1) | copy-start | bytes 1540
  2.8 9.5 %copy-start.2 = (f32[1,128]{1,0:T(1,128)S(1)}, f32[1,128]{1,0:T(1,128)}, u32[]{:S(2)}) copy-start(f32[1,128]{1,0:T(1,128)} %station_value_ref.1) | copy-start | bytes 1540
  2.8 5.8 %collective-permute-start.1 = (bf16[16,1024]{1,0:T(8,128)(2,1)S(1)}, bf16[16,1024]{1,0:T(8,128)(2,1)S(1)}, u32[]{:S(2)}, u32[]{:S(2)}) collective-permute-start(bf16[16,1024]{1,0:T(8,128)(2,1)S(1)} %get-tuple-element.24), channel_id=1, source_target_pairs={{0,1},{1,0},{2,3},{3,2},{4,5},{5,4},{6,7},{7,6},{8,9},{9,8},{10,11... | collective-permute-start | bytes 98312 | tf_op jit(solution)/shard_map/ppermute | solution.py:561
  8.6 26.7 %collective-permute-start.2 = (bf16[12,64,1024]{2,1,0:T(8,128)(2,1)S(1)}, bf16[12,64,1024]{2,1,0:T(8,128)(2,1)}, u32[]{:S(2)}, u32[]{:S(2)}) collective-permute-start(bf16[12,64,1024]{2,1,0:T(8,128)(2,1)S(1)} %get-tuple-element.27.outer_ref.refs_4_), channel_id=1, source_target_pairs={{1,2},{2,1},{3,4},{4,3},{5,6},{6,5},{7,8},{8,7},{9,10},{10,9},{11,... | collective-permute-start | bytes 4718600 | tf_op jit(solution)/shard_map/ppermute | solution.py:566
  10.5 24.9 %collective-permute-start.3 = (bf16[12,64,1024]{2,1,0:T(8,128)(2,1)S(1)}, bf16[12,64,1024]{2,1,0:T(8,128)(2,1)}, u32[]{:S(2)}, u32[]{:S(2)}) collective-permute-start(bf16[12,64,1024]{2,1,0:T(8,128)(2,1)S(1)} %get-tuple-element.28.inner_ref.refs_5_), channel_id=1, source_target_pairs={{0,1},{1,0},{2,3},{3,2},{4,5},{5,4},{6,7},{7,6},{8,9},{9,8},{10,11... | collective-permute-start | bytes 4718600 | tf_op jit(solution)/shard_map/ppermute | solution.py:567
  39.3 1.3 %collective-permute-start.4 = (f32[40,128]{1,0:T(8,128)S(1)}, f32[40,128]{1,0:T(8,128)S(1)}, u32[]{:S(2)}, u32[]{:S(2)}) collective-permute-start(f32[40,128]{1,0:T(8,128)S(1)} %join.1), channel_id=1, source_target_pairs={{1,0},{0,1},{3,2},{2,3},{5,4},{4,5},{7,6},{6,7},{9,8},{8,9},{11,10... | collective-permute-start | bytes 61448 | tf_op jit(solution)/shard_map/ppermute | solution.py:534
  40.6 5.3 %collective-permute-start.5 = (f32[40,128]{1,0:T(8,128)S(1)}, f32[40,128]{1,0:T(8,128)S(1)}, u32[]{:S(2)}, u32[]{:S(2)}) collective-permute-start(f32[40,128]{1,0:T(8,128)S(1)} %add.29), channel_id=1, source_target_pairs={{4,0},{6,2},{0,4},{2,6},{5,1},{7,3},{1,5},{3,7},{12,8},{14,10},{8,... | collective-permute-start | bytes 61448 | tf_op jit(solution)/shard_map/ppermute | solution.py:534
  43.5 3.8 %collective-permute-start.6 = (f32[40,128]{1,0:T(8,128)S(1)}, f32[40,128]{1,0:T(8,128)S(1)}, u32[]{:S(2)}, u32[]{:S(2)}) collective-permute-start(f32[40,128]{1,0:T(8,128)S(1)} %add.29), channel_id=1, source_target_pairs={{2,0},{4,2},{6,4},{0,6},{3,1},{5,3},{7,5},{1,7},{10,8},{12,10},{14... | collective-permute-start | bytes 61448 | tf_op jit(solution)/shard_map/ppermute | solution.py:534
  44.6 5.0 %collective-permute-start.7 = (f32[40,128]{1,0:T(8,128)S(1)}, f32[40,128]{1,0:T(8,128)S(1)}, u32[]{:S(2)}, u32[]{:S(2)}) collective-permute-start(f32[40,128]{1,0:T(8,128)S(1)} %add.29), channel_id=1, source_target_pairs={{6,0},{0,2},{2,4},{4,6},{7,1},{1,3},{3,5},{5,7},{14,8},{8,10},{10,... | collective-permute-start | bytes 61448 | tf_op jit(solution)/shard_map/ppermute | solution.py:534
  49.6 6.5 %collective-permute-start.10 = (f32[40,128]{1,0:T(8,128)S(1)}, f32[40,128]{1,0:T(8,128)S(1)}, u32[]{:S(2)}, u32[]{:S(2)}) collective-permute-start(f32[40,128]{1,0:T(8,128)S(1)} %add_add_fusion.1), channel_id=1, source_target_pairs={{24,0},{0,8},{8,16},{16,24},{25,1},{1,9},{9,17},{17,25},{26,2},{2,... | collective-permute-start | bytes 61448 | tf_op jit(solution)/shard_map/ppermute | solution.py:534
  51.6 5.5 %collective-permute-start.8 = (f32[40,128]{1,0:T(8,128)S(1)}, f32[40,128]{1,0:T(8,128)S(1)}, u32[]{:S(2)}, u32[]{:S(2)}) collective-permute-start(f32[40,128]{1,0:T(8,128)S(1)} %add_add_fusion.1), channel_id=1, source_target_pairs={{16,0},{24,8},{0,16},{8,24},{17,1},{25,9},{1,17},{9,25},{18,2},{26... | collective-permute-start | bytes 61448 | tf_op jit(solution)/shard_map/ppermute | solution.py:534
  55.1 3.8 %collective-permute-start.9 = (f32[40,128]{1,0:T(8,128)S(1)}, f32[40,128]{1,0:T(8,128)S(1)}, u32[]{:S(2)}, u32[]{:S(2)}) collective-permute-start(f32[40,128]{1,0:T(8,128)S(1)} %add_add_fusion.1), channel_id=1, source_target_pairs={{8,0},{16,8},{24,16},{0,24},{9,1},{17,9},{25,17},{1,25},{10,2},{18... | collective-permute-start | bytes 61448 | tf_op jit(solution)/shard_map/ppermute | solution.py:534
  58.9 7.0 %collective-permute-start.11 = (f32[40,128]{1,0:T(8,128)S(1)}, f32[40,128]{1,0:T(8,128)S(1)}, u32[]{:S(2)}, u32[]{:S(2)}) collective-permute-start(f32[40,128]{1,0:T(8,128)S(1)} %add_add_fusion.share_ref.refs_0_), channel_id=1, source_target_pairs={{64,0},{96,32},{0,64},{32,96},{65,1},{97,33},{1,65},{33,97},{66,2}... | collective-permute-start | bytes 61448 | tf_op jit(solution)/shard_map/ppermute | solution.py:534
  62.0 3.9 %collective-permute-start.12 = (f32[40,128]{1,0:T(8,128)S(1)}, f32[40,128]{1,0:T(8,128)S(1)}, u32[]{:S(2)}, u32[]{:S(2)}) collective-permute-start(f32[40,128]{1,0:T(8,128)S(1)} %add_add_fusion.share_ref.refs_0_), channel_id=1, source_target_pairs={{32,0},{64,32},{96,64},{0,96},{33,1},{65,33},{97,65},{1,97},{34,2}... | collective-permute-start | bytes 61448 | tf_op jit(solution)/shard_map/ppermute | solution.py:534
  63.1 5.0 %collective-permute-start.13 = (f32[40,128]{1,0:T(8,128)S(1)}, f32[40,128]{1,0:T(8,128)S(1)}, u32[]{:S(2)}, u32[]{:S(2)}) collective-permute-start(f32[40,128]{1,0:T(8,128)S(1)} %add_add_fusion.share_ref.refs_0_), channel_id=1, source_target_pairs={{96,0},{0,32},{32,64},{64,96},{97,1},{1,33},{33,65},{65,97},{98,2}... | collective-permute-start | bytes 61448 | tf_op jit(solution)/shard_map/ppermute | solution.py:534

commit v6 on v5

--- a/solution.py
+++ b/solution.py
@@ -432,7 +432,7 @@
     left = lane < rank
     row = jnp.zeros((1, 2 * rank), jnp.float32)
     cost = jnp.zeros((1, 2 * rank), jnp.float32)
-    places = dict(zip((0, *farthest_first(groups)), shares))
+    places = dict(zip((0, *nearest_first(groups)), shares))
     for ahead in reversed(range(groups)):
         share = places[ahead][...]
         cost += share[half + 1 : half + 2]
@@ -534,12 +534,12 @@
     return lax.ppermute(x, axis, [((i + by) % count, i) for i in range(count)])
 
 
-def farthest_first(count):
-    return sorted(range(1, count), key=lambda by: -min(by, count - by))
+def nearest_first(count):
+    return sorted(range(1, count), key=lambda by: min(by, count - by))
 
 
 def added_over(x, axis):
-    others = [from_ahead(x, axis, by) for by in farthest_first(lax.axis_size(axis))]
+    others = [from_ahead(x, axis, by) for by in nearest_first(lax.axis_size(axis))]
     return functools.reduce(jnp.add, others, x)
 
 
@@ -575,7 +575,7 @@
     for axis in ("lat_2", "lat_1", "lat_0"):
         share = added_over(share, axis)
     far_outer, far_inner = fetch(far_outer, far_inner, share)
-    order = farthest_first(groups)
+    order = nearest_first(groups)
     shares = [share] + [from_ahead(share, "tm", by) for by in order]
     increment, adjoint, total_cost = combine(
         group, band, core, shares, (outer, inner, far_outer, far_inner), coef, 1.0 / math.sqrt(rank), bands

time: 71.9 us -> 71.9 us (level)
  transfers between devices with their start and end apart: 14 -> 14, of which waited for: 7 -> 7; matrix products, arithmetic and copies ran while one was open for 0% -> 0% of each run, Pallas kernels for 38% -> 39%
where the time goes in v6:
time: 71.9 us; the launch traced here: 71.1 us
  Pallas kernels  35.7 us (50%)
  starting transfers between devices  23.8 us (33%)
  waiting for transfers between devices  9.99 us (14%)
  between operations  1.57 us (2%)
    pallas_call x1, Pallas kernels, sweep(): pl.pallas_call(functools.partial(sweep_kernel, scales, bands), out_shape=...  23 us
    ppermute x10, starting transfers between devices, from_ahead(): return lax.ppermute(x, axis, [((i + by) % count, i) for i in range(count)])  16.4 us
    ppermute x10, waiting for transfers between devices, from_ahead(): return lax.ppermute(x, axis, [((i + by) % count, i) for i in range(count)])  9.98 us
    pallas_call x1, Pallas kernels, join(): pl.pallas_call(functools.partial(join_kernel, scale), out_shape=jax.Shape...  3.97 us
    pallas_call x1, Pallas kernels, combine(): pl.pallas_call(functools.partial(combine_kernel, scale, len(shares), band...  3.34 us
    ppermute x1, starting transfers between devices, body(): far_inner_base = lax.ppermute(inner_base, 'lat_2', inside_chip)  3.1 us
    pallas_call x1, Pallas kernels, pack(): pl.pallas_call(pack_kernel, out_shape=(half, half), in_specs=[SMEM, HBM],...  2.68 us
    pallas_call x1, Pallas kernels, fetch(): pl.pallas_call(fetch_kernel, out_shape=(received, received), in_specs=[HB...  1.9 us
  transfers between devices with their start and end apart: 14, of which 7 were waited for; matrix products, arithmetic and copies ran while one was open for 0% of the time, Pallas kernels for 39%

profile of v6, /device:TPU:0, one launch (start us, length us, event | category | flops | bytes accessed | tf_op | source)
XLA Modules:
  0.0 71.1 jit_solution(14554378274356629021)
XLA Ops:
  1.3 0.8 %pick.1 = (bf16[16,1024]{1,0:T(8,128)(2,1)S(1)}, bf16[16,1024]{1,0:T(8,128)(2,1)S(1)}, f32[3,8,1024]{2,1,0:T(8,128)S(1)}) custom-call(s32[1]{0:T(128)S(6)} %copy.10.step_ref, s32[1]{0:T(128)} %bitcast.2.core_ref, bf16[4,3,8,1024]{3,2,1,0:T(8,128)(2,1)} %base_hbm.1), custom_call_target="tpu_custom_call" | custom-call | tf_op jit(solution)/shard_map/pick/pallas_call | solution.py:69
  2.1 0.7 collective-permute-start
  2.8 3.1 %collective-permute-start.1 = (bf16[16,1024]{1,0:T(8,128)(2,1)S(1)}, bf16[16,1024]{1,0:T(8,128)(2,1)S(1)}, u32[]{:S(2)}, u32[]{:S(2)}) collective-permute-start(bf16[16,1024]{1,0:T(8,128)(2,1)S(1)} %get-tuple-element.24), channel_id=1, source_target_pairs={{0,1},{1,0},{2,3},{3,2},{4,5},{5,4},{6,7},{7,6},{8,9},{9,8},{10,11... | collective-permute-start | bytes 98312 | tf_op jit(solution)/shard_map/ppermute | solution.py:561
  5.9 2.7 %pack.1 = (bf16[12,64,1024]{2,1,0:T(8,128)(2,1)S(1)}, bf16[12,64,1024]{2,1,0:T(8,128)(2,1)S(1)}) custom-call(s32[1]{0:T(128)} %bitcast.2.core_ref, bf16[64,3,8,1024]{3,2,1,0:T(8,128)(2,1)} %sketch_hbm.1), custom_call_target="tpu_custom_call" | custom-call | tf_op jit(solution)/shard_map/pack/pallas_call | solution.py:112
  8.6 1.8 %collective-permute-start.2 = (bf16[12,64,1024]{2,1,0:T(8,128)(2,1)S(1)}, bf16[12,64,1024]{2,1,0:T(8,128)(2,1)}, u32[]{:S(2)}, u32[]{:S(2)}) collective-permute-start(bf16[12,64,1024]{2,1,0:T(8,128)(2,1)S(1)} %get-tuple-element.27.outer_ref.refs_4_), channel_id=1, source_target_pairs={{1,2},{2,1},{3,4},{4,3},{5,6},{6,5},{7,8},{8,7},{9,10},{10,9},{11,... | collective-permute-start | bytes 4718600 | tf_op jit(solution)/shard_map/ppermute | solution.py:566
  10.5 1.8 %collective-permute-start.3 = (bf16[12,64,1024]{2,1,0:T(8,128)(2,1)S(1)}, bf16[12,64,1024]{2,1,0:T(8,128)(2,1)}, u32[]{:S(2)}, u32[]{:S(2)}) collective-permute-start(bf16[12,64,1024]{2,1,0:T(8,128)(2,1)S(1)} %get-tuple-element.28.inner_ref.refs_5_), channel_id=1, source_target_pairs={{0,1},{1,0},{2,3},{3,2},{4,5},{5,4},{6,7},{7,6},{8,9},{9,8},{10,11... | collective-permute-start | bytes 4718600 | tf_op jit(solution)/shard_map/ppermute | solution.py:567
  12.3 23.0 %sweep.1 = (bf16[48,128,1024]{2,1,0:T(8,128)(2,1)S(1)}, f32[3,16,1024]{2,1,0:T(8,128)S(1)}, f32[8,64]{1,0:T(8,128)S(1)}) custom-call(s32[1]{0:T(128)} %bitcast.1.band_ref, s32[1]{0:T(128)} %bitcast.2.core_ref, bf16[64,3,8,1024]{3,2,1,0:T(8,128)(2,1)} %test_hbm.1, f32[3,8,1024]{2,1,0:T(8,128)S(1)} %get-tuple-element.20.base_ref, ...), custom_call_target="tpu_custom_call" | custom-call | flops 2000000000 | bytes 30000000 | tf_op jit(solution)/shard_map/sweep/pallas_call | solution.py:285
  35.3 4.0 %join.1 = f32[40,128]{1,0:T(8,128)S(1)} custom-call(s32[1]{0:T(128)} %bitcast.2.core_ref, bf16[48,128,1024]{2,1,0:T(8,128)(2,1)S(1)} %get-tuple-element.29.back_ref, f32[8,64]{1,0:T(8,128)S(1)} %get-tuple-element.30.tail_ref, bf16[12,64,1024]{2,1,0:T(8,128)(2,1)S(1)} %get-tuple-element.27.outer_ref.refs_4_, ...), custom_call_target="tpu_custom_call" | custom-call | tf_op jit(solution)/shard_map/join/pallas_call | solution.py:358
  39.4 1.2 %collective-permute-done.4 = f32[40,128]{1,0:T(8,128)S(1)} collective-permute-done((f32[40,128]{1,0:T(8,128)S(1)}, f32[40,128]{1,0:T(8,128)S(1)}, u32[]{:S(2)}, u32[]{:S(2)}) %collective-permute-start.4) | collective-permute-done | bytes 20512 | tf_op jit(solution)/shard_map/ppermute | solution.py:534
  40.6 3.9 %collective-permute-start.5 = (f32[40,128]{1,0:T(8,128)S(1)}, f32[40,128]{1,0:T(8,128)S(1)}, u32[]{:S(2)}, u32[]{:S(2)}) collective-permute-start(f32[40,128]{1,0:T(8,128)S(1)} %add.29), channel_id=1, source_target_pairs={{2,0},{4,2},{6,4},{0,6},{3,1},{5,3},{7,5},{1,7},{10,8},{12,10},{14... | collective-permute-start | bytes 61448 | tf_op jit(solution)/shard_map/ppermute | solution.py:534
  44.5 1.5 %collective-permute-start.7 = (f32[40,128]{1,0:T(8,128)S(1)}, f32[40,128]{1,0:T(8,128)S(1)}, u32[]{:S(2)}, u32[]{:S(2)}) collective-permute-start(f32[40,128]{1,0:T(8,128)S(1)} %add.29), channel_id=1, source_target_pairs={{4,0},{6,2},{0,4},{2,6},{5,1},{7,3},{1,5},{3,7},{12,8},{14,10},{8,... | collective-permute-start | bytes 61448 | tf_op jit(solution)/shard_map/ppermute | solution.py:534
  46.0 3.5 %collective-permute-done.6 = f32[40,128]{1,0:T(8,128)S(1)} collective-permute-done((f32[40,128]{1,0:T(8,128)S(1)}, f32[40,128]{1,0:T(8,128)S(1)}, u32[]{:S(2)}, u32[]{:S(2)}) %collective-permute-start.6) | collective-permute-done | bytes 20512 | tf_op jit(solution)/shard_map/ppermute | solution.py:534
  49.5 0.3 collective-permute-done.7
  49.8 3.7 %collective-permute-start.10 = (f32[40,128]{1,0:T(8,128)S(1)}, f32[40,128]{1,0:T(8,128)S(1)}, u32[]{:S(2)}, u32[]{:S(2)}) collective-permute-start(f32[40,128]{1,0:T(8,128)S(1)} %add_add_fusion.1), channel_id=1, source_target_pairs={{16,0},{24,8},{0,16},{8,24},{17,1},{25,9},{1,17},{9,25},{18,2},{26... | collective-permute-start | bytes 61448 | tf_op jit(solution)/shard_map/ppermute | solution.py:534
  53.5 1.0 %collective-permute-start.8 = (f32[40,128]{1,0:T(8,128)S(1)}, f32[40,128]{1,0:T(8,128)S(1)}, u32[]{:S(2)}, u32[]{:S(2)}) collective-permute-start(f32[40,128]{1,0:T(8,128)S(1)} %add_add_fusion.1), channel_id=1, source_target_pairs={{8,0},{16,8},{24,16},{0,24},{9,1},{17,9},{25,17},{1,25},{10,2},{18... | collective-permute-start | bytes 61448 | tf_op jit(solution)/shard_map/ppermute | solution.py:534
  54.5 1.0 %collective-permute-start.9 = (f32[40,128]{1,0:T(8,128)S(1)}, f32[40,128]{1,0:T(8,128)S(1)}, u32[]{:S(2)}, u32[]{:S(2)}) collective-permute-start(f32[40,128]{1,0:T(8,128)S(1)} %add_add_fusion.1), channel_id=1, source_target_pairs={{24,0},{0,8},{8,16},{16,24},{25,1},{1,9},{9,17},{17,25},{26,2},{2,... | collective-permute-start | bytes 61448 | tf_op jit(solution)/shard_map/ppermute | solution.py:534
  55.5 1.8 %collective-permute-done.8 = f32[40,128]{1,0:T(8,128)S(1)} collective-permute-done((f32[40,128]{1,0:T(8,128)S(1)}, f32[40,128]{1,0:T(8,128)S(1)}, u32[]{:S(2)}, u32[]{:S(2)}) %collective-permute-start.8) | collective-permute-done | bytes 20512 | tf_op jit(solution)/shard_map/ppermute | solution.py:534
  57.3 2.2 %collective-permute-done.9 = f32[40,128]{1,0:T(8,128)S(1)} collective-permute-done((f32[40,128]{1,0:T(8,128)S(1)}, f32[40,128]{1,0:T(8,128)S(1)}, u32[]{:S(2)}, u32[]{:S(2)}) %collective-permute-start.9) | collective-permute-done | bytes 20512 | tf_op jit(solution)/shard_map/ppermute | solution.py:534
  59.5 2.8 %collective-permute-start.11 = (f32[40,128]{1,0:T(8,128)S(1)}, f32[40,128]{1,0:T(8,128)S(1)}, u32[]{:S(2)}, u32[]{:S(2)}) collective-permute-start(f32[40,128]{1,0:T(8,128)S(1)} %add_add_fusion.share_ref.refs_0_), channel_id=1, source_target_pairs={{32,0},{64,32},{96,64},{0,96},{33,1},{65,33},{97,65},{1,97},{34,2}... | collective-permute-start | bytes 61448 | tf_op jit(solution)/shard_map/ppermute | solution.py:534
  62.3 2.3 %collective-permute-start.13 = (f32[40,128]{1,0:T(8,128)S(1)}, f32[40,128]{1,0:T(8,128)S(1)}, u32[]{:S(2)}, u32[]{:S(2)}) collective-permute-start(f32[40,128]{1,0:T(8,128)S(1)} %add_add_fusion.share_ref.refs_0_), channel_id=1, source_target_pairs={{64,0},{96,32},{0,64},{32,96},{65,1},{97,33},{1,65},{33,97},{66,2}... | collective-permute-start | bytes 61448 | tf_op jit(solution)/shard_map/ppermute | solution.py:534
  64.6 1.9 %fetch.1 = (bf16[12,64,1024]{2,1,0:T(8,128)(2,1)S(1)}, bf16[12,64,1024]{2,1,0:T(8,128)(2,1)S(1)}) custom-call(bf16[12,64,1024]{2,1,0:T(8,128)(2,1)} %collective-permute-done.2.outer_hbm, bf16[12,64,1024]{2,1,0:T(8,128)(2,1)} %collective-permute-done.3.inner_hbm, f32[40,128]{1,0:T(8,128)S(1)} %add_add_fusion.share_ref.refs_0_), custom_call_target="tpu_custom_call" | custom-call | bytes 6300000 | tf_op jit(solution)/shard_map/fetch/pallas_call | solution.py:387
  66.5 0.8 %collective-permute-done.12.refs_2_ = f32[40,128]{1,0:T(8,128)S(1)} collective-permute-done((f32[40,128]{1,0:T(8,128)S(1)}, f32[40,128]{1,0:T(8,128)S(1)}, u32[]{:S(2)}, u32[]{:S(2)}) %collective-permute-start.12) | collective-permute-done | bytes 20512 | tf_op jit(solution)/shard_map/ppermute | solution.py:534
  67.3 0.3 collective-permute-done.13.refs_3_
  67.6 3.3 %combine.1 = (f32[1,3,8,1024]{3,2,1,0:T(8,128)}, f32[1,64]{1,0:T(1,128)}, f32[1,128]{1,0:T(1,128)}) custom-call(s32[1]{0:T(128)} %bitcast.group_ref, s32[1]{0:T(128)} %bitcast.1.band_ref, s32[1]{0:T(128)} %bitcast.2.core_ref, f32[40,128]{1,0:T(8,128)S(1)} %add_add_fusion.share_ref.refs_0_, f32[40,128]{1,0:T(8,128)S(1)} %collective-permute-done.11.refs_1_, ...), custom_call_target="tpu_custom_call" | custom-call | tf_op jit(solution)/shard_map/combine/pallas_call | solution.py:511
  (19 shorter events, 0.2 us)
Async XLA Ops:
  2.1 6.5 %collective-permute-start = (bf16[16,1024]{1,0:T(8,128)(2,1)S(1)}, bf16[16,1024]{1,0:T(8,128)(2,1)S(1)}, u32[]{:S(2)}, u32[]{:S(2)}) collective-permute-start(bf16[16,1024]{1,0:T(8,128)(2,1)S(1)} %get-tuple-element.23), channel_id=1, source_target_pairs={{1,2},{2,1},{3,4},{4,3},{5,6},{6,5},{7,8},{8,7},{9,10},{10,9},{11,... | collective-permute-start | bytes 98312 | tf_op jit(solution)/shard_map/ppermute | solution.py:560
  2.8 9.5 %copy-start = (s32[1,128]{1,0:T(1,128)S(1)}, s32[1,128]{1,0:T(1,128)}, u32[]{:S(2)}) copy-start(s32[1,128]{1,0:T(1,128)} %station_row_ref.1) | copy-start | bytes 1540
  2.8 9.5 %copy-start.1 = (s32[1,128]{1,0:T(1,128)S(1)}, s32[1,128]{1,0:T(1,128)}, u32[]{:S(2)}) copy-start(s32[1,128]{1,0:T(1,128)} %station_column_ref.1) | copy-start | bytes 1540
  2.8 9.5 %copy-start.2 = (f32[1,128]{1,0:T(1,128)S(1)}, f32[1,128]{1,0:T(1,128)}, u32[]{:S(2)}) copy-start(f32[1,128]{1,0:T(1,128)} %station_value_ref.1) | copy-start | bytes 1540
  2.8 5.8 %collective-permute-start.1 = (bf16[16,1024]{1,0:T(8,128)(2,1)S(1)}, bf16[16,1024]{1,0:T(8,128)(2,1)S(1)}, u32[]{:S(2)}, u32[]{:S(2)}) collective-permute-start(bf16[16,1024]{1,0:T(8,128)(2,1)S(1)} %get-tuple-element.24), channel_id=1, source_target_pairs={{0,1},{1,0},{2,3},{3,2},{4,5},{5,4},{6,7},{7,6},{8,9},{9,8},{10,11... | collective-permute-start | bytes 98312 | tf_op jit(solution)/shard_map/ppermute | solution.py:561
  8.6 26.7 %collective-permute-start.2 = (bf16[12,64,1024]{2,1,0:T(8,128)(2,1)S(1)}, bf16[12,64,1024]{2,1,0:T(8,128)(2,1)}, u32[]{:S(2)}, u32[]{:S(2)}) collective-permute-start(bf16[12,64,1024]{2,1,0:T(8,128)(2,1)S(1)} %get-tuple-element.27.outer_ref.refs_4_), channel_id=1, source_target_pairs={{1,2},{2,1},{3,4},{4,3},{5,6},{6,5},{7,8},{8,7},{9,10},{10,9},{11,... | collective-permute-start | bytes 4718600 | tf_op jit(solution)/shard_map/ppermute | solution.py:566
  10.5 24.9 %collective-permute-start.3 = (bf16[12,64,1024]{2,1,0:T(8,128)(2,1)S(1)}, bf16[12,64,1024]{2,1,0:T(8,128)(2,1)}, u32[]{:S(2)}, u32[]{:S(2)}) collective-permute-start(bf16[12,64,1024]{2,1,0:T(8,128)(2,1)S(1)} %get-tuple-element.28.inner_ref.refs_5_), channel_id=1, source_target_pairs={{0,1},{1,0},{2,3},{3,2},{4,5},{5,4},{6,7},{7,6},{8,9},{9,8},{10,11... | collective-permute-start | bytes 4718600 | tf_op jit(solution)/shard_map/ppermute | solution.py:567
  39.3 1.3 %collective-permute-start.4 = (f32[40,128]{1,0:T(8,128)S(1)}, f32[40,128]{1,0:T(8,128)S(1)}, u32[]{:S(2)}, u32[]{:S(2)}) collective-permute-start(f32[40,128]{1,0:T(8,128)S(1)} %join.1), channel_id=1, source_target_pairs={{1,0},{0,1},{3,2},{2,3},{5,4},{4,5},{7,6},{6,7},{9,8},{8,9},{11,10... | collective-permute-start | bytes 61448 | tf_op jit(solution)/shard_map/ppermute | solution.py:534
  40.6 5.5 %collective-permute-start.5 = (f32[40,128]{1,0:T(8,128)S(1)}, f32[40,128]{1,0:T(8,128)S(1)}, u32[]{:S(2)}, u32[]{:S(2)}) collective-permute-start(f32[40,128]{1,0:T(8,128)S(1)} %add.29), channel_id=1, source_target_pairs={{2,0},{4,2},{6,4},{0,6},{3,1},{5,3},{7,5},{1,7},{10,8},{12,10},{14... | collective-permute-start | bytes 61448 | tf_op jit(solution)/shard_map/ppermute | solution.py:534
  44.5 5.0 %collective-permute-start.6 = (f32[40,128]{1,0:T(8,128)S(1)}, f32[40,128]{1,0:T(8,128)S(1)}, u32[]{:S(2)}, u32[]{:S(2)}) collective-permute-start(f32[40,128]{1,0:T(8,128)S(1)} %add.29), channel_id=1, source_target_pairs={{6,0},{0,2},{2,4},{4,6},{7,1},{1,3},{3,5},{5,7},{14,8},{8,10},{10,... | collective-permute-start | bytes 61448 | tf_op jit(solution)/shard_map/ppermute | solution.py:534
  44.5 5.3 %collective-permute-start.7 = (f32[40,128]{1,0:T(8,128)S(1)}, f32[40,128]{1,0:T(8,128)S(1)}, u32[]{:S(2)}, u32[]{:S(2)}) collective-permute-start(f32[40,128]{1,0:T(8,128)S(1)} %add.29), channel_id=1, source_target_pairs={{4,0},{6,2},{0,4},{2,6},{5,1},{7,3},{1,5},{3,7},{12,8},{14,10},{8,... | collective-permute-start | bytes 61448 | tf_op jit(solution)/shard_map/ppermute | solution.py:534
  49.8 5.7 %collective-permute-start.10 = (f32[40,128]{1,0:T(8,128)S(1)}, f32[40,128]{1,0:T(8,128)S(1)}, u32[]{:S(2)}, u32[]{:S(2)}) collective-permute-start(f32[40,128]{1,0:T(8,128)S(1)} %add_add_fusion.1), channel_id=1, source_target_pairs={{16,0},{24,8},{0,16},{8,24},{17,1},{25,9},{1,17},{9,25},{18,2},{26... | collective-permute-start | bytes 61448 | tf_op jit(solution)/shard_map/ppermute | solution.py:534
  53.5 3.8 %collective-permute-start.8 = (f32[40,128]{1,0:T(8,128)S(1)}, f32[40,128]{1,0:T(8,128)S(1)}, u32[]{:S(2)}, u32[]{:S(2)}) collective-permute-start(f32[40,128]{1,0:T(8,128)S(1)} %add_add_fusion.1), channel_id=1, source_target_pairs={{8,0},{16,8},{24,16},{0,24},{9,1},{17,9},{25,17},{1,25},{10,2},{18... | collective-permute-start | bytes 61448 | tf_op jit(solution)/shard_map/ppermute | solution.py:534
  54.5 5.0 %collective-permute-start.9 = (f32[40,128]{1,0:T(8,128)S(1)}, f32[40,128]{1,0:T(8,128)S(1)}, u32[]{:S(2)}, u32[]{:S(2)}) collective-permute-start(f32[40,128]{1,0:T(8,128)S(1)} %add_add_fusion.1), channel_id=1, source_target_pairs={{24,0},{0,8},{8,16},{16,24},{25,1},{1,9},{9,17},{17,25},{26,2},{2,... | collective-permute-start | bytes 61448 | tf_op jit(solution)/shard_map/ppermute | solution.py:534
  59.5 7.0 %collective-permute-start.11 = (f32[40,128]{1,0:T(8,128)S(1)}, f32[40,128]{1,0:T(8,128)S(1)}, u32[]{:S(2)}, u32[]{:S(2)}) collective-permute-start(f32[40,128]{1,0:T(8,128)S(1)} %add_add_fusion.share_ref.refs_0_), channel_id=1, source_target_pairs={{32,0},{64,32},{96,64},{0,96},{33,1},{65,33},{97,65},{1,97},{34,2}... | collective-permute-start | bytes 61448 | tf_op jit(solution)/shard_map/ppermute | solution.py:534
  62.3 5.0 %collective-permute-start.12 = (f32[40,128]{1,0:T(8,128)S(1)}, f32[40,128]{1,0:T(8,128)S(1)}, u32[]{:S(2)}, u32[]{:S(2)}) collective-permute-start(f32[40,128]{1,0:T(8,128)S(1)} %add_add_fusion.share_ref.refs_0_), channel_id=1, source_target_pairs={{96,0},{0,32},{32,64},{64,96},{97,1},{1,33},{33,65},{65,97},{98,2}... | collective-permute-start | bytes 61448 | tf_op jit(solution)/shard_map/ppermute | solution.py:534
  62.3 5.3 %collective-permute-start.13 = (f32[40,128]{1,0:T(8,128)S(1)}, f32[40,128]{1,0:T(8,128)S(1)}, u32[]{:S(2)}, u32[]{:S(2)}) collective-permute-start(f32[40,128]{1,0:T(8,128)S(1)} %add_add_fusion.share_ref.refs_0_), channel_id=1, source_target_pairs={{64,0},{96,32},{0,64},{32,96},{65,1},{97,33},{1,65},{33,97},{66,2}... | collective-permute-start | bytes 61448 | tf_op jit(solution)/shard_map/ppermute | solution.py:534

commit v7 on v4

--- a/solution.py
+++ b/solution.py
@@ -462,16 +462,16 @@
         (far_inner_ref, (1 - core) * (extended - HALO)),
     )
 
-    def one_field(f, carry):
+    def one_field(f):
         for ref, first in places:
             for r in range(HALO):
                 part = lax.dot_general(
                     factor, ref[f * HALO + r], (((1,), (0,)), ((), ())), preferred_element_type=jnp.float32
                 )
                 combined[f, pl.ds(first + r, 1)] = jnp.sum(part, axis=0, keepdims=True)
-        return carry
-
-    lax.fori_loop(0, fields, one_field, 0)
+
+    for f in range(fields):
+        one_field(f)
 
     latitude = band_ref[0] * rows - HALO + lax.broadcasted_iota(jnp.int32, (extended, lon), 0)
     present = (latitude >= 0) & (latitude < rows * bands)
@@ -481,7 +481,7 @@
     def lat_difference(x):
         return pltpu.roll(x, extended - 1, 0) - pltpu.roll(x, 1, 0)
 
-    def step(_, carry):
+    def step():
         depth, east, north = (coef_ref[f] for f in range(3))
         h, u, v = (combined[f] for f in range(3))
         dxh, dxu, dxv = (lon_difference(x) for x in (h, u, v))
@@ -491,9 +491,9 @@
         new_h = h - depth * (dxu + dyv) - east * dxh - north * dyh
         for f, x in enumerate((new_h, new_u, new_v)):
             combined[f] = jnp.where(present, x, 0.0)
-        return carry
-
-    lax.fori_loop(0, STEPS, step, 0)
+
+    for _ in range(STEPS):
+        step()
     for f in range(fields):
         value = combined[f, HALO : HALO + rows]
         increment[0, f] = 4.0 * value if f == 0 else value

time: 70.8 us -> 70.4 us (level)
  no operation moved by 1% of the time
where the time goes in v7:
time: 70.4 us; the launch traced here: 70.1 us
  Pallas kernels  35.3 us (50%)
  starting transfers between devices  22.6 us (32%)
  waiting for transfers between devices  10.6 us (15%)
  between operations  1.57 us (2%)
    pallas_call x1, Pallas kernels, sweep(): pl.pallas_call(functools.partial(sweep_kernel, scales, bands), out_shape=...  23 us
    ppermute x10, starting transfers between devices, from_ahead(): return lax.ppermute(x, axis, [((i + by) % count, i) for i in range(count)])  15.1 us
    ppermute x10, waiting for transfers between devices, from_ahead(): return lax.ppermute(x, axis, [((i + by) % count, i) for i in range(count)])  10.6 us
    pallas_call x1, Pallas kernels, join(): pl.pallas_call(functools.partial(join_kernel, scale), out_shape=jax.Shape...  3.97 us
    ppermute x1, starting transfers between devices, body(): far_inner_base = lax.ppermute(inner_base, 'lat_2', inside_chip)  3.1 us
    pallas_call x1, Pallas kernels, combine(): pl.pallas_call(functools.partial(combine_kernel, scale, len(shares), band...  2.94 us
    pallas_call x1, Pallas kernels, pack(): pl.pallas_call(pack_kernel, out_shape=(half, half), in_specs=[SMEM, HBM],...  2.68 us
    pallas_call x1, Pallas kernels, fetch(): pl.pallas_call(fetch_kernel, out_shape=(received, received), in_specs=[HB...  1.9 us
  transfers between devices with their start and end apart: 14, of which 7 were waited for; matrix products, arithmetic and copies ran while one was open for 0% of the time, Pallas kernels for 39%

profile of v7, /device:TPU:0, one launch (start us, length us, event | category | flops | bytes accessed | tf_op | source)
XLA Modules:
  0.0 70.1 jit_solution(14307181281696003163)
XLA Ops:
  1.3 0.8 %pick.1 = (bf16[16,1024]{1,0:T(8,128)(2,1)S(1)}, bf16[16,1024]{1,0:T(8,128)(2,1)S(1)}, f32[3,8,1024]{2,1,0:T(8,128)S(1)}) custom-call(s32[1]{0:T(128)S(6)} %copy.10.step_ref, s32[1]{0:T(128)} %bitcast.2.core_ref, bf16[4,3,8,1024]{3,2,1,0:T(8,128)(2,1)} %base_hbm.1), custom_call_target="tpu_custom_call" | custom-call | tf_op jit(solution)/shard_map/pick/pallas_call | solution.py:69
  2.1 0.7 collective-permute-start
  2.8 3.1 %collective-permute-start.1 = (bf16[16,1024]{1,0:T(8,128)(2,1)S(1)}, bf16[16,1024]{1,0:T(8,128)(2,1)S(1)}, u32[]{:S(2)}, u32[]{:S(2)}) collective-permute-start(bf16[16,1024]{1,0:T(8,128)(2,1)S(1)} %get-tuple-element.24), channel_id=1, source_target_pairs={{0,1},{1,0},{2,3},{3,2},{4,5},{5,4},{6,7},{7,6},{8,9},{9,8},{10,11... | collective-permute-start | bytes 98312 | tf_op jit(solution)/shard_map/ppermute | solution.py:556
  5.9 2.7 %pack.1 = (bf16[12,64,1024]{2,1,0:T(8,128)(2,1)S(1)}, bf16[12,64,1024]{2,1,0:T(8,128)(2,1)S(1)}) custom-call(s32[1]{0:T(128)} %bitcast.2.core_ref, bf16[64,3,8,1024]{3,2,1,0:T(8,128)(2,1)} %sketch_hbm.1), custom_call_target="tpu_custom_call" | custom-call | tf_op jit(solution)/shard_map/pack/pallas_call | solution.py:112
  8.6 1.8 %collective-permute-start.2 = (bf16[12,64,1024]{2,1,0:T(8,128)(2,1)S(1)}, bf16[12,64,1024]{2,1,0:T(8,128)(2,1)}, u32[]{:S(2)}, u32[]{:S(2)}) collective-permute-start(bf16[12,64,1024]{2,1,0:T(8,128)(2,1)S(1)} %get-tuple-element.27.outer_ref.refs_4_), channel_id=1, source_target_pairs={{1,2},{2,1},{3,4},{4,3},{5,6},{6,5},{7,8},{8,7},{9,10},{10,9},{11,... | collective-permute-start | bytes 4718600 | tf_op jit(solution)/shard_map/ppermute | solution.py:561
  10.5 1.8 %collective-permute-start.3 = (bf16[12,64,1024]{2,1,0:T(8,128)(2,1)S(1)}, bf16[12,64,1024]{2,1,0:T(8,128)(2,1)}, u32[]{:S(2)}, u32[]{:S(2)}) collective-permute-start(bf16[12,64,1024]{2,1,0:T(8,128)(2,1)S(1)} %get-tuple-element.28.inner_ref.refs_5_), channel_id=1, source_target_pairs={{0,1},{1,0},{2,3},{3,2},{4,5},{5,4},{6,7},{7,6},{8,9},{9,8},{10,11... | collective-permute-start | bytes 4718600 | tf_op jit(solution)/shard_map/ppermute | solution.py:562
  12.3 23.0 %sweep.1 = (bf16[48,128,1024]{2,1,0:T(8,128)(2,1)S(1)}, f32[3,16,1024]{2,1,0:T(8,128)S(1)}, f32[8,64]{1,0:T(8,128)S(1)}) custom-call(s32[1]{0:T(128)} %bitcast.1.band_ref, s32[1]{0:T(128)} %bitcast.2.core_ref, bf16[64,3,8,1024]{3,2,1,0:T(8,128)(2,1)} %test_hbm.1, f32[3,8,1024]{2,1,0:T(8,128)S(1)} %get-tuple-element.20.base_ref, ...), custom_call_target="tpu_custom_call" | custom-call | flops 2000000000 | bytes 30000000 | tf_op jit(solution)/shard_map/sweep/pallas_call | solution.py:285
  35.3 4.0 %join.1 = f32[40,128]{1,0:T(8,128)S(1)} custom-call(s32[1]{0:T(128)} %bitcast.2.core_ref, bf16[48,128,1024]{2,1,0:T(8,128)(2,1)S(1)} %get-tuple-element.29.back_ref, f32[8,64]{1,0:T(8,128)S(1)} %get-tuple-element.30.tail_ref, bf16[12,64,1024]{2,1,0:T(8,128)(2,1)S(1)} %get-tuple-element.27.outer_ref.refs_4_, ...), custom_call_target="tpu_custom_call" | custom-call | tf_op jit(solution)/shard_map/join/pallas_call | solution.py:358
  39.4 1.2 %collective-permute-done.4 = f32[40,128]{1,0:T(8,128)S(1)} collective-permute-done((f32[40,128]{1,0:T(8,128)S(1)}, f32[40,128]{1,0:T(8,128)S(1)}, u32[]{:S(2)}, u32[]{:S(2)}) %collective-permute-start.4) | collective-permute-done | bytes 20512 | tf_op jit(solution)/shard_map/ppermute | solution.py:533
  40.6 3.9 %collective-permute-start.5 = (f32[40,128]{1,0:T(8,128)S(1)}, f32[40,128]{1,0:T(8,128)S(1)}, u32[]{:S(2)}, u32[]{:S(2)}) collective-permute-start(f32[40,128]{1,0:T(8,128)S(1)} %add.29), channel_id=1, source_target_pairs={{2,0},{4,2},{6,4},{0,6},{3,1},{5,3},{7,5},{1,7},{10,8},{12,10},{14... | collective-permute-start | bytes 61448 | tf_op jit(solution)/shard_map/ppermute | solution.py:533
  44.5 0.9 %collective-permute-start.7 = (f32[40,128]{1,0:T(8,128)S(1)}, f32[40,128]{1,0:T(8,128)S(1)}, u32[]{:S(2)}, u32[]{:S(2)}) collective-permute-start(f32[40,128]{1,0:T(8,128)S(1)} %add.29), channel_id=1, source_target_pairs={{6,0},{0,2},{2,4},{4,6},{7,1},{1,3},{3,5},{5,7},{14,8},{8,10},{10,... | collective-permute-start | bytes 61448 | tf_op jit(solution)/shard_map/ppermute | solution.py:533
  45.4 0.5 collective-permute-done.5
  46.0 3.8 %collective-permute-done.6 = f32[40,128]{1,0:T(8,128)S(1)} collective-permute-done((f32[40,128]{1,0:T(8,128)S(1)}, f32[40,128]{1,0:T(8,128)S(1)}, u32[]{:S(2)}, u32[]{:S(2)}) %collective-permute-start.6) | collective-permute-done | bytes 20512 | tf_op jit(solution)/shard_map/ppermute | solution.py:533
  49.8 2.0 %collective-permute-start.10 = (f32[40,128]{1,0:T(8,128)S(1)}, f32[40,128]{1,0:T(8,128)S(1)}, u32[]{:S(2)}, u32[]{:S(2)}) collective-permute-start(f32[40,128]{1,0:T(8,128)S(1)} %add_add_fusion.1), channel_id=1, source_target_pairs={{24,0},{0,8},{8,16},{16,24},{25,1},{1,9},{9,17},{17,25},{26,2},{2,... | collective-permute-start | bytes 61448 | tf_op jit(solution)/shard_map/ppermute | solution.py:533
  51.8 1.3 %collective-permute-start.8 = (f32[40,128]{1,0:T(8,128)S(1)}, f32[40,128]{1,0:T(8,128)S(1)}, u32[]{:S(2)}, u32[]{:S(2)}) collective-permute-start(f32[40,128]{1,0:T(8,128)S(1)} %add_add_fusion.1), channel_id=1, source_target_pairs={{8,0},{16,8},{24,16},{0,24},{9,1},{17,9},{25,17},{1,25},{10,2},{18... | collective-permute-start | bytes 61448 | tf_op jit(solution)/shard_map/ppermute | solution.py:533
  53.1 2.4 %collective-permute-start.9 = (f32[40,128]{1,0:T(8,128)S(1)}, f32[40,128]{1,0:T(8,128)S(1)}, u32[]{:S(2)}, u32[]{:S(2)}) collective-permute-start(f32[40,128]{1,0:T(8,128)S(1)} %add_add_fusion.1), channel_id=1, source_target_pairs={{16,0},{24,8},{0,16},{8,24},{17,1},{25,9},{1,17},{9,25},{18,2},{26... | collective-permute-start | bytes 61448 | tf_op jit(solution)/shard_map/ppermute | solution.py:533
  55.6 2.8 %collective-permute-done.9 = f32[40,128]{1,0:T(8,128)S(1)} collective-permute-done((f32[40,128]{1,0:T(8,128)S(1)}, f32[40,128]{1,0:T(8,128)S(1)}, u32[]{:S(2)}, u32[]{:S(2)}) %collective-permute-start.9) | collective-permute-done | bytes 20512 | tf_op jit(solution)/shard_map/ppermute | solution.py:533
  58.4 2.8 %collective-permute-start.11 = (f32[40,128]{1,0:T(8,128)S(1)}, f32[40,128]{1,0:T(8,128)S(1)}, u32[]{:S(2)}, u32[]{:S(2)}) collective-permute-start(f32[40,128]{1,0:T(8,128)S(1)} %add_add_fusion.share_ref.refs_0_), channel_id=1, source_target_pairs={{32,0},{64,32},{96,64},{0,96},{33,1},{65,33},{97,65},{1,97},{34,2}... | collective-permute-start | bytes 61448 | tf_op jit(solution)/shard_map/ppermute | solution.py:533
  61.3 0.8 %collective-permute-start.12 = (f32[40,128]{1,0:T(8,128)S(1)}, f32[40,128]{1,0:T(8,128)S(1)}, u32[]{:S(2)}, u32[]{:S(2)}) collective-permute-start(f32[40,128]{1,0:T(8,128)S(1)} %add_add_fusion.share_ref.refs_0_), channel_id=1, source_target_pairs={{64,0},{96,32},{0,64},{32,96},{65,1},{97,33},{1,65},{33,97},{66,2}... | collective-permute-start | bytes 61448 | tf_op jit(solution)/shard_map/ppermute | solution.py:533
  62.0 0.9 %collective-permute-start.13 = (f32[40,128]{1,0:T(8,128)S(1)}, f32[40,128]{1,0:T(8,128)S(1)}, u32[]{:S(2)}, u32[]{:S(2)}) collective-permute-start(f32[40,128]{1,0:T(8,128)S(1)} %add_add_fusion.share_ref.refs_0_), channel_id=1, source_target_pairs={{96,0},{0,32},{32,64},{64,96},{97,1},{1,33},{33,65},{65,97},{98,2}... | collective-permute-start | bytes 61448 | tf_op jit(solution)/shard_map/ppermute | solution.py:533
  62.9 1.9 %fetch.1 = (bf16[12,64,1024]{2,1,0:T(8,128)(2,1)S(1)}, bf16[12,64,1024]{2,1,0:T(8,128)(2,1)S(1)}) custom-call(bf16[12,64,1024]{2,1,0:T(8,128)(2,1)} %collective-permute-done.2.outer_hbm, bf16[12,64,1024]{2,1,0:T(8,128)(2,1)} %collective-permute-done.3.inner_hbm, f32[40,128]{1,0:T(8,128)S(1)} %add_add_fusion.share_ref.refs_0_), custom_call_target="tpu_custom_call" | custom-call | bytes 6300000 | tf_op jit(solution)/shard_map/fetch/pallas_call | solution.py:387
  64.9 1.7 %collective-permute-done.12.refs_2_ = f32[40,128]{1,0:T(8,128)S(1)} collective-permute-done((f32[40,128]{1,0:T(8,128)S(1)}, f32[40,128]{1,0:T(8,128)S(1)}, u32[]{:S(2)}, u32[]{:S(2)}) %collective-permute-start.12) | collective-permute-done | bytes 20512 | tf_op jit(solution)/shard_map/ppermute | solution.py:533
  66.5 0.5 collective-permute-done.13.refs_3_
  67.0 2.9 %combine.1 = (f32[1,3,8,1024]{3,2,1,0:T(8,128)}, f32[1,64]{1,0:T(1,128)}, f32[1,128]{1,0:T(1,128)}) custom-call(s32[1]{0:T(128)} %bitcast.group_ref, s32[1]{0:T(128)} %bitcast.1.band_ref, s32[1]{0:T(128)} %bitcast.2.core_ref, f32[40,128]{1,0:T(8,128)S(1)} %add_add_fusion.share_ref.refs_0_, f32[40,128]{1,0:T(8,128)S(1)} %collective-permute-done.11.refs_1_, ...), custom_call_target="tpu_custom_call" | custom-call | tf_op jit(solution)/shard_map/combine/pallas_call | solution.py:510
  (19 shorter events, 0.2 us)
Async XLA Ops:
  2.1 6.5 %collective-permute-start = (bf16[16,1024]{1,0:T(8,128)(2,1)S(1)}, bf16[16,1024]{1,0:T(8,128)(2,1)S(1)}, u32[]{:S(2)}, u32[]{:S(2)}) collective-permute-start(bf16[16,1024]{1,0:T(8,128)(2,1)S(1)} %get-tuple-element.23), channel_id=1, source_target_pairs={{1,2},{2,1},{3,4},{4,3},{5,6},{6,5},{7,8},{8,7},{9,10},{10,9},{11,... | collective-permute-start | bytes 98312 | tf_op jit(solution)/shard_map/ppermute | solution.py:555
  2.8 9.5 %copy-start = (s32[1,128]{1,0:T(1,128)S(1)}, s32[1,128]{1,0:T(1,128)}, u32[]{:S(2)}) copy-start(s32[1,128]{1,0:T(1,128)} %station_row_ref.1) | copy-start | bytes 1540
  2.8 9.5 %copy-start.1 = (s32[1,128]{1,0:T(1,128)S(1)}, s32[1,128]{1,0:T(1,128)}, u32[]{:S(2)}) copy-start(s32[1,128]{1,0:T(1,128)} %station_column_ref.1) | copy-start | bytes 1540
  2.8 9.5 %copy-start.2 = (f32[1,128]{1,0:T(1,128)S(1)}, f32[1,128]{1,0:T(1,128)}, u32[]{:S(2)}) copy-start(f32[1,128]{1,0:T(1,128)} %station_value_ref.1) | copy-start | bytes 1540
  2.8 5.8 %collective-permute-start.1 = (bf16[16,1024]{1,0:T(8,128)(2,1)S(1)}, bf16[16,1024]{1,0:T(8,128)(2,1)S(1)}, u32[]{:S(2)}, u32[]{:S(2)}) collective-permute-start(bf16[16,1024]{1,0:T(8,128)(2,1)S(1)} %get-tuple-element.24), channel_id=1, source_target_pairs={{0,1},{1,0},{2,3},{3,2},{4,5},{5,4},{6,7},{7,6},{8,9},{9,8},{10,11... | collective-permute-start | bytes 98312 | tf_op jit(solution)/shard_map/ppermute | solution.py:556
  8.6 26.7 %collective-permute-start.2 = (bf16[12,64,1024]{2,1,0:T(8,128)(2,1)S(1)}, bf16[12,64,1024]{2,1,0:T(8,128)(2,1)}, u32[]{:S(2)}, u32[]{:S(2)}) collective-permute-start(bf16[12,64,1024]{2,1,0:T(8,128)(2,1)S(1)} %get-tuple-element.27.outer_ref.refs_4_), channel_id=1, source_target_pairs={{1,2},{2,1},{3,4},{4,3},{5,6},{6,5},{7,8},{8,7},{9,10},{10,9},{11,... | collective-permute-start | bytes 4718600 | tf_op jit(solution)/shard_map/ppermute | solution.py:561
  10.5 24.9 %collective-permute-start.3 = (bf16[12,64,1024]{2,1,0:T(8,128)(2,1)S(1)}, bf16[12,64,1024]{2,1,0:T(8,128)(2,1)}, u32[]{:S(2)}, u32[]{:S(2)}) collective-permute-start(bf16[12,64,1024]{2,1,0:T(8,128)(2,1)S(1)} %get-tuple-element.28.inner_ref.refs_5_), channel_id=1, source_target_pairs={{0,1},{1,0},{2,3},{3,2},{4,5},{5,4},{6,7},{7,6},{8,9},{9,8},{10,11... | collective-permute-start | bytes 4718600 | tf_op jit(solution)/shard_map/ppermute | solution.py:562
  39.3 1.3 %collective-permute-start.4 = (f32[40,128]{1,0:T(8,128)S(1)}, f32[40,128]{1,0:T(8,128)S(1)}, u32[]{:S(2)}, u32[]{:S(2)}) collective-permute-start(f32[40,128]{1,0:T(8,128)S(1)} %join.1), channel_id=1, source_target_pairs={{1,0},{0,1},{3,2},{2,3},{5,4},{4,5},{7,6},{6,7},{9,8},{8,9},{11,10... | collective-permute-start | bytes 61448 | tf_op jit(solution)/shard_map/ppermute | solution.py:533
  40.6 5.4 %collective-permute-start.5 = (f32[40,128]{1,0:T(8,128)S(1)}, f32[40,128]{1,0:T(8,128)S(1)}, u32[]{:S(2)}, u32[]{:S(2)}) collective-permute-start(f32[40,128]{1,0:T(8,128)S(1)} %add.29), channel_id=1, source_target_pairs={{2,0},{4,2},{6,4},{0,6},{3,1},{5,3},{7,5},{1,7},{10,8},{12,10},{14... | collective-permute-start | bytes 61448 | tf_op jit(solution)/shard_map/ppermute | solution.py:533
  44.5 5.3 %collective-permute-start.6 = (f32[40,128]{1,0:T(8,128)S(1)}, f32[40,128]{1,0:T(8,128)S(1)}, u32[]{:S(2)}, u32[]{:S(2)}) collective-permute-start(f32[40,128]{1,0:T(8,128)S(1)} %add.29), channel_id=1, source_target_pairs={{4,0},{6,2},{0,4},{2,6},{5,1},{7,3},{1,5},{3,7},{12,8},{14,10},{8,... | collective-permute-start | bytes 61448 | tf_op jit(solution)/shard_map/ppermute | solution.py:533
  44.5 5.3 %collective-permute-start.7 = (f32[40,128]{1,0:T(8,128)S(1)}, f32[40,128]{1,0:T(8,128)S(1)}, u32[]{:S(2)}, u32[]{:S(2)}) collective-permute-start(f32[40,128]{1,0:T(8,128)S(1)} %add.29), channel_id=1, source_target_pairs={{6,0},{0,2},{2,4},{4,6},{7,1},{1,3},{3,5},{5,7},{14,8},{8,10},{10,... | collective-permute-start | bytes 61448 | tf_op jit(solution)/shard_map/ppermute | solution.py:533
  49.8 5.7 %collective-permute-start.10 = (f32[40,128]{1,0:T(8,128)S(1)}, f32[40,128]{1,0:T(8,128)S(1)}, u32[]{:S(2)}, u32[]{:S(2)}) collective-permute-start(f32[40,128]{1,0:T(8,128)S(1)} %add_add_fusion.1), channel_id=1, source_target_pairs={{24,0},{0,8},{8,16},{16,24},{25,1},{1,9},{9,17},{17,25},{26,2},{2,... | collective-permute-start | bytes 61448 | tf_op jit(solution)/shard_map/ppermute | solution.py:533
  51.8 3.8 %collective-permute-start.8 = (f32[40,128]{1,0:T(8,128)S(1)}, f32[40,128]{1,0:T(8,128)S(1)}, u32[]{:S(2)}, u32[]{:S(2)}) collective-permute-start(f32[40,128]{1,0:T(8,128)S(1)} %add_add_fusion.1), channel_id=1, source_target_pairs={{8,0},{16,8},{24,16},{0,24},{9,1},{17,9},{25,17},{1,25},{10,2},{18... | collective-permute-start | bytes 61448 | tf_op jit(solution)/shard_map/ppermute | solution.py:533
  53.1 5.3 %collective-permute-start.9 = (f32[40,128]{1,0:T(8,128)S(1)}, f32[40,128]{1,0:T(8,128)S(1)}, u32[]{:S(2)}, u32[]{:S(2)}) collective-permute-start(f32[40,128]{1,0:T(8,128)S(1)} %add_add_fusion.1), channel_id=1, source_target_pairs={{16,0},{24,8},{0,16},{8,24},{17,1},{25,9},{1,17},{9,25},{18,2},{26... | collective-permute-start | bytes 61448 | tf_op jit(solution)/shard_map/ppermute | solution.py:533
  58.4 6.4 %collective-permute-start.11 = (f32[40,128]{1,0:T(8,128)S(1)}, f32[40,128]{1,0:T(8,128)S(1)}, u32[]{:S(2)}, u32[]{:S(2)}) collective-permute-start(f32[40,128]{1,0:T(8,128)S(1)} %add_add_fusion.share_ref.refs_0_), channel_id=1, source_target_pairs={{32,0},{64,32},{96,64},{0,96},{33,1},{65,33},{97,65},{1,97},{34,2}... | collective-permute-start | bytes 61448 | tf_op jit(solution)/shard_map/ppermute | solution.py:533
  61.3 5.3 %collective-permute-start.12 = (f32[40,128]{1,0:T(8,128)S(1)}, f32[40,128]{1,0:T(8,128)S(1)}, u32[]{:S(2)}, u32[]{:S(2)}) collective-permute-start(f32[40,128]{1,0:T(8,128)S(1)} %add_add_fusion.share_ref.refs_0_), channel_id=1, source_target_pairs={{64,0},{96,32},{0,64},{32,96},{65,1},{97,33},{1,65},{33,97},{66,2}... | collective-permute-start | bytes 61448 | tf_op jit(solution)/shard_map/ppermute | solution.py:533
  62.0 5.0 %collective-permute-start.13 = (f32[40,128]{1,0:T(8,128)S(1)}, f32[40,128]{1,0:T(8,128)S(1)}, u32[]{:S(2)}, u32[]{:S(2)}) collective-permute-start(f32[40,128]{1,0:T(8,128)S(1)} %add_add_fusion.share_ref.refs_0_), channel_id=1, source_target_pairs={{96,0},{0,32},{32,64},{64,96},{97,1},{1,33},{33,65},{65,97},{98,2}... | collective-permute-start | bytes 61448 | tf_op jit(solution)/shard_map/ppermute | solution.py:533
